TPU v7x, 256 devices: a whole 4x4x8 slice. The times are simulated.
256 devices in a mesh: expert: 8 (over y, core), hidden: 32 (over z, x).
Axes of the slice: x: 4, y: 4, z: 8, core: 2. Of those that a mesh axis runs over, the one named last changes fastest.
Arguments:
- tokens: bfloat16 [2048, 3584], P('hidden'), may hold values from -6 to 6
- cotangent: bfloat16 [2048, 3584], P('hidden'), may hold values from -6 to 6
- routes: int32 [2048, 8], P('hidden'), may hold values from 0 to 63, all different within a row; in each aligned block of 64 rows (0 to 63, 64 to 127, ...) at most 20 rows name the same one
- route_weights: float32 [2048, 8], P('hidden'), may hold values from 0.08 to 1
- gate_weight: bfloat16 [65536, 3584], P(('expert', 'hidden')), may hold values from -0.09375 to 0.09375
- up_weight: bfloat16 [65536, 3584], P(('expert', 'hidden')), may hold values from -0.09375 to 0.09375
- down_weight: bfloat16 [65536, 3584], P(('expert', 'hidden')), may hold values from -6 to 6
- cluster: int32 [64], replicated, may hold values from 0 to 23, as said below
- merged_slot: int32 [24], replicated, may hold values from 0 to 23, each once
Outputs:
- merged_down: bfloat16 [24, 4, 256, 3584], P('expert', None, 'hidden')
Inputs may be any that keep to these rules, and one draw needn't show every extreme that they name: `routes`: each row names 8 different experts. Within the rows of one shard of 64 tokens no expert is named by more than 20 rows, a bound that some block reaches. Every one of the 24 clusters has 1 to 6 member experts, and some cluster has exactly 6. `merged_slot`: each slot holds exactly one cluster.
All inputs are finite; a program needn't handle non-finite values.
Results may differ from a plain program's by a relative error of at most 0.014.
Values may be sent and summed in bfloat16 or wider, within the bound.
No kernel may reach another device: no remote copies, remote signals or barrier semaphores. Data moves between devices by JAX's collectives and lax.ppermute only.
A program may use at most 128 MiB of HBM per device.

v0:
```python
import functools

import jax
import jax.numpy as jnp
from jax import lax
from jax.experimental import pallas as pl
from jax.experimental.pallas import tpu as pltpu
from jax.sharding import Mesh, PartitionSpec as P


F = 1024
EXPERTS = 64
MERGED = 24
CAP = 20
PRIOR = 0.1
NY, NC, NZ, NX = 4, 2, 8, 4
OWN = MERGED // (NY * NC)
ROWS = NZ * CAP
TALL = 24
STEPS = (0, 1, 7, 2, 6, 3, 5, 4)
PIECE = F // (NZ * NX * NX)
HALVES = ((0, 1), (3, 2))
ORDER = (0, 1, 3, 2)
HOPS = (1, 3, 0)
COLS = 7
INTERPRET = False


bf16 = jnp.bfloat16
f32 = jnp.float32


def shift(a, axis, size, step):
    return lax.ppermute(a, axis, [(i, (i + step) % size) for i in range(size)])


def slot_lookup(cluster, merged_slot):
    ids = jnp.arange(MERGED, dtype=jnp.int32)
    return jnp.sum(jnp.where(cluster[:, None] == ids[None, :], merged_slot[None, :], 0), axis=1)


def pack_kernel(here_ref, route_ref, weight_ref, tok_ref, *refs):
    outs, pick_ref, scale_ref = refs[:NZ], refs[NZ], refs[NZ + 1]
    toks, width = tok_ref.shape
    per = toks // (NY * NC)
    y, c, z = here_ref[0], here_ref[1], here_ref[2]
    first = (y * NC + c) * NZ
    routes = route_ref[...]
    weights = weight_ref[...]
    marks, scales = [], []
    for step in STEPS:
        match = routes == first + lax.rem(z + step, NZ)
        marks.append(jnp.sum(jnp.where(match, 1.0, 0.0), axis=0, keepdims=True))
        scales.append(jnp.sum(jnp.where(match, weights, 0.0), axis=0, keepdims=True))
    row = lax.broadcasted_iota(jnp.int32, (toks, toks), 0)
    col = lax.broadcasted_iota(jnp.int32, (toks, toks), 1)
    before = jnp.where(row < col, 1.0, 0.0).astype(bf16)
    marked = jnp.concatenate(marks, axis=0)
    places = jnp.dot(marked.astype(bf16), before, preferred_element_type=f32)
    place = lax.broadcasted_iota(jnp.int32, (TALL, toks), 0).astype(f32)
    for n in range(NZ):
        hit = (places[n : n + 1] == place) & (marks[n] > 0.0)
        pick_ref[n * TALL : (n + 1) * TALL, :] = jnp.where(hit, 1.0, 0.0)
        scale_ref[n * TALL : (n + 1) * TALL, :] = jnp.where(hit, scales[n], 0.0)
    pick = pick_ref[...].astype(bf16)
    step = width // COLS

    def body(k, carry):
        cols = pl.ds(pl.multiple_of(k * step, step), step)
        rows = jnp.dot(pick, tok_ref[:, cols], preferred_element_type=f32).astype(bf16)
        for n, out in enumerate(outs):
            out[:, cols] = rows[n * TALL : n * TALL + CAP]
        return carry

    lax.fori_loop(0, COLS, body, 0)
    ahead = lax.rem(y + col // (NC * per), NY)
    other = lax.rem(c + lax.rem(col // per, NC), NC)
    turned = (ahead * NC + other) * per + lax.rem(col, per)
    turn = jnp.where(row == turned, 1.0, 0.0).astype(bf16)
    scale = scale_ref[...]
    high = scale.astype(bf16)
    low = (scale - high.astype(f32)).astype(bf16)
    high = jnp.dot(high, turn, preferred_element_type=f32)
    low = jnp.dot(low, turn, preferred_element_type=f32)
    tail = jnp.concatenate([high, low], axis=1).astype(bf16)
    for n, out in enumerate(outs):
        out[:, width:] = tail[n * TALL : n * TALL + CAP]


def pack(here, routes, weights, tokens):
    toks, width = tokens.shape
    shape = jax.ShapeDtypeStruct((CAP, width + 2 * toks), bf16)
    return pl.pallas_call(
        pack_kernel,
        in_specs=[pl.BlockSpec(memory_space=pltpu.SMEM)] + [pl.BlockSpec(memory_space=pltpu.VMEM)] * 3,
        out_shape=[shape] * NZ,
        scratch_shapes=[pltpu.VMEM((NZ * TALL, toks), f32)] * 2,
        interpret=INTERPRET,
        name="pack",
    )(here, routes.T, weights.T, tokens)


def pick_kernel(here_ref, *refs):
    tails, cots, out_ref, tail_ref = refs[: 2 * NX], refs[2 * NX : -2], refs[-2], refs[-1]
    group = NZ // 2
    height = group * CAP
    per = cots[0].shape[2]
    tok = per * len(cots)
    row = lax.broadcasted_iota(jnp.int32, (height, group * tok), 0) // CAP
    col = lax.broadcasted_iota(jnp.int32, (height, group * tok), 1) // tok
    same = row == col
    lanes = tail_ref.shape[-1]
    lane = lax.broadcasted_iota(jnp.int32, (lanes, 2 * group * tok), 0)
    wide = lax.broadcasted_iota(jnp.int32, (lanes, 2 * group * tok), 1)
    match = (lane % tok == wide % tok) & (lane // tok == wide // (group * tok))
    spread = jnp.where(match, 1.0, 0.0).astype(bf16)
    z, x = here_ref[2], here_ref[3]
    for n, t in enumerate(tails):
        tail_ref[n] = t[...]

    def body(n, carry):
        half = n % 2
        xs = lax.rem(x + n // 2, NX)
        wide = jnp.dot(tail_ref[n], spread, preferred_element_type=f32)
        high = jnp.where(same, wide[:, : group * tok], 0.0).astype(bf16)
        low = jnp.where(same, wide[:, group * tok :], 0.0).astype(bf16)
        blocks = []
        for j in range(group):
            step = jnp.where(half == 0, STEPS[j], STEPS[group + j])
            zs = lax.rem(z + NZ - step, NZ)
            blocks += [cot[zs, xs].astype(f32) for cot in cots]
        cot = jnp.concatenate(blocks, axis=0).astype(bf16)
        val = jnp.dot(high, cot, preferred_element_type=f32)
        val = val + jnp.dot(low, cot, preferred_element_type=f32)
        val = val.astype(bf16).astype(f32)
        out_ref[n] = (val * val).astype(bf16)
        return carry

    lax.fori_loop(0, 2 * NX, body, 0)


def pick(here, pieces, cots, width):
    lanes = pieces[0].shape[1] - width
    height = pieces[0].shape[0]
    chunk = cots[0].shape[-1]
    tail = pl.BlockSpec((height, lanes), lambda i, src: (0, width // lanes))
    whole = lambda a: pl.BlockSpec(a.shape, lambda i, src: (0,) * a.ndim)
    return pl.pallas_call(
        pick_kernel,
        grid_spec=pltpu.PrefetchScalarGridSpec(
            num_scalar_prefetch=1,
            grid=(1,),
            in_specs=[tail] * len(pieces) + [whole(c) for c in cots],
            out_specs=pl.BlockSpec((2 * NX, ROWS // 2, chunk), lambda i, src: (0, 0, 0)),
            scratch_shapes=[pltpu.VMEM((2 * NX, height, lanes), bf16)],
        ),
        out_shape=jax.ShapeDtypeStruct((2 * NX, ROWS // 2, chunk), bf16),
        interpret=INTERPRET,
        name="pick",
    )(here, *pieces, *cots).reshape(NX, ROWS, chunk)


def hidden_kernel(*refs, pieces, known):
    blocks, gate_ref, up_ref = refs[:pieces], refs[pieces], refs[pieces + 1]
    outs, acc_ref = refs[pieces + 2 + known : -1], refs[-1]
    step = pl.program_id(0)
    rows = jnp.concatenate([b[...] for b in blocks], axis=0)
    units = gate_ref.shape[0]
    dims = (((1,), (1,)), ((), ()))
    g = lax.dot_general(rows, gate_ref[...], dims, preferred_element_type=f32)
    u = lax.dot_general(rows, up_ref[...], dims, preferred_element_type=f32)

    @pl.when(step == 0)
    def _():
        acc_ref[:, :units] = g
        acc_ref[:, units:] = u

    @pl.when(step > 0)
    def _():
        acc_ref[:, :units] += g
        acc_ref[:, units:] += u

    @pl.when(step == pl.num_programs(0) - 1)
    def _():
        gv = acc_ref[:, :units]
        h = gv / (1.0 + jnp.exp(-gv)) * acc_ref[:, units:]
        h = (h * h).astype(bf16)
        outs[0][...] = h
        if known:
            old = refs[pieces + 2]
            outs[1][: old.shape[0], :] = old[...]
            outs[1][old.shape[0] :, :] = h


def hidden(pieces, gate, up, *known):
    units, width = gate.shape
    step = width // NX
    total = sum(p.shape[0] for p in pieces)
    col = lambda k: (0, k)
    fixed = lambda k: (0, 0)
    heights = [total] + [total + k.shape[0] for k in known]
    return pl.pallas_call(
        functools.partial(hidden_kernel, pieces=len(pieces), known=len(known)),
        grid=(NX,),
        in_specs=[pl.BlockSpec((p.shape[0], step), col) for p in pieces]
        + [pl.BlockSpec((units, step), col)] * 2
        + [pl.BlockSpec(k.shape, fixed) for k in known],
        out_specs=[pl.BlockSpec((h, units), fixed) for h in heights],
        out_shape=[jax.ShapeDtypeStruct((h, units), bf16) for h in heights],
        scratch_shapes=[pltpu.VMEM((total, 2 * units), f32)],
        interpret=INTERPRET,
        name="hidden",
    )(*pieces, gate, up, *known)


def fisher_kernel(*refs, half, counts):
    g_ref, out_ref = refs[-2:]
    start = 0
    for j, count in enumerate(counts):
        e = half[j]
        parts = [r[...] for r in refs[start : start + count]]
        start += count
        h = jnp.concatenate(parts, axis=0) if count > 1 else parts[0]
        g = jnp.concatenate([g_ref[(e + d) % NX] for d in ORDER], axis=0)
        acc = lax.dot_general(h, g, (((0,), (0,)), ((), ())), preferred_element_type=f32)
        acc = acc + PRIOR
        out_ref[:, j * PIECE : (j + 1) * PIECE, :] = acc.reshape(-1, PIECE, acc.shape[1]).astype(bf16)


def fisher_half(half, parts, grad_sq):
    flat = [h for e in half for h in parts[e]]
    units = flat[0].shape[1] // 2
    chunk = grad_sq.shape[-1]
    return pl.pallas_call(
        functools.partial(fisher_kernel, half=half, counts=[len(parts[e]) for e in half]),
        grid=(2,),
        in_specs=[pl.BlockSpec((h.shape[0], units), lambda k: (0, k)) for h in flat]
        + [pl.BlockSpec(grad_sq.shape, lambda k: (0, 0, 0))],
        out_specs=pl.BlockSpec((NZ * NX // 2, 2 * PIECE, chunk), lambda k: (k, 0, 0)),
        out_shape=jax.ShapeDtypeStruct((NZ * NX, 2 * PIECE, chunk), bf16),
        interpret=INTERPRET,
        name="fisher",
    )(*flat, grad_sq)


def mix_kernel(kron_ref, den_ref, da_ref, db_ref, *refs):
    snd2_ref, snd_ref, own2_ref, own_ref, val_ref = refs[-5:]
    mix = kron_ref[...]
    block = OWN * PIECE
    for j, down_ref in enumerate((da_ref, db_ref)):
        den_all = den_ref[:, 0, j * PIECE : (j + 1) * PIECE, :].astype(f32)
        num_all = den_all * down_ref[:, 0].astype(f32)
        val_ref[2 * j] = num_all.reshape(NZ * PIECE, -1).astype(bf16)
        val_ref[2 * j + 1] = den_all.reshape(NZ * PIECE, -1).astype(bf16)

    def body(n, carry):
        arr = n % 2
        rows = pl.ds(pl.multiple_of(n // 2 * block, PIECE), block)
        res = jnp.dot(mix, val_ref[n], preferred_element_type=f32).astype(bf16)
        for core, (two, rest) in enumerate(((own2_ref, own_ref), (snd2_ref, snd_ref))):
            base = core * NY * block
            two[arr, rows, :] = res[base + 2 * block : base + 3 * block]
            for i, hop in enumerate(HOPS):
                rest[arr, i, rows, :] = res[base + hop * block : base + (hop + 1) * block]
        return carry

    lax.fori_loop(0, 4, body, 0)


def mix(half, kron, den, down, after):
    chunk = den.shape[-1]
    width = down.shape[-1]
    tall = 2 * OWN * PIECE
    two = jax.ShapeDtypeStruct((2, tall, width), bf16)
    rest = jax.ShapeDtypeStruct((2, len(HOPS), tall, width), bf16)
    two_spec = pl.BlockSpec((2, tall, chunk), lambda k: (0, 0, k))
    rest_spec = pl.BlockSpec((2, len(HOPS), tall, chunk), lambda k: (0, 0, 0, k))

    def down_spec(e):
        return pl.BlockSpec((NZ, 1, PIECE, chunk), lambda k: (0, lax.rem(k + e, NX), 0, k))

    return pl.pallas_call(
        mix_kernel,
        grid=(NX,),
        in_specs=[
            pl.BlockSpec(kron.shape, lambda k: (0, 0)),
            pl.BlockSpec((NZ, 1, 2 * PIECE, chunk), lambda k: (0, k, 0, 0)),
            down_spec(half[0]),
            down_spec(half[1]),
        ]
        + [pl.BlockSpec(memory_space=pl.ANY)] * len(after),
        out_specs=[two_spec, rest_spec, two_spec, rest_spec],
        out_shape=[two, rest, two, rest],
        scratch_shapes=[pltpu.VMEM((4, NZ * PIECE, chunk), bf16)],
        interpret=INTERPRET,
        name="mix",
    )(kron, den.reshape(NZ, NX, 2 * PIECE, chunk), down, down, *after)


def final_kernel(*refs):
    out_ref = refs[-1]
    block = OWN * PIECE
    k = pl.program_id(0)
    for n, half in enumerate(HALVES):
        own, oth, up_num, up_den, dn_num, dn_den = refs[6 * n : 6 * n + 6]
        tot = []
        for arr, up, dn in ((0, up_num, dn_num), (1, up_den, dn_den)):
            tot.append(
                own[arr, 0].astype(f32) + oth[arr, 0].astype(f32) + up[...].astype(f32) + dn[...].astype(f32)
            )
        res = (tot[0] / tot[1]).astype(bf16)
        for j, e in enumerate(half):
            s = lax.rem(k + e, NX)
            for m in range(OWN):
                out_ref[m, s] = res[j * block + m * PIECE : j * block + (m + 1) * PIECE]


def final(groups):
    tall, width = groups[0][2].shape
    chunk = width // NX
    flat = pl.BlockSpec((tall, chunk), lambda k: (0, k))
    rest = pl.BlockSpec((2, 1, tall, chunk), lambda k: (0, 2, 0, k))
    return pl.pallas_call(
        final_kernel,
        grid=(NX,),
        in_specs=[rest, rest, flat, flat, flat, flat] * 2,
        out_specs=pl.BlockSpec((OWN, NX, PIECE, chunk), lambda k: (0, 0, 0, k)),
        out_shape=jax.ShapeDtypeStruct((OWN, NX, PIECE, width), bf16),
        interpret=INTERPRET,
        name="final",
    )(*groups[0], *groups[1])


def sums_kernel(*refs, counts):
    outs = refs[-len(counts) :]
    step = outs[0].shape[1] // COLS

    def body(k, carry):
        cols = pl.ds(pl.multiple_of(k * step, step), step)
        start = 0
        for out, count in zip(outs, counts):
            total = refs[start][:, cols].astype(f32)
            for r in refs[start + 1 : start + count]:
                total = total + r[:, cols].astype(f32)
            out[:, cols] = total.astype(bf16)
            start += count
        return carry

    lax.fori_loop(0, COLS, body, 0)


def sums(*groups):
    specs, args = [], []
    for group in groups:
        for arr, lead in group:
            shape = (None,) * len(lead) + arr.shape[len(lead) :]
            specs.append(pl.BlockSpec(shape, lambda i, lead=lead: lead + (0, 0)))
            args.append(arr)
    shape = groups[0][0][0].shape[-2:]
    return pl.pallas_call(
        functools.partial(sums_kernel, counts=[len(g) for g in groups]),
        grid=(1,),
        in_specs=specs,
        out_specs=[pl.BlockSpec(shape, lambda i: (0, 0))] * len(groups),
        out_shape=[jax.ShapeDtypeStruct(shape, bf16)] * len(groups),
        interpret=INTERPRET,
        name="sums",
    )(*args)


def reduce_slots(snd2, snd, own2, own):
    oth2 = shift(snd2, "c", NC, 1)
    oth = shift(snd, "c", NC, 1)
    two_num, two_den = sums([(own2, (0,)), (oth2, (0,))], [(own2, (1,)), (oth2, (1,))])
    one_den, three_num = sums([(own, (1, 0)), (oth, (1, 0))], [(own, (0, 1)), (oth, (0, 1))])
    up1 = shift(two_num, "y", NY, 1)
    dn1 = shift(two_den, "y", NY, -1)
    up_den = shift(one_den, "y", NY, 1)
    dn_num = shift(three_num, "y", NY, -1)
    one_num, three_den = sums(
        [(own, (0, 0)), (oth, (0, 0)), (up1, ())], [(own, (1, 1)), (oth, (1, 1)), (dn1, ())]
    )
    up_num = shift(one_num, "y", NY, 1)
    dn_den = shift(three_den, "y", NY, -1)
    return (own, oth, up_num, up_den, dn_num, dn_den), (one_num, three_den)


def per_device(tokens, cotangent, routes, route_weights, gate, up, down, cluster, merged_slot):
    width = gate.shape[1]
    chunk = width // NX
    toks = tokens.shape[0]
    per = toks // (NY * NC)
    y, c = lax.axis_index("y"), lax.axis_index("c")
    z, x = lax.axis_index("z"), lax.axis_index("x")
    group = y * NC + c
    first_expert = group * NZ
    here = jnp.stack([y, c, z, x]).astype(jnp.int32)
    blocks = pack(here, routes, route_weights, tokens)
    got = [blocks[0]]
    for n, step in enumerate(STEPS[1:]):
        got.append(shift(blocks[n + 1], "z", NZ, step))
    part_a = jnp.concatenate(got[: NZ // 2])
    part_b = jnp.concatenate(got[NZ // 2 :])
    right_a = shift(part_a, "x", NX, 1)
    left_a = shift(part_a, "x", NX, -1)
    left_b = shift(part_b, "x", NX, -1)
    right_b = shift(part_b, "x", NX, 1)
    far_a = shift(right_a, "x", NX, 1)
    far_b = shift(left_b, "x", NX, -1)

    cot_own = lax.dynamic_slice_in_dim(cotangent, group * per, per, 0)
    cot_own = cot_own.reshape(per, NX, chunk).transpose(1, 0, 2)
    cot_send = jnp.broadcast_to(cot_own[None], (NZ, NX, per, chunk)).reshape(NZ * NX, per, chunk)
    cot0 = lax.all_to_all(cot_send, ("z", "x"), 0, 0, tiled=True)
    cot3 = shift(cot0, "y", NY, 1)
    cot1 = shift(cot0, "y", NY, -1)
    cot2 = shift(cot0, "y", NY, 2)
    cots = []
    for a in (cot0, cot1, cot2, cot3):
        b = shift(a, "c", NC, 1)
        cots += [a.reshape(NZ, NX, per, chunk), b.reshape(NZ, NX, per, chunk)]

    down_recv = lax.all_to_all(down, ("z", "x"), 0, 0, tiled=True)
    down_recv = down_recv.reshape(NZ, NX, PIECE, width)

    (main,) = hidden((part_a, part_b, left_a, left_b, right_a, right_b), gate, up)
    main1 = shift(main, "x", NX, -1)
    late, full = hidden((far_a, far_b), gate, up, main)
    late1 = shift(late, "x", NX, -1)
    full3 = shift(full, "x", NX, -3)
    full2 = shift(full, "x", NX, -2)
    parts = {0: (full,), 1: (main1, late1), 2: (full2,), 3: (full3,)}
    pieces = (part_a, part_b, left_a, left_b, far_a, far_b, right_a, right_b)
    grad_sq = pick(here, pieces, cots, width)

    slot_table = slot_lookup(cluster, merged_slot)
    expert_ids = jnp.arange(EXPERTS, dtype=jnp.int32)
    member = first_expert + jnp.arange(NZ, dtype=jnp.int32)
    member_slot = jnp.sum(
        jnp.where(member[:, None] == expert_ids[None, :], slot_table[None, :], 0), axis=1
    )
    owner_core = (c + jnp.arange(NC, dtype=jnp.int32)) % NC
    owner_y = (y + jnp.arange(NY, dtype=jnp.int32)) % NY
    owner = owner_y[None, :] * NC + owner_core[:, None]
    slots = (owner[:, :, None] * OWN + jnp.arange(OWN, dtype=jnp.int32)).reshape(-1)
    same_slot = jnp.repeat(slots, PIECE)[:, None] == jnp.repeat(member_slot, PIECE)[None, :]
    q_row = jnp.arange(MERGED * PIECE, dtype=jnp.int32)[:, None] % PIECE
    q_col = jnp.arange(NZ * PIECE, dtype=jnp.int32)[None, :] % PIECE
    kron = (same_slot & (q_row == q_col)).astype(bf16)

    groups = []
    after = ()
    for half in HALVES:
        denom = fisher_half(half, parts, grad_sq)
        denom_recv = lax.all_to_all(denom, ("z", "x"), 0, 0, tiled=True)
        mixed = mix(half, kron, denom_recv, down_recv, after)
        group, after = reduce_slots(*mixed)
        groups.append(group)
    return final(groups)


def solution(mesh):
    fine = Mesh(mesh.devices.reshape(NY, NC, NZ, NX), ("y", "c", "z", "x"))
    rows = P(("z", "x"), None)
    units = P(("y", "c", "z", "x"), None)

    return jax.shard_map(
        per_device,
        mesh=fine,
        in_specs=(rows, rows, rows, rows, units, units, units, P(), P()),
        out_specs=P(("y", "c"), None, ("z", "x"), None),
        check_vma=False,
    )
```

profile of v0, /device:TPU:2, one launch (start us, length us, event | category | flops | bytes accessed | tf_op | source)
XLA Modules:
  0.0 310.1 jit_solution(17494793498185254883)
XLA Ops:
  1.1 26.9 %all_to_all.24 = bf16[32,8,896]{2,1,0:T(8,128)(2,1)} all-to-all(bf16[32,8,896]{2,1,0:T(8,128)(2,1)S(1)} %bitcast.32), channel_id=1, replica_groups=mesh['y'=4,'c'=2,'z'=8,'x'=4] {'z','x'}, dimensions={0} | all-to-all | bytes 917504 | tf_op jit(solution)/shard_map/all_to_all | solution.py:414
  28.0 5.6 %all-to-all-start.2 = ((bf16[32,8,3584]{2,1,0:T(8,128)(2,1)}), bf16[32,8,3584]{2,1,0:T(8,128)(2,1)S(1)}, u32[]{:S(2)}, u32[]{:S(2)}) async-start(bf16[32,8,3584]{2,1,0:T(8,128)(2,1)} %bitcast.31), calls=%async_computation.2 | async-start | bytes 3670016 | tf_op jit(solution)/shard_map/all_to_all | solution.py:423
  34.2 3.8 %pack.1 = (bf16[20,3712]{1,0:T(8,128)(2,1)}, bf16[20,3712]{1,0:T(8,128)(2,1)}, bf16[20,3712]{1,0:T(8,128)(2,1)}, bf16[20,3712]{1,0:T(8,128)(2,1)}, bf16[20,3712]...) custom-call(s32[4]{0:T(128)} %pad_add_fusion.here_ref, ...), custom_call_target="tpu_custom_call" | custom-call | tf_op jit(solution)/shard_map/pack/pallas_call | solution.py:93
  38.1 3.6 %collective-permute-start.5 = (bf16[20,3712]{1,0:T(8,128)(2,1)}, bf16[20,3712]{1,0:T(8,128)(2,1)S(1)}, u32[]{:S(2)}, u32[]{:S(2)}) collective-permute-start(bf16[20,3712]{1,0:T(8,128)(2,1)} %get-tuple-element.39), channel_id=1, source_target_pairs={{0,24},{4,28},{8,0},{12,4},{16,8},{20,12},{24,16},{28,20},{1,25},{... | collective-permute-start | bytes 445448 | tf_op jit(solution)/shard_map/ppermute | solution.py:34
  41.9 4.8 %collective-permute-start.7 = (bf16[20,3712]{1,0:T(8,128)(2,1)}, bf16[20,3712]{1,0:T(8,128)(2,1)S(1)}, u32[]{:S(2)}, u32[]{:S(2)}) collective-permute-start(bf16[20,3712]{1,0:T(8,128)(2,1)} %get-tuple-element.41), channel_id=1, source_target_pairs={{0,20},{4,24},{8,28},{12,0},{16,4},{20,8},{24,12},{28,16},{1,21},{... | collective-permute-start | bytes 445448 | tf_op jit(solution)/shard_map/ppermute | solution.py:34
  50.5 37.0 %collective-permute-done.5 = bf16[20,3712]{1,0:T(8,128)(2,1)S(1)} collective-permute-done((bf16[20,3712]{1,0:T(8,128)(2,1)}, bf16[20,3712]{1,0:T(8,128)(2,1)S(1)}, u32[]{:S(2)}, u32[]{:S(2)}) %collective-permute-start.5) | collective-permute-done | bytes 148512 | tf_op jit(solution)/shard_map/ppermute | solution.py:34
  92.1 3.5 %collective-permute-start.2 = (bf16[20,3712]{1,0:T(8,128)(2,1)}, bf16[20,3712]{1,0:T(8,128)(2,1)S(1)}, u32[]{:S(2)}, u32[]{:S(2)}) collective-permute-start(bf16[20,3712]{1,0:T(8,128)(2,1)} %get-tuple-element.38), channel_id=1, source_target_pairs={{0,8},{4,12},{8,16},{12,20},{16,24},{20,28},{24,0},{28,4},{1,9},{5... | collective-permute-start | bytes 445448 | tf_op jit(solution)/shard_map/ppermute | solution.py:34
  100.4 3.9 %collective-permute-done.1 = bf16[20,3712]{1,0:T(8,128)(2,1)S(1)} collective-permute-done((bf16[20,3712]{1,0:T(8,128)(2,1)}, bf16[20,3712]{1,0:T(8,128)(2,1)S(1)}, u32[]{:S(2)}, u32[]{:S(2)}) %collective-permute-start.1) | collective-permute-done | bytes 148512 | tf_op jit(solution)/shard_map/ppermute | solution.py:34
  104.9 3.7 %collective-permute-start.3 = (bf16[80,3712]{1,0:T(8,128)(2,1)S(1)}, bf16[80,3712]{1,0:T(8,128)(2,1)}, u32[]{:S(2)}, u32[]{:S(2)}) collective-permute-start(bf16[80,3712]{1,0:T(8,128)(2,1)S(1)} %pad_maximum_fusion.refs_0_), channel_id=1, source_target_pairs={{0,1},{1,2},{2,3},{3,0},{4,5},{5,6},{6,7},{7,4},{8,9},{9,10},{10,1... | collective-permute-start | bytes 1781768 | tf_op jit(solution)/shard_map/ppermute | solution.py:34
  116.1 6.3 %collective-permute-done.3.refs_4_.refs_6_ = bf16[80,3712]{1,0:T(8,128)(2,1)} collective-permute-done((bf16[80,3712]{1,0:T(8,128)(2,1)S(1)}, bf16[80,3712]{1,0:T(8,128)(2,1)}, u32[]{:S(2)}, u32[]{:S(2)}) %collective-permute-start.3) | collective-permute-done | bytes 593952 | tf_op jit(solution)/shard_map/ppermute | solution.py:34
  122.4 3.2 %collective-permute-start.18 = (bf16[32,8,896]{2,1,0:T(8,128)(2,1)}, bf16[32,8,896]{2,1,0:T(8,128)(2,1)}, u32[]{:S(2)}, u32[]{:S(2)}) collective-permute-start(bf16[32,8,896]{2,1,0:T(8,128)(2,1)} %all_to_all.24), channel_id=1, source_target_pairs={{0,128},{64,192},{128,0},{192,64},{1,129},{65,193},{129,1},{193,65... | collective-permute-start | bytes 1376264 | tf_op jit(solution)/shard_map/ppermute | solution.py:34
  125.6 5.7 %collective-permute-done.12.refs_5_.refs_7_ = bf16[80,3712]{1,0:T(8,128)(2,1)S(1)} collective-permute-done((bf16[80,3712]{1,0:T(8,128)(2,1)S(1)}, bf16[80,3712]{1,0:T(8,128)(2,1)S(1)}, u32[]{:S(2)}, u32[]{:S(2)}) %collective-permute-start.12) | collective-permute-done | bytes 593952 | tf_op jit(solution)/shard_map/ppermute | solution.py:34
  136.2 6.7 %collective-permute-done.20 = bf16[32,8,896]{2,1,0:T(8,128)(2,1)} collective-permute-done((bf16[32,8,896]{2,1,0:T(8,128)(2,1)}, bf16[32,8,896]{2,1,0:T(8,128)(2,1)}, u32[]{:S(2)}, u32[]{:S(2)}) %collective-permute-start.20) | collective-permute-done | bytes 458784 | tf_op jit(solution)/shard_map/ppermute | solution.py:34
  143.0 6.5 %hidden.2.refs_4_ = bf16[480,256]{1,0:T(8,128)(2,1)} custom-call(bf16[80,3712]{1,0:T(8,128)(2,1)} %copy-done.5, bf16[80,3712]{1,0:T(8,128)(2,1)} %copy-done.4, bf16[80,3712]{1,0:T(8,128)(2,1)} %copy-done.11, bf16[80,3712]{1,0:T(8,128)(2,1)} %copy-done.9, bf16[80,3712]{1,0:T(8,128)(2,1)} %collective-permute-done.3.refs_4_.refs_6_, ...), custom_call_target="tpu_custom_call" | custom-call | tf_op jit(solution)/shard_map/hidden/pallas_call | solution.py:202
  151.8 5.1 %hidden.3 = (bf16[160,256]{1,0:T(8,128)(2,1)}, bf16[640,256]{1,0:T(8,128)(2,1)}) custom-call(bf16[80,3712]{1,0:T(8,128)(2,1)} %collective-permute-done.4.refs_0_.refs_4_, bf16[80,3712]{1,0:T(8,128)(2,1)} %copy-done.12, bf16[256,3584]{1,0:T(8,128)(2,1)} %refs_2_.1, bf16[256,3584]{1,0:T(8,128)(2,1)} %refs_3_.1, bf16[480,256]{1,0:T(8,128)(2,1)} %hidden.2.refs_4_), custom_call_target="tpu_custom_call" | custom-call | tf_op jit(solution)/shard_map/hidden/pallas_call | solution.py:202
  158.9 7.3 %pick.1 = bf16[8,80,896]{2,1,0:T(8,128)(2,1)} custom-call(s32[4]{0:T(128)} %pad_add_fusion.here_ref, bf16[80,3712]{1,0:T(8,128)(2,1)} %copy-done.5, bf16[80,3712]{1,0:T(8,128)(2,1)} %copy-done.4, bf16[80,3712]{1,0:T(8,128)(2,1)} %copy-done.11, bf16[80,3712]{1,0:T(8,128)(2,1)} %copy-done.9, bf16[80,3712]{1,0:T(8,128)(2,1)} %collective-permute-done.4.refs_0_.refs_4_, ...), custom_call_target="tpu_custom_call" | custom-call | tf_op jit(solution)/shard_map/pick/pallas_call | solution.py:148
  166.9 3.5 %fisher.2 = bf16[32,16,896]{2,1,0:T(8,128)(2,1)} custom-call(bf16[640,256]{1,0:T(8,128)(2,1)} %get-tuple-element.43.refs_0_, bf16[480,256]{1,0:T(8,128)(2,1)} %copy-done.24, bf16[160,256]{1,0:T(8,128)(2,1)} %copy-done.26, bf16[4,160,896]{2,1,0:T(8,128)(2,1)} %bitcast.27), custom_call_target="tpu_custom_call" | custom-call | tf_op jit(solution)/shard_map/fisher/pallas_call | solution.py:234
  170.5 8.4 %all-to-all-start.1 = ((bf16[32,16,896]{2,1,0:T(8,128)(2,1)}), bf16[32,16,896]{2,1,0:T(8,128)(2,1)S(1)}, u32[]{:S(2)}, u32[]{:S(2)}) async-start(bf16[32,16,896]{2,1,0:T(8,128)(2,1)} %fisher.2), calls=%async_computation.1 | async-start | bytes 1835008 | tf_op jit(solution)/shard_map/all_to_all | solution.py:455
  184.0 20.1 %all-to-all-done.1 = bf16[32,16,896]{2,1,0:T(8,128)(2,1)S(1)} async-done(((bf16[32,16,896]{2,1,0:T(8,128)(2,1)}), bf16[32,16,896]{2,1,0:T(8,128)(2,1)S(1)}, u32[]{:S(2)}, u32[]{:S(2)}) %all-to-all-start.1) | async-done | bytes 917536 | tf_op jit(solution)/shard_map/all_to_all | solution.py:455
  205.1 6.7 %mix.2 = (bf16[2,48,3584]{2,1,0:T(8,128)(2,1)}, bf16[2,3,48,3584]{3,2,1,0:T(8,128)(2,1)}, bf16[2,48,3584]{2,1,0:T(8,128)(2,1)}, bf16[2,3,48,3584]{3,2,1,0:T(8,128)(2,1)}) custom-call(bf16[192,64]{1,0:T(8,128)(2,1)} %and_convert_fusion.kron_ref, bf16[8,4,16,896]{3,2,1,0:T(8,128)(2,1)} %bitcast.30, bf16[8,4,8,3584]{3,2,1,0:T(8,128)(2,1)} %bitcast.23, ...), custom_call_target="tpu_custom_call" | custom-call | tf_op jit(solution)/shard_map/mix/pallas_call | solution.py:282
  211.9 3.5 %fisher.3 = bf16[32,16,896]{2,1,0:T(8,128)(2,1)} custom-call(bf16[640,256]{1,0:T(8,128)(2,1)} %collective-permute-done.30.refs_0_, bf16[640,256]{1,0:T(8,128)(2,1)} %collective-permute-done.31.refs_1_, bf16[4,160,896]{2,1,0:T(8,128)(2,1)} %bitcast.28), custom_call_target="tpu_custom_call" | custom-call | tf_op jit(solution)/shard_map/fisher/pallas_call | solution.py:234
  215.4 5.6 %all-to-all-start.3 = ((bf16[32,16,896]{2,1,0:T(8,128)(2,1)}), bf16[32,16,896]{2,1,0:T(8,128)(2,1)S(1)}, u32[]{:S(2)}, u32[]{:S(2)}) async-start(bf16[32,16,896]{2,1,0:T(8,128)(2,1)} %fisher.3), calls=%async_computation.3 | async-start | bytes 1835008 | tf_op jit(solution)/shard_map/all_to_all | solution.py:455
  226.0 3.0 collective-permute-start.25
  229.1 8.3 %collective-permute-done.24.refs_2_ = bf16[48,3584]{1,0:T(8,128)(2,1)S(1)} collective-permute-done((bf16[48,3584]{1,0:T(8,128)(2,1)}, bf16[48,3584]{1,0:T(8,128)(2,1)S(1)}, u32[]{:S(2)}, u32[]{:S(2)}) %collective-permute-start.24) | collective-permute-done | bytes 344096 | tf_op jit(solution)/shard_map/ppermute | solution.py:34
  242.2 4.6 %all-to-all-done.3 = bf16[32,16,896]{2,1,0:T(8,128)(2,1)S(1)} async-done(((bf16[32,16,896]{2,1,0:T(8,128)(2,1)}), bf16[32,16,896]{2,1,0:T(8,128)(2,1)S(1)}, u32[]{:S(2)}, u32[]{:S(2)}) %all-to-all-start.3) | async-done | bytes 917536 | tf_op jit(solution)/shard_map/all_to_all | solution.py:455
  247.8 6.8 %mix.3 = (bf16[2,48,3584]{2,1,0:T(8,128)(2,1)}, bf16[2,3,48,3584]{3,2,1,0:T(8,128)(2,1)}, bf16[2,48,3584]{2,1,0:T(8,128)(2,1)}, bf16[2,3,48,3584]{3,2,1,0:T(8,128)(2,1)}) custom-call(bf16[192,64]{1,0:T(8,128)(2,1)} %and_convert_fusion.kron_ref, bf16[8,4,16,896]{3,2,1,0:T(8,128)(2,1)} %bitcast.29, bf16[8,4,8,3584]{3,2,1,0:T(8,128)(2,1)} %bitcast.25, ...), custom_call_target="tpu_custom_call" | custom-call | tf_op jit(solution)/shard_map/mix/pallas_call | solution.py:282
  255.1 4.8 %collective-permute-done.33.refs_1_.refs_3_ = bf16[2,48,3584]{2,1,0:T(8,128)(2,1)S(1)} collective-permute-done((bf16[2,48,3584]{2,1,0:T(8,128)(2,1)}, bf16[2,48,3584]{2,1,0:T(8,128)(2,1)S(1)}, u32[]{:S(2)}, u32[]{:S(2)}) %collective-permute-start.33) | collective-permute-done | bytes 688160 | tf_op jit(solution)/shard_map/ppermute | solution.py:34
  268.6 3.2 %collective-permute-start.28 = (bf16[48,3584]{1,0:T(8,128)(2,1)}, bf16[48,3584]{1,0:T(8,128)(2,1)S(1)}, u32[]{:S(2)}, u32[]{:S(2)}) collective-permute-start(bf16[48,3584]{1,0:T(8,128)(2,1)} %get-tuple-element.53), channel_id=1, source_target_pairs={{0,192},{64,0},{128,64},{192,128},{1,193},{65,1},{129,65},{193,129... | collective-permute-start | bytes 1032200 | tf_op jit(solution)/shard_map/ppermute | solution.py:34
  284.8 5.3 %collective-permute-done.26.refs_2_ = bf16[48,3584]{1,0:T(8,128)(2,1)S(1)} collective-permute-done((bf16[48,3584]{1,0:T(8,128)(2,1)}, bf16[48,3584]{1,0:T(8,128)(2,1)S(1)}, u32[]{:S(2)}, u32[]{:S(2)}) %collective-permute-start.26) | collective-permute-done | bytes 344096 | tf_op jit(solution)/shard_map/ppermute | solution.py:34
  290.7 6.8 %collective-permute-done.37.refs_9_ = bf16[48,3584]{1,0:T(8,128)(2,1)S(1)} collective-permute-done((bf16[48,3584]{1,0:T(8,128)(2,1)}, bf16[48,3584]{1,0:T(8,128)(2,1)S(1)}, u32[]{:S(2)}, u32[]{:S(2)}) %collective-permute-start.37) | collective-permute-done | bytes 344096 | tf_op jit(solution)/shard_map/ppermute | solution.py:34
  297.5 6.5 %collective-permute-done.36.refs_8_ = bf16[48,3584]{1,0:T(8,128)(2,1)S(1)} collective-permute-done((bf16[48,3584]{1,0:T(8,128)(2,1)}, bf16[48,3584]{1,0:T(8,128)(2,1)S(1)}, u32[]{:S(2)}, u32[]{:S(2)}) %collective-permute-start.36) | collective-permute-done | bytes 344096 | tf_op jit(solution)/shard_map/ppermute | solution.py:34
  305.5 4.5 %final.1 = bf16[3,4,8,3584]{3,2,1,0:T(8,128)(2,1)} custom-call(bf16[2,3,48,3584]{3,2,1,0:T(8,128)(2,1)} %get-tuple-element.45.refs_0_.refs_3_.refs_2_, bf16[2,3,48,3584]{3,2,1,0:T(8,128)(2,1)} %copy-done.1, bf16[48,3584]{1,0:T(8,128)(2,1)} %copy-done.15, bf16[48,3584]{1,0:T(8,128)(2,1)} %copy-done.13, bf16[48,3584]{1,0:T(8,128)(2,1)} %copy-done.14, ...), custom_call_target="tpu_custom_call" | custom-call | tf_op jit(solution)/shard_map/final/pallas_call | solution.py:323
  (150 shorter events, 74.2 us)
Async XLA Ops:
  28.0 142.4 %all-to-all-start.2 = ((bf16[32,8,3584]{2,1,0:T(8,128)(2,1)}), bf16[32,8,3584]{2,1,0:T(8,128)(2,1)S(1)}, u32[]{:S(2)}, u32[]{:S(2)}) async-start(bf16[32,8,3584]{2,1,0:T(8,128)(2,1)} %bitcast.31), calls=%async_computation.2 | async-start | bytes 3670016 | tf_op jit(solution)/shard_map/all_to_all | solution.py:423
  38.1 49.5 %collective-permute-start.5 = (bf16[20,3712]{1,0:T(8,128)(2,1)}, bf16[20,3712]{1,0:T(8,128)(2,1)S(1)}, u32[]{:S(2)}, u32[]{:S(2)}) collective-permute-start(bf16[20,3712]{1,0:T(8,128)(2,1)} %get-tuple-element.39), channel_id=1, source_target_pairs={{0,24},{4,28},{8,0},{12,4},{16,8},{20,12},{24,16},{28,20},{1,25},{... | collective-permute-start | bytes 445448 | tf_op jit(solution)/shard_map/ppermute | solution.py:34
  41.7 50.4 %collective-permute-start.6 = (bf16[20,3712]{1,0:T(8,128)(2,1)}, bf16[20,3712]{1,0:T(8,128)(2,1)S(1)}, u32[]{:S(2)}, u32[]{:S(2)}) collective-permute-start(bf16[20,3712]{1,0:T(8,128)(2,1)} %get-tuple-element.40), channel_id=1, source_target_pairs={{0,12},{4,16},{8,20},{12,24},{16,28},{20,0},{24,4},{28,8},{1,13},{... | collective-permute-start | bytes 445448 | tf_op jit(solution)/shard_map/ppermute | solution.py:34
  41.9 55.4 %collective-permute-start.7 = (bf16[20,3712]{1,0:T(8,128)(2,1)}, bf16[20,3712]{1,0:T(8,128)(2,1)S(1)}, u32[]{:S(2)}, u32[]{:S(2)}) collective-permute-start(bf16[20,3712]{1,0:T(8,128)(2,1)} %get-tuple-element.41), channel_id=1, source_target_pairs={{0,20},{4,24},{8,28},{12,0},{16,4},{20,8},{24,12},{28,16},{1,21},{... | collective-permute-start | bytes 445448 | tf_op jit(solution)/shard_map/ppermute | solution.py:34
  46.7 51.4 %collective-permute-start.8 = (bf16[20,3712]{1,0:T(8,128)(2,1)}, bf16[20,3712]{1,0:T(8,128)(2,1)S(1)}, u32[]{:S(2)}, u32[]{:S(2)}) collective-permute-start(bf16[20,3712]{1,0:T(8,128)(2,1)} %get-tuple-element.42), channel_id=1, source_target_pairs={{0,16},{4,20},{8,24},{12,28},{16,0},{20,4},{24,8},{28,12},{1,17},{... | collective-permute-start | bytes 445448 | tf_op jit(solution)/shard_map/ppermute | solution.py:34
  49.0 51.4 %collective-permute-start = (bf16[20,3712]{1,0:T(8,128)(2,1)}, bf16[20,3712]{1,0:T(8,128)(2,1)S(1)}, u32[]{:S(2)}, u32[]{:S(2)}) collective-permute-start(bf16[20,3712]{1,0:T(8,128)(2,1)} %get-tuple-element.36), channel_id=1, source_target_pairs={{0,4},{4,8},{8,12},{12,16},{16,20},{20,24},{24,28},{28,0},{1,5},{5... | collective-permute-start | bytes 445448 | tf_op jit(solution)/shard_map/ppermute | solution.py:34
  87.5 16.8 %collective-permute-start.1 = (bf16[20,3712]{1,0:T(8,128)(2,1)}, bf16[20,3712]{1,0:T(8,128)(2,1)S(1)}, u32[]{:S(2)}, u32[]{:S(2)}) collective-permute-start(bf16[20,3712]{1,0:T(8,128)(2,1)} %get-tuple-element.37), channel_id=1, source_target_pairs={{0,28},{4,0},{8,4},{12,8},{16,12},{20,16},{24,20},{28,24},{1,29},{... | collective-permute-start | bytes 445448 | tf_op jit(solution)/shard_map/ppermute | solution.py:34
  104.9 17.6 %collective-permute-start.3 = (bf16[80,3712]{1,0:T(8,128)(2,1)S(1)}, bf16[80,3712]{1,0:T(8,128)(2,1)}, u32[]{:S(2)}, u32[]{:S(2)}) collective-permute-start(bf16[80,3712]{1,0:T(8,128)(2,1)S(1)} %pad_maximum_fusion.refs_0_), channel_id=1, source_target_pairs={{0,1},{1,2},{2,3},{3,0},{4,5},{5,6},{6,7},{7,4},{8,9},{9,10},{10,1... | collective-permute-start | bytes 1781768 | tf_op jit(solution)/shard_map/ppermute | solution.py:34
  108.6 22.7 %collective-permute-start.12 = (bf16[80,3712]{1,0:T(8,128)(2,1)S(1)}, bf16[80,3712]{1,0:T(8,128)(2,1)S(1)}, u32[]{:S(2)}, u32[]{:S(2)}) collective-permute-start(bf16[80,3712]{1,0:T(8,128)(2,1)S(1)} %pad_maximum_fusion.1.refs_1_), channel_id=1, source_target_pairs={{0,1},{1,2},{2,3},{3,0},{4,5},{5,6},{6,7},{7,4},{8,9},{9,10},{10,1... | collective-permute-start | bytes 1781768 | tf_op jit(solution)/shard_map/ppermute | solution.py:34
  110.1 22.8 %collective-permute-start.11 = (bf16[80,3712]{1,0:T(8,128)(2,1)S(1)}, bf16[80,3712]{1,0:T(8,128)(2,1)S(1)}, u32[]{:S(2)}, u32[]{:S(2)}) collective-permute-start(bf16[80,3712]{1,0:T(8,128)(2,1)S(1)} %pad_maximum_fusion.refs_0_), channel_id=1, source_target_pairs={{0,3},{1,0},{2,1},{3,2},{4,7},{5,4},{6,5},{7,6},{8,11},{9,8},{10,9... | collective-permute-start | bytes 1781768 | tf_op jit(solution)/shard_map/ppermute | solution.py:34
  111.0 23.9 %collective-permute-start.10 = (bf16[80,3712]{1,0:T(8,128)(2,1)S(1)}, bf16[80,3712]{1,0:T(8,128)(2,1)S(1)}, u32[]{:S(2)}, u32[]{:S(2)}) collective-permute-start(bf16[80,3712]{1,0:T(8,128)(2,1)S(1)} %collective-permute-done.9.refs_3_), channel_id=1, source_target_pairs={{0,3},{1,0},{2,1},{3,2},{4,7},{5,4},{6,5},{7,6},{8,11},{9,8},{10,9... | collective-permute-start | bytes 1781768 | tf_op jit(solution)/shard_map/ppermute | solution.py:34
  113.1 21.8 %collective-permute-start.16 = (bf16[32,8,896]{2,1,0:T(8,128)(2,1)}, bf16[32,8,896]{2,1,0:T(8,128)(2,1)}, u32[]{:S(2)}, u32[]{:S(2)}) collective-permute-start(bf16[32,8,896]{2,1,0:T(8,128)(2,1)} %all_to_all.24), channel_id=1, source_target_pairs={{0,192},{64,0},{128,64},{192,128},{1,193},{65,1},{129,65},{193,129... | collective-permute-start | bytes 1376264 | tf_op jit(solution)/shard_map/ppermute | solution.py:34
  132.9 16.5 %collective-permute-start.4 = (bf16[80,3712]{1,0:T(8,128)(2,1)}, bf16[80,3712]{1,0:T(8,128)(2,1)}, u32[]{:S(2)}, u32[]{:S(2)}) collective-permute-start(bf16[80,3712]{1,0:T(8,128)(2,1)} %collective-permute-done.3.refs_4_.refs_6_), channel_id=1, source_target_pairs={{0,1},{1,2},{2,3},{3,0},{4,5},{5,6},{6,7},{7,4},{8,9},{9,10},{10,1... | collective-permute-start | bytes 1781768 | tf_op jit(solution)/shard_map/ppermute | solution.py:34
  134.9 21.9 %collective-permute-start.15 = (bf16[32,8,896]{2,1,0:T(8,128)(2,1)}, bf16[32,8,896]{2,1,0:T(8,128)(2,1)}, u32[]{:S(2)}, u32[]{:S(2)}) collective-permute-start(bf16[32,8,896]{2,1,0:T(8,128)(2,1)} %all_to_all.24), channel_id=1, source_target_pairs={{0,32},{32,0},{1,33},{33,1},{2,34},{34,2},{3,35},{35,3},{4,36},{36... | collective-permute-start | bytes 1376264 | tf_op jit(solution)/shard_map/ppermute | solution.py:34
  135.7 23.2 %collective-permute-start.17 = (bf16[32,8,896]{2,1,0:T(8,128)(2,1)}, bf16[32,8,896]{2,1,0:T(8,128)(2,1)}, u32[]{:S(2)}, u32[]{:S(2)}) collective-permute-start(bf16[32,8,896]{2,1,0:T(8,128)(2,1)} %collective-permute-done.16), channel_id=1, source_target_pairs={{0,32},{32,0},{1,33},{33,1},{2,34},{34,2},{3,35},{35,3},{4,36},{36... | collective-permute-start | bytes 1376264 | tf_op jit(solution)/shard_map/ppermute | solution.py:34
  135.7 23.2 %collective-permute-start.19 = (bf16[32,8,896]{2,1,0:T(8,128)(2,1)}, bf16[32,8,896]{2,1,0:T(8,128)(2,1)}, u32[]{:S(2)}, u32[]{:S(2)}) collective-permute-start(bf16[32,8,896]{2,1,0:T(8,128)(2,1)} %collective-permute-done.18), channel_id=1, source_target_pairs={{0,32},{32,0},{1,33},{33,1},{2,34},{34,2},{3,35},{35,3},{4,36},{36... | collective-permute-start | bytes 1376264 | tf_op jit(solution)/shard_map/ppermute | solution.py:34
  143.0 16.0 %collective-permute-start.21 = (bf16[32,8,896]{2,1,0:T(8,128)(2,1)}, bf16[32,8,896]{2,1,0:T(8,128)(2,1)}, u32[]{:S(2)}, u32[]{:S(2)}) collective-permute-start(bf16[32,8,896]{2,1,0:T(8,128)(2,1)} %collective-permute-done.20), channel_id=1, source_target_pairs={{0,32},{32,0},{1,33},{33,1},{2,34},{34,2},{3,35},{35,3},{4,36},{36... | collective-permute-start | bytes 1376264 | tf_op jit(solution)/shard_map/ppermute | solution.py:34
  149.5 16.7 %collective-permute-start.13 = (bf16[480,256]{1,0:T(8,128)(2,1)}, bf16[480,256]{1,0:T(8,128)(2,1)S(1)}, u32[]{:S(2)}, u32[]{:S(2)}) collective-permute-start(bf16[480,256]{1,0:T(8,128)(2,1)} %hidden.2.refs_4_), channel_id=1, source_target_pairs={{0,3},{1,0},{2,1},{3,2},{4,7},{5,4},{6,5},{7,6},{8,11},{9,8},{10,9... | collective-permute-start | bytes 737288 | tf_op jit(solution)/shard_map/ppermute | solution.py:34
  170.5 33.7 %all-to-all-start.1 = ((bf16[32,16,896]{2,1,0:T(8,128)(2,1)}), bf16[32,16,896]{2,1,0:T(8,128)(2,1)S(1)}, u32[]{:S(2)}, u32[]{:S(2)}) async-start(bf16[32,16,896]{2,1,0:T(8,128)(2,1)} %fisher.2), calls=%async_computation.1 | async-start | bytes 1835008 | tf_op jit(solution)/shard_map/all_to_all | solution.py:455
  180.3 31.6 %collective-permute-start.30 = (bf16[640,256]{1,0:T(8,128)(2,1)S(1)}, bf16[640,256]{1,0:T(8,128)(2,1)}, u32[]{:S(2)}, u32[]{:S(2)}) collective-permute-start(bf16[640,256]{1,0:T(8,128)(2,1)S(1)} %copy-done.23), channel_id=1, source_target_pairs={{0,1},{1,2},{2,3},{3,0},{4,5},{5,6},{6,7},{7,4},{8,9},{9,10},{10,1... | collective-permute-start | bytes 983048 | tf_op jit(solution)/shard_map/ppermute | solution.py:34
  181.8 30.1 %collective-permute-start.31 = (bf16[640,256]{1,0:T(8,128)(2,1)S(1)}, bf16[640,256]{1,0:T(8,128)(2,1)}, u32[]{:S(2)}, u32[]{:S(2)}) collective-permute-start(bf16[640,256]{1,0:T(8,128)(2,1)S(1)} %copy-done.23), channel_id=1, source_target_pairs={{0,2},{1,3},{2,0},{3,1},{4,6},{5,7},{6,4},{7,5},{8,10},{9,11},{10,... | collective-permute-start | bytes 983048 | tf_op jit(solution)/shard_map/ppermute | solution.py:34
  211.9 25.5 %collective-permute-start.22 = (bf16[2,3,48,3584]{3,2,1,0:T(8,128)(2,1)}, bf16[2,3,48,3584]{3,2,1,0:T(8,128)(2,1)S(1)}, u32[]{:S(2)}, u32[]{:S(2)}) collective-permute-start(bf16[2,3,48,3584]{3,2,1,0:T(8,128)(2,1)} %get-tuple-element.46), channel_id=1, source_target_pairs={{0,32},{32,0},{1,33},{33,1},{2,34},{34,2},{3,35},{35,3},{4,36},{36... | collective-permute-start | bytes 6193160 | tf_op jit(solution)/shard_map/ppermute | solution.py:34
  215.4 31.5 %all-to-all-start.3 = ((bf16[32,16,896]{2,1,0:T(8,128)(2,1)}), bf16[32,16,896]{2,1,0:T(8,128)(2,1)S(1)}, u32[]{:S(2)}, u32[]{:S(2)}) async-start(bf16[32,16,896]{2,1,0:T(8,128)(2,1)} %fisher.3), calls=%async_computation.3 | async-start | bytes 1835008 | tf_op jit(solution)/shard_map/all_to_all | solution.py:455
  254.6 17.3 %collective-permute-start.32 = (bf16[2,3,48,3584]{3,2,1,0:T(8,128)(2,1)}, bf16[2,3,48,3584]{3,2,1,0:T(8,128)(2,1)S(1)}, u32[]{:S(2)}, u32[]{:S(2)}) collective-permute-start(bf16[2,3,48,3584]{3,2,1,0:T(8,128)(2,1)} %get-tuple-element.56), channel_id=1, source_target_pairs={{0,32},{32,0},{1,33},{33,1},{2,34},{34,2},{3,35},{35,3},{4,36},{36... | collective-permute-start | bytes 6193160 | tf_op jit(solution)/shard_map/ppermute | solution.py:34
  263.2 14.2 %collective-permute-start.35 = (bf16[48,3584]{1,0:T(8,128)(2,1)}, bf16[48,3584]{1,0:T(8,128)(2,1)}, u32[]{:S(2)}, u32[]{:S(2)}) collective-permute-start(bf16[48,3584]{1,0:T(8,128)(2,1)} %get-tuple-element.60), channel_id=1, source_target_pairs={{0,192},{64,0},{128,64},{192,128},{1,193},{65,1},{129,65},{193,129... | collective-permute-start | bytes 1032200 | tf_op jit(solution)/shard_map/ppermute | solution.py:34
  268.6 14.2 %collective-permute-start.27 = (bf16[48,3584]{1,0:T(8,128)(2,1)}, bf16[48,3584]{1,0:T(8,128)(2,1)S(1)}, u32[]{:S(2)}, u32[]{:S(2)}) collective-permute-start(bf16[48,3584]{1,0:T(8,128)(2,1)} %get-tuple-element.52), channel_id=1, source_target_pairs={{0,64},{64,128},{128,192},{192,0},{1,65},{65,129},{129,193},{193,1... | collective-permute-start | bytes 1032200 | tf_op jit(solution)/shard_map/ppermute | solution.py:34
  268.6 14.8 %collective-permute-start.28 = (bf16[48,3584]{1,0:T(8,128)(2,1)}, bf16[48,3584]{1,0:T(8,128)(2,1)S(1)}, u32[]{:S(2)}, u32[]{:S(2)}) collective-permute-start(bf16[48,3584]{1,0:T(8,128)(2,1)} %get-tuple-element.53), channel_id=1, source_target_pairs={{0,192},{64,0},{128,64},{192,128},{1,193},{65,1},{129,65},{193,129... | collective-permute-start | bytes 1032200 | tf_op jit(solution)/shard_map/ppermute | solution.py:34
  271.9 18.3 %collective-permute-start.26 = (bf16[48,3584]{1,0:T(8,128)(2,1)}, bf16[48,3584]{1,0:T(8,128)(2,1)S(1)}, u32[]{:S(2)}, u32[]{:S(2)}) collective-permute-start(bf16[48,3584]{1,0:T(8,128)(2,1)} %get-tuple-element.51.refs_0_), channel_id=1, source_target_pairs={{0,64},{64,128},{128,192},{192,0},{1,65},{65,129},{129,193},{193,1... | collective-permute-start | bytes 1032200 | tf_op jit(solution)/shard_map/ppermute | solution.py:34
  275.6 15.1 %collective-permute-start.29 = (bf16[48,3584]{1,0:T(8,128)(2,1)}, bf16[48,3584]{1,0:T(8,128)(2,1)S(1)}, u32[]{:S(2)}, u32[]{:S(2)}) collective-permute-start(bf16[48,3584]{1,0:T(8,128)(2,1)} %get-tuple-element.54.refs_1_), channel_id=1, source_target_pairs={{0,192},{64,0},{128,64},{192,128},{1,193},{65,1},{129,65},{193,129... | collective-permute-start | bytes 1032200 | tf_op jit(solution)/shard_map/ppermute | solution.py:34
  277.4 20.1 %collective-permute-start.37 = (bf16[48,3584]{1,0:T(8,128)(2,1)}, bf16[48,3584]{1,0:T(8,128)(2,1)S(1)}, u32[]{:S(2)}, u32[]{:S(2)}) collective-permute-start(bf16[48,3584]{1,0:T(8,128)(2,1)} %get-tuple-element.62), channel_id=1, source_target_pairs={{0,64},{64,128},{128,192},{192,0},{1,65},{65,129},{129,193},{193,1... | collective-permute-start | bytes 1032200 | tf_op jit(solution)/shard_map/ppermute | solution.py:34
  282.8 14.7 %collective-permute-start.38 = (bf16[48,3584]{1,0:T(8,128)(2,1)S(1)}, bf16[48,3584]{1,0:T(8,128)(2,1)S(1)}, u32[]{:S(2)}, u32[]{:S(2)}) collective-permute-start(bf16[48,3584]{1,0:T(8,128)(2,1)S(1)} %copy-done.27), channel_id=1, source_target_pairs={{0,192},{64,0},{128,64},{192,128},{1,193},{65,1},{129,65},{193,129... | collective-permute-start | bytes 1032200 | tf_op jit(solution)/shard_map/ppermute | solution.py:34
  283.4 20.7 %collective-permute-start.36 = (bf16[48,3584]{1,0:T(8,128)(2,1)}, bf16[48,3584]{1,0:T(8,128)(2,1)S(1)}, u32[]{:S(2)}, u32[]{:S(2)}) collective-permute-start(bf16[48,3584]{1,0:T(8,128)(2,1)} %get-tuple-element.61), channel_id=1, source_target_pairs={{0,64},{64,128},{128,192},{192,0},{1,65},{65,129},{129,193},{193,1... | collective-permute-start | bytes 1032200 | tf_op jit(solution)/shard_map/ppermute | solution.py:34
  (41 other events, 453.8 us)
where the time goes:
time: 311 us; the launch traced here: 310 us
  waiting for transfers between devices  129 us (41%)
  starting transfers between devices  77.6 us (25%)
  Pallas kernels  62.3 us (20%)
  blocking collectives  26.9 us (9%)
  local copies, waits for them, and re-layouts  11.2 us (4%)
    ppermute x40, waiting for transfers between devices, shift(): return lax.ppermute(a, axis, [(i, (i + step) % size) for i in range(size)])  104 us
    ppermute x40, starting transfers between devices, shift(): return lax.ppermute(a, axis, [(i, (i + step) % size) for i in range(size)])  58.1 us
    all_to_all x1, blocking collectives, per_device(): cot0 = lax.all_to_all(cot_send, ('z', 'x'), 0, 0, tiled=True)  26.9 us
    all_to_all x2, waiting for transfers between devices, per_device(): denom_recv = lax.all_to_all(denom, ('z', 'x'), 0, 0, tiled=True)  24.7 us
    pallas_call x6, Pallas kernels, sums(): pl.pallas_call(functools.partial(sums_kernel, counts=[len(g) for g in gro...  14.6 us
    all_to_all x2, starting transfers between devices, per_device(): denom_recv = lax.all_to_all(denom, ('z', 'x'), 0, 0, tiled=True)  13.9 us
    pallas_call x2, Pallas kernels, mix(): pl.pallas_call(mix_kernel, grid=(NX,), in_specs=[pl.BlockSpec(kron.shape,...  13.5 us
    pallas_call x2, Pallas kernels, hidden(): pl.pallas_call(functools.partial(hidden_kernel, pieces=len(pieces), known...  11.6 us
  transfers between devices with their start and end apart: 43, of which 21 were waited for; matrix products, arithmetic and copies ran while one was open for 1% of the time, Pallas kernels for 16%

commit v1 on v0

--- a/solution.py
+++ b/solution.py
@@ -100,8 +100,9 @@
     )(here, routes.T, weights.T, tokens)
 
 
-def pick_kernel(here_ref, *refs):
-    tails, cots, out_ref, tail_ref = refs[: 2 * NX], refs[2 * NX : -2], refs[-2], refs[-1]
+def pick_kernel(here_ref, *refs, ahead):
+    count = 2 * len(ahead)
+    tails, cots, out_ref, tail_ref = refs[:count], refs[count:-2], refs[-2], refs[-1]
     group = NZ // 2
     height = group * CAP
     per = cots[0].shape[2]
@@ -120,7 +121,10 @@
 
     def body(n, carry):
         half = n % 2
-        xs = lax.rem(x + n // 2, NX)
+        turn = ahead[0]
+        for i in range(1, len(ahead)):
+            turn = jnp.where(n // 2 == i, ahead[i], turn)
+        xs = lax.rem(x + turn, NX)
         wide = jnp.dot(tail_ref[n], spread, preferred_element_type=f32)
         high = jnp.where(same, wide[:, : group * tok], 0.0).astype(bf16)
         low = jnp.where(same, wide[:, group * tok :], 0.0).astype(bf16)
@@ -136,28 +140,29 @@
         out_ref[n] = (val * val).astype(bf16)
         return carry
 
-    lax.fori_loop(0, 2 * NX, body, 0)
-
-
-def pick(here, pieces, cots, width):
+    lax.fori_loop(0, count, body, 0)
+
+
+def pick(here, ahead, pieces, cots, width):
     lanes = pieces[0].shape[1] - width
     height = pieces[0].shape[0]
     chunk = cots[0].shape[-1]
+    count = len(pieces)
     tail = pl.BlockSpec((height, lanes), lambda i, src: (0, width // lanes))
     whole = lambda a: pl.BlockSpec(a.shape, lambda i, src: (0,) * a.ndim)
     return pl.pallas_call(
-        pick_kernel,
+        functools.partial(pick_kernel, ahead=ahead),
         grid_spec=pltpu.PrefetchScalarGridSpec(
             num_scalar_prefetch=1,
             grid=(1,),
-            in_specs=[tail] * len(pieces) + [whole(c) for c in cots],
-            out_specs=pl.BlockSpec((2 * NX, ROWS // 2, chunk), lambda i, src: (0, 0, 0)),
-            scratch_shapes=[pltpu.VMEM((2 * NX, height, lanes), bf16)],
+            in_specs=[tail] * count + [whole(c) for c in cots],
+            out_specs=pl.BlockSpec((count, ROWS // 2, chunk), lambda i, src: (0, 0, 0)),
+            scratch_shapes=[pltpu.VMEM((count, height, lanes), bf16)],
         ),
-        out_shape=jax.ShapeDtypeStruct((2 * NX, ROWS // 2, chunk), bf16),
+        out_shape=jax.ShapeDtypeStruct((count, ROWS // 2, chunk), bf16),
         interpret=INTERPRET,
         name="pick",
-    )(here, *pieces, *cots).reshape(NX, ROWS, chunk)
+    )(here, *pieces, *cots).reshape(count // 2, ROWS, chunk)
 
 
 def hidden_kernel(*refs, pieces, known):
@@ -192,16 +197,16 @@
             outs[1][old.shape[0] :, :] = h
 
 
-def hidden(pieces, gate, up, *known):
+def hidden(count, pieces, gate, up, *known):
     units, width = gate.shape
-    step = width // NX
+    step = width // count
     total = sum(p.shape[0] for p in pieces)
     col = lambda k: (0, k)
     fixed = lambda k: (0, 0)
     heights = [total] + [total + k.shape[0] for k in known]
     return pl.pallas_call(
         functools.partial(hidden_kernel, pieces=len(pieces), known=len(known)),
-        grid=(NX,),
+        grid=(count,),
         in_specs=[pl.BlockSpec((p.shape[0], step), col) for p in pieces]
         + [pl.BlockSpec((units, step), col)] * 2
         + [pl.BlockSpec(k.shape, fixed) for k in known],
@@ -214,60 +219,65 @@
 
 
 def fisher_kernel(*refs, half, counts):
-    g_ref, out_ref = refs[-2:]
+    near_ref, far_ref, out_ref = refs[-3:]
+    grads = {r: near_ref.at[i] for i, r in enumerate(ORDER[:3])}
+    grads[ORDER[3]] = far_ref.at[0]
     start = 0
     for j, count in enumerate(counts):
         e = half[j]
         parts = [r[...] for r in refs[start : start + count]]
         start += count
         h = jnp.concatenate(parts, axis=0) if count > 1 else parts[0]
-        g = jnp.concatenate([g_ref[(e + d) % NX] for d in ORDER], axis=0)
+        g = jnp.concatenate([grads[(e + d) % NX][...] for d in ORDER], axis=0)
         acc = lax.dot_general(h, g, (((0,), (0,)), ((), ())), preferred_element_type=f32)
         acc = acc + PRIOR
         out_ref[:, j * PIECE : (j + 1) * PIECE, :] = acc.reshape(-1, PIECE, acc.shape[1]).astype(bf16)
 
 
-def fisher_half(half, parts, grad_sq):
+def fisher_half(half, parts, near, far):
     flat = [h for e in half for h in parts[e]]
     units = flat[0].shape[1] // 2
-    chunk = grad_sq.shape[-1]
+    chunk = near.shape[-1]
     return pl.pallas_call(
         functools.partial(fisher_kernel, half=half, counts=[len(parts[e]) for e in half]),
         grid=(2,),
         in_specs=[pl.BlockSpec((h.shape[0], units), lambda k: (0, k)) for h in flat]
-        + [pl.BlockSpec(grad_sq.shape, lambda k: (0, 0, 0))],
+        + [pl.BlockSpec(a.shape, lambda k: (0, 0, 0)) for a in (near, far)],
         out_specs=pl.BlockSpec((NZ * NX // 2, 2 * PIECE, chunk), lambda k: (k, 0, 0)),
         out_shape=jax.ShapeDtypeStruct((NZ * NX, 2 * PIECE, chunk), bf16),
         interpret=INTERPRET,
         name="fisher",
-    )(*flat, grad_sq)
-
-
-def mix_kernel(kron_ref, den_ref, da_ref, db_ref, *refs):
-    snd2_ref, snd_ref, own2_ref, own_ref, val_ref = refs[-5:]
-    mix = kron_ref[...]
-    block = OWN * PIECE
+    )(*flat, near, far)
+
+
+def mix_kernel(spot_ref, den_ref, da_ref, db_ref, *refs):
+    two, rest, val_ref, acc_ref = refs[-6:-4], refs[-4:-2], refs[-2], refs[-1]
     for j, down_ref in enumerate((da_ref, db_ref)):
-        den_all = den_ref[:, 0, j * PIECE : (j + 1) * PIECE, :].astype(f32)
-        num_all = den_all * down_ref[:, 0].astype(f32)
-        val_ref[2 * j] = num_all.reshape(NZ * PIECE, -1).astype(bf16)
-        val_ref[2 * j + 1] = den_all.reshape(NZ * PIECE, -1).astype(bf16)
+        den = den_ref[:, 0, j * PIECE : (j + 1) * PIECE, :].astype(f32)
+        val_ref[2 * j + 1] = den.astype(f32)
+        val_ref[2 * j] = (den * down_ref[:, 0].astype(f32)).astype(bf16).astype(f32)
 
     def body(n, carry):
         arr = n % 2
-        rows = pl.ds(pl.multiple_of(n // 2 * block, PIECE), block)
-        res = jnp.dot(mix, val_ref[n], preferred_element_type=f32).astype(bf16)
-        for core, (two, rest) in enumerate(((own2_ref, own_ref), (snd2_ref, snd_ref))):
-            base = core * NY * block
-            two[arr, rows, :] = res[base + 2 * block : base + 3 * block]
-            for i, hop in enumerate(HOPS):
-                rest[arr, i, rows, :] = res[base + hop * block : base + (hop + 1) * block]
+        rows = pl.ds(pl.multiple_of(n // 2 * OWN * PIECE, PIECE), OWN * PIECE)
+        acc_ref[...] = jnp.zeros(acc_ref.shape, f32)
+        for i in range(NZ):
+            acc_ref[spot_ref[i]] += val_ref[n, i]
+        for core in range(NC):
+            for hop in range(NY):
+                start = (core * NY + hop) * OWN
+                res = acc_ref[start : start + OWN]
+                res = res.reshape(OWN * PIECE, res.shape[-1]).astype(bf16)
+                if hop == 2:
+                    two[core][arr, rows, :] = res
+                else:
+                    rest[core][arr, HOPS.index(hop), rows, :] = res
         return carry
 
     lax.fori_loop(0, 4, body, 0)
 
 
-def mix(half, kron, den, down, after):
+def mix(half, spots, den, down, after):
     chunk = den.shape[-1]
     width = down.shape[-1]
     tall = 2 * OWN * PIECE
@@ -283,89 +293,65 @@
         mix_kernel,
         grid=(NX,),
         in_specs=[
-            pl.BlockSpec(kron.shape, lambda k: (0, 0)),
+            pl.BlockSpec(memory_space=pltpu.SMEM),
             pl.BlockSpec((NZ, 1, 2 * PIECE, chunk), lambda k: (0, k, 0, 0)),
             down_spec(half[0]),
             down_spec(half[1]),
         ]
         + [pl.BlockSpec(memory_space=pl.ANY)] * len(after),
-        out_specs=[two_spec, rest_spec, two_spec, rest_spec],
-        out_shape=[two, rest, two, rest],
-        scratch_shapes=[pltpu.VMEM((4, NZ * PIECE, chunk), bf16)],
+        out_specs=[two_spec, two_spec, rest_spec, rest_spec],
+        out_shape=[two, two, rest, rest],
+        scratch_shapes=[
+            pltpu.VMEM((4, NZ, PIECE, chunk), f32),
+            pltpu.VMEM((MERGED, PIECE, chunk), f32),
+        ],
         interpret=INTERPRET,
         name="mix",
-    )(kron, den.reshape(NZ, NX, 2 * PIECE, chunk), down, down, *after)
+    )(spots, den.reshape(NZ, NX, 2 * PIECE, chunk), down, down, *after)
 
 
 def final_kernel(*refs):
+    own, oth, up_num, up_den, dn_num, dn_den = refs[:6]
     out_ref = refs[-1]
+    tot = []
+    for arr, up, dn in ((0, up_num, dn_num), (1, up_den, dn_den)):
+        tot.append(
+            own[arr, 0].astype(f32) + oth[arr, 0].astype(f32) + up[...].astype(f32) + dn[...].astype(f32)
+        )
+    res = (tot[0] / tot[1]).astype(bf16)
+    for m in range(OWN):
+        out_ref[m, 0] = res[m * PIECE : (m + 1) * PIECE]
+
+
+def final(half, group, *before):
+    _, width = group[2].shape
+    chunk = width // NX
     block = OWN * PIECE
-    k = pl.program_id(0)
-    for n, half in enumerate(HALVES):
-        own, oth, up_num, up_den, dn_num, dn_den = refs[6 * n : 6 * n + 6]
-        tot = []
-        for arr, up, dn in ((0, up_num, dn_num), (1, up_den, dn_den)):
-            tot.append(
-                own[arr, 0].astype(f32) + oth[arr, 0].astype(f32) + up[...].astype(f32) + dn[...].astype(f32)
-            )
-        res = (tot[0] / tot[1]).astype(bf16)
-        for j, e in enumerate(half):
-            s = lax.rem(k + e, NX)
-            for m in range(OWN):
-                out_ref[m, s] = res[j * block + m * PIECE : j * block + (m + 1) * PIECE]
-
-
-def final(groups):
-    tall, width = groups[0][2].shape
-    chunk = width // NX
-    flat = pl.BlockSpec((tall, chunk), lambda k: (0, k))
-    rest = pl.BlockSpec((2, 1, tall, chunk), lambda k: (0, 2, 0, k))
+    flat = pl.BlockSpec((block, chunk), lambda k, j: (j, k))
+    rest = pl.BlockSpec((2, 1, block, chunk), lambda k, j: (0, 2, j, k))
+    first, gap = half[0], half[1] - half[0]
     return pl.pallas_call(
         final_kernel,
-        grid=(NX,),
-        in_specs=[rest, rest, flat, flat, flat, flat] * 2,
-        out_specs=pl.BlockSpec((OWN, NX, PIECE, chunk), lambda k: (0, 0, 0, k)),
+        grid=(NX, 2),
+        in_specs=[rest, rest, flat, flat, flat, flat] + [pl.BlockSpec(memory_space=pl.ANY)] * len(before),
+        out_specs=pl.BlockSpec(
+            (OWN, 1, PIECE, chunk), lambda k, j: (0, lax.rem(k + first + gap * j, NX), 0, k)
+        ),
         out_shape=jax.ShapeDtypeStruct((OWN, NX, PIECE, width), bf16),
+        input_output_aliases={6: 0} if before else {},
         interpret=INTERPRET,
         name="final",
-    )(*groups[0], *groups[1])
-
-
-def sums_kernel(*refs, counts):
-    outs = refs[-len(counts) :]
-    step = outs[0].shape[1] // COLS
-
-    def body(k, carry):
-        cols = pl.ds(pl.multiple_of(k * step, step), step)
-        start = 0
-        for out, count in zip(outs, counts):
-            total = refs[start][:, cols].astype(f32)
-            for r in refs[start + 1 : start + count]:
-                total = total + r[:, cols].astype(f32)
-            out[:, cols] = total.astype(bf16)
-            start += count
-        return carry
-
-    lax.fori_loop(0, COLS, body, 0)
+    )(*group, *before)
 
 
 def sums(*groups):
-    specs, args = [], []
+    outs = []
     for group in groups:
+        total = 0.0
         for arr, lead in group:
-            shape = (None,) * len(lead) + arr.shape[len(lead) :]
-            specs.append(pl.BlockSpec(shape, lambda i, lead=lead: lead + (0, 0)))
-            args.append(arr)
-    shape = groups[0][0][0].shape[-2:]
-    return pl.pallas_call(
-        functools.partial(sums_kernel, counts=[len(g) for g in groups]),
-        grid=(1,),
-        in_specs=specs,
-        out_specs=[pl.BlockSpec(shape, lambda i: (0, 0))] * len(groups),
-        out_shape=[jax.ShapeDtypeStruct(shape, bf16)] * len(groups),
-        interpret=INTERPRET,
-        name="sums",
-    )(*args)
+            total = total + arr[lead].astype(f32)
+        outs.append(total.astype(bf16))
+    return outs
 
 
 def reduce_slots(snd2, snd, own2, own):
@@ -423,15 +409,16 @@
     down_recv = lax.all_to_all(down, ("z", "x"), 0, 0, tiled=True)
     down_recv = down_recv.reshape(NZ, NX, PIECE, width)
 
-    (main,) = hidden((part_a, part_b, left_a, left_b, right_a, right_b), gate, up)
+    (main,) = hidden(COLS, (part_a, part_b, left_a, left_b, right_a, right_b), gate, up)
     main1 = shift(main, "x", NX, -1)
-    late, full = hidden((far_a, far_b), gate, up, main)
+    late, full = hidden(NX, (far_a, far_b), gate, up, main)
     late1 = shift(late, "x", NX, -1)
     full3 = shift(full, "x", NX, -3)
     full2 = shift(full, "x", NX, -2)
     parts = {0: (full,), 1: (main1, late1), 2: (full2,), 3: (full3,)}
-    pieces = (part_a, part_b, left_a, left_b, far_a, far_b, right_a, right_b)
-    grad_sq = pick(here, pieces, cots, width)
+    near = (part_a, part_b, left_a, left_b, right_a, right_b)
+    grad_near = pick(here, ORDER[:3], near, cots, width)
+    grad_far = pick(here, ORDER[3:], (far_a, far_b), cots, width)
 
     slot_table = slot_lookup(cluster, merged_slot)
     expert_ids = jnp.arange(EXPERTS, dtype=jnp.int32)
@@ -439,24 +426,21 @@
     member_slot = jnp.sum(
         jnp.where(member[:, None] == expert_ids[None, :], slot_table[None, :], 0), axis=1
     )
-    owner_core = (c + jnp.arange(NC, dtype=jnp.int32)) % NC
-    owner_y = (y + jnp.arange(NY, dtype=jnp.int32)) % NY
-    owner = owner_y[None, :] * NC + owner_core[:, None]
-    slots = (owner[:, :, None] * OWN + jnp.arange(OWN, dtype=jnp.int32)).reshape(-1)
-    same_slot = jnp.repeat(slots, PIECE)[:, None] == jnp.repeat(member_slot, PIECE)[None, :]
-    q_row = jnp.arange(MERGED * PIECE, dtype=jnp.int32)[:, None] % PIECE
-    q_col = jnp.arange(NZ * PIECE, dtype=jnp.int32)[None, :] % PIECE
-    kron = (same_slot & (q_row == q_col)).astype(bf16)
+    owner, row = member_slot // OWN, member_slot % OWN
+    core, hop = (owner % NC - c) % NC, (owner // NC - y) % NY
+    spots = (core * NY + hop) * OWN + row
 
     groups = []
     after = ()
     for half in HALVES:
-        denom = fisher_half(half, parts, grad_sq)
+        denom = fisher_half(half, parts, grad_near, grad_far)
         denom_recv = lax.all_to_all(denom, ("z", "x"), 0, 0, tiled=True)
-        mixed = mix(half, kron, denom_recv, down_recv, after)
-        group, after = reduce_slots(*mixed)
+        mixed = mix(half, spots, denom_recv, down_recv, after)
+        own2, snd2, own, snd = mixed
+        group, after = reduce_slots(snd2, snd, own2, own)
         groups.append(group)
-    return final(groups)
+    first = final(HALVES[0], groups[0])
+    return final(HALVES[1], groups[1], first)
 
 
 def solution(mesh):

time: 311 us -> 329 us (1.058)
  waiting for transfers between devices: 129 us -> 143 us
  starting transfers between devices: 77.6 us -> 85.6 us
  other arithmetic: 2.74 us -> 9.43 us
  Pallas kernels: 62.3 us -> 56.9 us
  local copies, waits for them, and re-layouts: 11.2 us -> 5.95 us
    all_to_all x2, waiting for transfers between devices: 24.7 us -> 31.9 us  [per_device(): denom_recv = lax.all_to_all(denom, ('z', 'x'), 0, 0, tiled=True)]
    pallas_call x10 -> x6, Pallas kernels: 39.9 us -> 32.9 us  [the longest x2 11.6 us: mix(): pl.pallas_call(mix_kernel, grid=(NX,), in_specs=[pl.BlockSpec(memory_spac...]
    ppermute x40, waiting for transfers between devices: 104 us -> 111 us  [shift(): return lax.ppermute(a, axis, [(i, (i + step) % size) for i in range(size)])]
    convert_element_type x1 -> x6, other arithmetic: 1.39 us -> 6.74 us  [sums(): outs.append(total.astype(bf16))]
    unnamed x60 -> x50, local copies, waits for them, and re-layouts: 10.3 us -> 5.91 us
    ppermute x40, starting transfers between devices: 58.1 us -> 62.3 us  [shift(): return lax.ppermute(a, axis, [(i, (i + step) % size) for i in range(size)])]
    all_to_all x2, starting transfers between devices: 13.9 us -> 17.8 us  [per_device(): denom_recv = lax.all_to_all(denom, ('z', 'x'), 0, 0, tiled=True)]
  transfers between devices with their start and end apart: 43 -> 43, of which waited for: 21 -> 22; matrix products, arithmetic and copies ran while one was open for 1% -> 3% of each run, Pallas kernels for 16% -> 12%
where the time goes in v1:
time: 329 us; the launch traced here: 328 us
  waiting for transfers between devices  143 us (43%)
  starting transfers between devices  85.6 us (26%)
  Pallas kernels  56.9 us (17%)
  blocking collectives  26.9 us (8%)
  other arithmetic  9.43 us (3%)
  local copies, waits for them, and re-layouts  5.95 us (2%)
    ppermute x40, waiting for transfers between devices, shift(): return lax.ppermute(a, axis, [(i, (i + step) % size) for i in range(size)])  111 us
    ppermute x40, starting transfers between devices, shift(): return lax.ppermute(a, axis, [(i, (i + step) % size) for i in range(size)])  62.3 us
    all_to_all x2, waiting for transfers between devices, per_device(): denom_recv = lax.all_to_all(denom, ('z', 'x'), 0, 0, tiled=True)  31.9 us
    all_to_all x1, blocking collectives, per_device(): cot0 = lax.all_to_all(cot_send, ('z', 'x'), 0, 0, tiled=True)  26.9 us
    all_to_all x2, starting transfers between devices, per_device(): denom_recv = lax.all_to_all(denom, ('z', 'x'), 0, 0, tiled=True)  17.8 us
    pallas_call x2, Pallas kernels, hidden(): pl.pallas_call(functools.partial(hidden_kernel, pieces=len(pieces), known...  13.3 us
    pallas_call x2, Pallas kernels, mix(): pl.pallas_call(mix_kernel, grid=(NX,), in_specs=[pl.BlockSpec(memory_spac...  11.6 us
    pallas_call x2, Pallas kernels, final(): pl.pallas_call(final_kernel, grid=(NX, 2), in_specs=[rest, rest, flat, fl...  10.7 us
  transfers between devices with their start and end apart: 43, of which 22 were waited for; matrix products, arithmetic and copies ran while one was open for 3% of the time, Pallas kernels for 12%

profile of v1, /device:TPU:2, one launch (start us, length us, event | category | flops | bytes accessed | tf_op | source)
XLA Modules:
  0.0 327.9 jit_solution(9755291022449826018)
XLA Ops:
  1.1 26.9 %all_to_all.24 = bf16[32,8,896]{2,1,0:T(8,128)(2,1)} all-to-all(bf16[32,8,896]{2,1,0:T(8,128)(2,1)S(1)} %bitcast.69), channel_id=1, replica_groups=mesh['y'=4,'c'=2,'z'=8,'x'=4] {'z','x'}, dimensions={0} | all-to-all | bytes 917504 | tf_op jit(solution)/shard_map/all_to_all | solution.py:400
  28.0 5.6 %all-to-all-start.2 = ((bf16[32,8,3584]{2,1,0:T(8,128)(2,1)}), bf16[32,8,3584]{2,1,0:T(8,128)(2,1)S(1)}, u32[]{:S(2)}, u32[]{:S(2)}) async-start(bf16[32,8,3584]{2,1,0:T(8,128)(2,1)} %bitcast.68), calls=%async_computation.2 | async-start | bytes 3670016 | tf_op jit(solution)/shard_map/all_to_all | solution.py:409
  34.3 3.8 %pack.1 = (bf16[20,3712]{1,0:T(8,128)(2,1)}, bf16[20,3712]{1,0:T(8,128)(2,1)}, bf16[20,3712]{1,0:T(8,128)(2,1)}, bf16[20,3712]{1,0:T(8,128)(2,1)}, bf16[20,3712]...) custom-call(s32[4]{0:T(128)} %pad_add_fusion.here_ref, ...), custom_call_target="tpu_custom_call" | custom-call | tf_op jit(solution)/shard_map/pack/pallas_call | solution.py:93
  38.1 3.6 %collective-permute-start.5 = (bf16[20,3712]{1,0:T(8,128)(2,1)}, bf16[20,3712]{1,0:T(8,128)(2,1)S(1)}, u32[]{:S(2)}, u32[]{:S(2)}) collective-permute-start(bf16[20,3712]{1,0:T(8,128)(2,1)} %get-tuple-element.27), channel_id=1, source_target_pairs={{0,24},{4,28},{8,0},{12,4},{16,8},{20,12},{24,16},{28,20},{1,25},{... | collective-permute-start | bytes 445448 | tf_op jit(solution)/shard_map/ppermute | solution.py:34
  41.9 4.8 %collective-permute-start.7 = (bf16[20,3712]{1,0:T(8,128)(2,1)}, bf16[20,3712]{1,0:T(8,128)(2,1)S(1)}, u32[]{:S(2)}, u32[]{:S(2)}) collective-permute-start(bf16[20,3712]{1,0:T(8,128)(2,1)} %get-tuple-element.29), channel_id=1, source_target_pairs={{0,20},{4,24},{8,28},{12,0},{16,4},{20,8},{24,12},{28,16},{1,21},{... | collective-permute-start | bytes 445448 | tf_op jit(solution)/shard_map/ppermute | solution.py:34
  50.5 37.0 %collective-permute-done.5 = bf16[20,3712]{1,0:T(8,128)(2,1)S(1)} collective-permute-done((bf16[20,3712]{1,0:T(8,128)(2,1)}, bf16[20,3712]{1,0:T(8,128)(2,1)S(1)}, u32[]{:S(2)}, u32[]{:S(2)}) %collective-permute-start.5) | collective-permute-done | bytes 148512 | tf_op jit(solution)/shard_map/ppermute | solution.py:34
  92.1 3.5 %collective-permute-start.2 = (bf16[20,3712]{1,0:T(8,128)(2,1)}, bf16[20,3712]{1,0:T(8,128)(2,1)S(1)}, u32[]{:S(2)}, u32[]{:S(2)}) collective-permute-start(bf16[20,3712]{1,0:T(8,128)(2,1)} %get-tuple-element.26), channel_id=1, source_target_pairs={{0,8},{4,12},{8,16},{12,20},{16,24},{20,28},{24,0},{28,4},{1,9},{5... | collective-permute-start | bytes 445448 | tf_op jit(solution)/shard_map/ppermute | solution.py:34
  100.4 3.9 %collective-permute-done.1 = bf16[20,3712]{1,0:T(8,128)(2,1)S(1)} collective-permute-done((bf16[20,3712]{1,0:T(8,128)(2,1)}, bf16[20,3712]{1,0:T(8,128)(2,1)S(1)}, u32[]{:S(2)}, u32[]{:S(2)}) %collective-permute-start.1) | collective-permute-done | bytes 148512 | tf_op jit(solution)/shard_map/ppermute | solution.py:34
  109.6 5.4 %collective-permute-done.9.refs_3_ = bf16[80,3712]{1,0:T(8,128)(2,1)S(1)} collective-permute-done((bf16[80,3712]{1,0:T(8,128)(2,1)S(1)}, bf16[80,3712]{1,0:T(8,128)(2,1)S(1)}, u32[]{:S(2)}, u32[]{:S(2)}) %collective-permute-start.9) | collective-permute-done | bytes 593952 | tf_op jit(solution)/shard_map/ppermute | solution.py:34
  119.7 8.0 %collective-permute-done.11.refs_2_ = bf16[80,3712]{1,0:T(8,128)(2,1)S(1)} collective-permute-done((bf16[80,3712]{1,0:T(8,128)(2,1)S(1)}, bf16[80,3712]{1,0:T(8,128)(2,1)S(1)}, u32[]{:S(2)}, u32[]{:S(2)}) %collective-permute-start.11) | collective-permute-done | bytes 593952 | tf_op jit(solution)/shard_map/ppermute | solution.py:34
  132.4 3.9 %collective-permute-done.10.refs_1_ = bf16[80,3712]{1,0:T(8,128)(2,1)S(1)} collective-permute-done((bf16[80,3712]{1,0:T(8,128)(2,1)S(1)}, bf16[80,3712]{1,0:T(8,128)(2,1)S(1)}, u32[]{:S(2)}, u32[]{:S(2)}) %collective-permute-start.10) | collective-permute-done | bytes 593952 | tf_op jit(solution)/shard_map/ppermute | solution.py:34
  137.8 8.2 %hidden.2.refs_4_ = bf16[480,256]{1,0:T(8,128)(2,1)} custom-call(bf16[80,3712]{1,0:T(8,128)(2,1)} %copy-done.6, bf16[80,3712]{1,0:T(8,128)(2,1)} %copy-done.5, bf16[80,3712]{1,0:T(8,128)(2,1)} %copy-done.11, bf16[80,3712]{1,0:T(8,128)(2,1)} %copy-done.10, bf16[80,3712]{1,0:T(8,128)(2,1)} %collective-permute-done.3.refs_4_, bf16[80,3712]{1,0:T(8,128)(2,1)} %copy-done.9, ...), custom_call_target="tpu_custom_call" | custom-call | tf_op jit(solution)/shard_map/hidden/pallas_call | solution.py:207
  146.4 5.1 %hidden.3 = (bf16[160,256]{1,0:T(8,128)(2,1)}, bf16[640,256]{1,0:T(8,128)(2,1)}) custom-call(bf16[80,3712]{1,0:T(8,128)(2,1)} %collective-permute-done.4.refs_0_, bf16[80,3712]{1,0:T(8,128)(2,1)} %copy-done.12, bf16[256,3584]{1,0:T(8,128)(2,1)} %refs_2_.1, bf16[256,3584]{1,0:T(8,128)(2,1)} %refs_3_.1, bf16[480,256]{1,0:T(8,128)(2,1)} %hidden.2.refs_4_), custom_call_target="tpu_custom_call" | custom-call | tf_op jit(solution)/shard_map/hidden/pallas_call | solution.py:207
  154.7 6.3 %pick.2 = bf16[6,80,896]{2,1,0:T(8,128)(2,1)} custom-call(s32[4]{0:T(128)} %pad_add_fusion.here_ref, bf16[80,3712]{1,0:T(8,128)(2,1)} %copy-done.6, bf16[80,3712]{1,0:T(8,128)(2,1)} %copy-done.5, bf16[80,3712]{1,0:T(8,128)(2,1)} %copy-done.11, bf16[80,3712]{1,0:T(8,128)(2,1)} %copy-done.10, bf16[80,3712]{1,0:T(8,128)(2,1)} %collective-permute-done.3.refs_4_, ...), custom_call_target="tpu_custom_call" | custom-call | tf_op jit(solution)/shard_map/pick/pallas_call | solution.py:153
  161.0 4.3 %pick.3 = bf16[2,80,896]{2,1,0:T(8,128)(2,1)} custom-call(s32[4]{0:T(128)} %pad_add_fusion.here_ref, bf16[80,3712]{1,0:T(8,128)(2,1)} %collective-permute-done.4.refs_0_, bf16[80,3712]{1,0:T(8,128)(2,1)} %copy-done.12, bf16[8,4,8,896]{3,2,1,0:T(8,128)(2,1)} %bitcast.63, bf16[8,4,8,896]{3,2,1,0:T(8,128)(2,1)} %bitcast.10.refs_7_.refs_3_, ...), custom_call_target="tpu_custom_call" | custom-call | tf_op jit(solution)/shard_map/pick/pallas_call | solution.py:153
  169.5 12.1 %all-to-all-start.3 = ((bf16[32,16,896]{2,1,0:T(8,128)(2,1)}), bf16[32,16,896]{2,1,0:T(8,128)(2,1)S(1)}, u32[]{:S(2)}, u32[]{:S(2)}) async-start(bf16[32,16,896]{2,1,0:T(8,128)(2,1)} %fisher.3), calls=%async_computation.3 | async-start | bytes 1835008 | tf_op jit(solution)/shard_map/all_to_all | solution.py:437
  182.5 24.5 %all-to-all-done.3 = bf16[32,16,896]{2,1,0:T(8,128)(2,1)S(1)} async-done(((bf16[32,16,896]{2,1,0:T(8,128)(2,1)}), bf16[32,16,896]{2,1,0:T(8,128)(2,1)S(1)}, u32[]{:S(2)}, u32[]{:S(2)}) %all-to-all-start.3) | async-done | bytes 917536 | tf_op jit(solution)/shard_map/all_to_all | solution.py:437
  207.9 5.8 %mix.2 = (bf16[2,48,3584]{2,1,0:T(8,128)(2,1)}, bf16[2,48,3584]{2,1,0:T(8,128)(2,1)}, bf16[2,3,48,3584]{3,2,1,0:T(8,128)(2,1)}, bf16[2,3,48,3584]{3,2,1,0:T(8,128)(2,1)}) custom-call(s32[8]{0:T(128)} %fusion.13.spot_ref, bf16[8,4,16,896]{3,2,1,0:T(8,128)(2,1)} %bitcast.64, bf16[8,4,8,3584]{3,2,1,0:T(8,128)(2,1)} %bitcast.56, bf16[8,4,8,3584]{3,2,1,0:T(8,128)(2,1)} %bitcast.57), custom_call_target="tpu_custom_call" | custom-call | tf_op jit(solution)/shard_map/mix/pallas_call | solution.py:292
  216.4 9.1 %collective-permute-done.14.refs_1_ = bf16[640,256]{1,0:T(8,128)(2,1)S(1)} collective-permute-done((bf16[640,256]{1,0:T(8,128)(2,1)S(1)}, bf16[640,256]{1,0:T(8,128)(2,1)S(1)}, u32[]{:S(2)}, u32[]{:S(2)}) %collective-permute-start.14) | collective-permute-done | bytes 327712 | tf_op jit(solution)/shard_map/ppermute | solution.py:34
  225.5 7.1 %collective-permute-done.13.refs_0_ = bf16[640,256]{1,0:T(8,128)(2,1)S(1)} collective-permute-done((bf16[640,256]{1,0:T(8,128)(2,1)S(1)}, bf16[640,256]{1,0:T(8,128)(2,1)S(1)}, u32[]{:S(2)}, u32[]{:S(2)}) %collective-permute-start.13) | collective-permute-done | bytes 327712 | tf_op jit(solution)/shard_map/ppermute | solution.py:34
  236.7 5.6 %all-to-all-start.1 = ((bf16[32,16,896]{2,1,0:T(8,128)(2,1)}), bf16[32,16,896]{2,1,0:T(8,128)(2,1)S(1)}, u32[]{:S(2)}, u32[]{:S(2)}) async-start(bf16[32,16,896]{2,1,0:T(8,128)(2,1)} %fisher.2), calls=%async_computation.1 | async-start | bytes 1835008 | tf_op jit(solution)/shard_map/all_to_all | solution.py:437
  243.9 4.0 %collective-permute-start.27 = (bf16[48,3584]{1,0:T(8,128)(2,1)S(1)}, bf16[48,3584]{1,0:T(8,128)(2,1)S(1)}, u32[]{:S(2)}, u32[]{:S(2)}) collective-permute-start(bf16[48,3584]{1,0:T(8,128)(2,1)S(1)} %get-tuple-element.51), channel_id=1, source_target_pairs={{0,192},{64,0},{128,64},{192,128},{1,193},{65,1},{129,65},{193,129... | collective-permute-start | bytes 1032200 | tf_op jit(solution)/shard_map/ppermute | solution.py:34
  247.9 6.9 %collective-permute-done.27 = bf16[48,3584]{1,0:T(8,128)(2,1)S(1)} collective-permute-done((bf16[48,3584]{1,0:T(8,128)(2,1)S(1)}, bf16[48,3584]{1,0:T(8,128)(2,1)S(1)}, u32[]{:S(2)}, u32[]{:S(2)}) %collective-permute-start.27) | collective-permute-done | bytes 344096 | tf_op jit(solution)/shard_map/ppermute | solution.py:34
  260.5 7.4 %all-to-all-done.1 = bf16[32,16,896]{2,1,0:T(8,128)(2,1)S(1)} async-done(((bf16[32,16,896]{2,1,0:T(8,128)(2,1)}), bf16[32,16,896]{2,1,0:T(8,128)(2,1)S(1)}, u32[]{:S(2)}, u32[]{:S(2)}) %all-to-all-start.1) | async-done | bytes 917536 | tf_op jit(solution)/shard_map/all_to_all | solution.py:437
  268.8 5.7 %mix.3 = (bf16[2,48,3584]{2,1,0:T(8,128)(2,1)}, bf16[2,48,3584]{2,1,0:T(8,128)(2,1)}, bf16[2,3,48,3584]{3,2,1,0:T(8,128)(2,1)}, bf16[2,3,48,3584]{3,2,1,0:T(8,128)(2,1)}) custom-call(s32[8]{0:T(128)} %fusion.13.spot_ref, bf16[8,4,16,896]{3,2,1,0:T(8,128)(2,1)} %bitcast.65, bf16[8,4,8,3584]{3,2,1,0:T(8,128)(2,1)} %bitcast.58, ...), custom_call_target="tpu_custom_call" | custom-call | tf_op jit(solution)/shard_map/mix/pallas_call | solution.py:292
  275.0 3.7 %collective-permute-start.39 = (bf16[48,3584]{1,0:T(8,128)(2,1)}, bf16[48,3584]{1,0:T(8,128)(2,1)S(1)}, u32[]{:S(2)}, u32[]{:S(2)}) collective-permute-start(bf16[48,3584]{1,0:T(8,128)(2,1)} %get-tuple-element.47.refs_1_), channel_id=1, source_target_pairs={{0,192},{64,0},{128,64},{192,128},{1,193},{65,1},{129,65},{193,129... | collective-permute-start | bytes 1032200 | tf_op jit(solution)/shard_map/ppermute | solution.py:34
  284.6 9.2 %collective-permute-done.34 = bf16[48,3584]{1,0:T(8,128)(2,1)S(1)} collective-permute-done((bf16[48,3584]{1,0:T(8,128)(2,1)S(1)}, bf16[48,3584]{1,0:T(8,128)(2,1)S(1)}, u32[]{:S(2)}, u32[]{:S(2)}) %collective-permute-start.34) | collective-permute-done | bytes 344096 | tf_op jit(solution)/shard_map/ppermute | solution.py:34
  293.8 3.7 %collective-permute-start.38 = (bf16[48,3584]{1,0:T(8,128)(2,1)S(1)}, bf16[48,3584]{1,0:T(8,128)(2,1)S(1)}, u32[]{:S(2)}, u32[]{:S(2)}) collective-permute-start(bf16[48,3584]{1,0:T(8,128)(2,1)S(1)} %get-tuple-element.41), channel_id=1, source_target_pairs={{0,192},{64,0},{128,64},{192,128},{1,193},{65,1},{129,65},{193,129... | collective-permute-start | bytes 1032200 | tf_op jit(solution)/shard_map/ppermute | solution.py:34
  306.0 3.7 %collective-permute-done.37.refs_3_ = bf16[48,3584]{1,0:T(8,128)(2,1)S(1)} collective-permute-done((bf16[48,3584]{1,0:T(8,128)(2,1)S(1)}, bf16[48,3584]{1,0:T(8,128)(2,1)S(1)}, u32[]{:S(2)}, u32[]{:S(2)}) %collective-permute-start.37) | collective-permute-done | bytes 344096 | tf_op jit(solution)/shard_map/ppermute | solution.py:34
  310.4 5.3 %final.2.refs_6_ = bf16[3,4,8,3584]{3,2,1,0:T(8,128)(2,1)} custom-call(bf16[2,3,48,3584]{3,2,1,0:T(8,128)(2,1)} %get-tuple-element.33.refs_0_, bf16[2,3,48,3584]{3,2,1,0:T(8,128)(2,1)} %collective-permute-done.24.refs_1_, bf16[48,3584]{1,0:T(8,128)(2,1)} %copy-done.14, bf16[48,3584]{1,0:T(8,128)(2,1)} %copy-done.16, bf16[48,3584]{1,0:T(8,128)(2,1)} %copy-done.15, ...), custom_call_target="tpu_custom_call" | custom-call | tf_op jit(solution)/shard_map/final/pallas_call | solution.py:333
  319.0 3.5 %collective-permute-done.32.refs_3_ = bf16[48,3584]{1,0:T(8,128)(2,1)} collective-permute-done((bf16[48,3584]{1,0:T(8,128)(2,1)S(1)}, bf16[48,3584]{1,0:T(8,128)(2,1)}, u32[]{:S(2)}, u32[]{:S(2)}) %collective-permute-start.32) | collective-permute-done | bytes 344096 | tf_op jit(solution)/shard_map/ppermute | solution.py:34
  322.5 5.4 %final.3 = bf16[3,4,8,3584]{3,2,1,0:T(8,128)(2,1)} custom-call(bf16[2,3,48,3584]{3,2,1,0:T(8,128)(2,1)} %get-tuple-element.37.refs_0_, bf16[2,3,48,3584]{3,2,1,0:T(8,128)(2,1)} %copy-done.4, bf16[48,3584]{1,0:T(8,128)(2,1)} %collective-permute-done.31.refs_2_, bf16[48,3584]{1,0:T(8,128)(2,1)} %collective-permute-done.32.refs_3_, ...), custom_call_target="tpu_custom_call", output_to_operand_aliasing={{}: (6, {})} | custom-call | tf_op jit(solution)/shard_map/final/pallas_call | solution.py:333
  (131 shorter events, 74.3 us)
Async XLA Ops:
  28.0 141.5 %all-to-all-start.2 = ((bf16[32,8,3584]{2,1,0:T(8,128)(2,1)}), bf16[32,8,3584]{2,1,0:T(8,128)(2,1)S(1)}, u32[]{:S(2)}, u32[]{:S(2)}) async-start(bf16[32,8,3584]{2,1,0:T(8,128)(2,1)} %bitcast.68), calls=%async_computation.2 | async-start | bytes 3670016 | tf_op jit(solution)/shard_map/all_to_all | solution.py:409
  38.1 49.4 %collective-permute-start.5 = (bf16[20,3712]{1,0:T(8,128)(2,1)}, bf16[20,3712]{1,0:T(8,128)(2,1)S(1)}, u32[]{:S(2)}, u32[]{:S(2)}) collective-permute-start(bf16[20,3712]{1,0:T(8,128)(2,1)} %get-tuple-element.27), channel_id=1, source_target_pairs={{0,24},{4,28},{8,0},{12,4},{16,8},{20,12},{24,16},{28,20},{1,25},{... | collective-permute-start | bytes 445448 | tf_op jit(solution)/shard_map/ppermute | solution.py:34
  41.7 50.4 %collective-permute-start.6 = (bf16[20,3712]{1,0:T(8,128)(2,1)}, bf16[20,3712]{1,0:T(8,128)(2,1)S(1)}, u32[]{:S(2)}, u32[]{:S(2)}) collective-permute-start(bf16[20,3712]{1,0:T(8,128)(2,1)} %get-tuple-element.28), channel_id=1, source_target_pairs={{0,12},{4,16},{8,20},{12,24},{16,28},{20,0},{24,4},{28,8},{1,13},{... | collective-permute-start | bytes 445448 | tf_op jit(solution)/shard_map/ppermute | solution.py:34
  41.9 55.3 %collective-permute-start.7 = (bf16[20,3712]{1,0:T(8,128)(2,1)}, bf16[20,3712]{1,0:T(8,128)(2,1)S(1)}, u32[]{:S(2)}, u32[]{:S(2)}) collective-permute-start(bf16[20,3712]{1,0:T(8,128)(2,1)} %get-tuple-element.29), channel_id=1, source_target_pairs={{0,20},{4,24},{8,28},{12,0},{16,4},{20,8},{24,12},{28,16},{1,21},{... | collective-permute-start | bytes 445448 | tf_op jit(solution)/shard_map/ppermute | solution.py:34
  46.8 51.4 %collective-permute-start.8 = (bf16[20,3712]{1,0:T(8,128)(2,1)}, bf16[20,3712]{1,0:T(8,128)(2,1)S(1)}, u32[]{:S(2)}, u32[]{:S(2)}) collective-permute-start(bf16[20,3712]{1,0:T(8,128)(2,1)} %get-tuple-element.30), channel_id=1, source_target_pairs={{0,16},{4,20},{8,24},{12,28},{16,0},{20,4},{24,8},{28,12},{1,17},{... | collective-permute-start | bytes 445448 | tf_op jit(solution)/shard_map/ppermute | solution.py:34
  49.1 51.4 %collective-permute-start = (bf16[20,3712]{1,0:T(8,128)(2,1)}, bf16[20,3712]{1,0:T(8,128)(2,1)S(1)}, u32[]{:S(2)}, u32[]{:S(2)}) collective-permute-start(bf16[20,3712]{1,0:T(8,128)(2,1)} %get-tuple-element.24), channel_id=1, source_target_pairs={{0,4},{4,8},{8,12},{12,16},{16,20},{20,24},{24,28},{28,0},{1,5},{5... | collective-permute-start | bytes 445448 | tf_op jit(solution)/shard_map/ppermute | solution.py:34
  87.5 16.8 %collective-permute-start.1 = (bf16[20,3712]{1,0:T(8,128)(2,1)}, bf16[20,3712]{1,0:T(8,128)(2,1)S(1)}, u32[]{:S(2)}, u32[]{:S(2)}) collective-permute-start(bf16[20,3712]{1,0:T(8,128)(2,1)} %get-tuple-element.25), channel_id=1, source_target_pairs={{0,28},{4,0},{8,4},{12,8},{16,12},{20,16},{24,20},{28,24},{1,29},{... | collective-permute-start | bytes 445448 | tf_op jit(solution)/shard_map/ppermute | solution.py:34
  98.3 18.5 %collective-permute-start.12 = (bf16[80,3712]{1,0:T(8,128)(2,1)S(1)}, bf16[80,3712]{1,0:T(8,128)(2,1)S(1)}, u32[]{:S(2)}, u32[]{:S(2)}) collective-permute-start(bf16[80,3712]{1,0:T(8,128)(2,1)S(1)} %pad_maximum_fusion.1.refs_1_), channel_id=1, source_target_pairs={{0,1},{1,2},{2,3},{3,0},{4,5},{5,6},{6,7},{7,4},{8,9},{9,10},{10,1... | collective-permute-start | bytes 1781768 | tf_op jit(solution)/shard_map/ppermute | solution.py:34
  99.5 15.5 %collective-permute-start.9 = (bf16[80,3712]{1,0:T(8,128)(2,1)S(1)}, bf16[80,3712]{1,0:T(8,128)(2,1)S(1)}, u32[]{:S(2)}, u32[]{:S(2)}) collective-permute-start(bf16[80,3712]{1,0:T(8,128)(2,1)S(1)} %pad_maximum_fusion.1.refs_1_), channel_id=1, source_target_pairs={{0,3},{1,0},{2,1},{3,2},{4,7},{5,4},{6,5},{7,6},{8,11},{9,8},{10,9... | collective-permute-start | bytes 1781768 | tf_op jit(solution)/shard_map/ppermute | solution.py:34
  105.8 21.9 %collective-permute-start.11 = (bf16[80,3712]{1,0:T(8,128)(2,1)S(1)}, bf16[80,3712]{1,0:T(8,128)(2,1)S(1)}, u32[]{:S(2)}, u32[]{:S(2)}) collective-permute-start(bf16[80,3712]{1,0:T(8,128)(2,1)S(1)} %pad_maximum_fusion.refs_0_), channel_id=1, source_target_pairs={{0,3},{1,0},{2,1},{3,2},{4,7},{5,4},{6,5},{7,6},{8,11},{9,8},{10,9... | collective-permute-start | bytes 1781768 | tf_op jit(solution)/shard_map/ppermute | solution.py:34
  106.9 23.8 %collective-permute-start.3 = (bf16[80,3712]{1,0:T(8,128)(2,1)S(1)}, bf16[80,3712]{1,0:T(8,128)(2,1)}, u32[]{:S(2)}, u32[]{:S(2)}) collective-permute-start(bf16[80,3712]{1,0:T(8,128)(2,1)S(1)} %pad_maximum_fusion.refs_0_), channel_id=1, source_target_pairs={{0,1},{1,2},{2,3},{3,0},{4,5},{5,6},{6,7},{7,4},{8,9},{9,10},{10,1... | collective-permute-start | bytes 1781768 | tf_op jit(solution)/shard_map/ppermute | solution.py:34
  115.0 21.4 %collective-permute-start.10 = (bf16[80,3712]{1,0:T(8,128)(2,1)S(1)}, bf16[80,3712]{1,0:T(8,128)(2,1)S(1)}, u32[]{:S(2)}, u32[]{:S(2)}) collective-permute-start(bf16[80,3712]{1,0:T(8,128)(2,1)S(1)} %collective-permute-done.9.refs_3_), channel_id=1, source_target_pairs={{0,3},{1,0},{2,1},{3,2},{4,7},{5,4},{6,5},{7,6},{8,11},{9,8},{10,9... | collective-permute-start | bytes 1781768 | tf_op jit(solution)/shard_map/ppermute | solution.py:34
  115.2 22.0 %collective-permute-start.20 = (bf16[32,8,896]{2,1,0:T(8,128)(2,1)}, bf16[32,8,896]{2,1,0:T(8,128)(2,1)}, u32[]{:S(2)}, u32[]{:S(2)}) collective-permute-start(bf16[32,8,896]{2,1,0:T(8,128)(2,1)} %all_to_all.24), channel_id=1, source_target_pairs={{0,64},{64,128},{128,192},{192,0},{1,65},{65,129},{129,193},{193,1... | collective-permute-start | bytes 1376264 | tf_op jit(solution)/shard_map/ppermute | solution.py:34
  116.8 20.4 %collective-permute-start.18 = (bf16[32,8,896]{2,1,0:T(8,128)(2,1)}, bf16[32,8,896]{2,1,0:T(8,128)(2,1)}, u32[]{:S(2)}, u32[]{:S(2)}) collective-permute-start(bf16[32,8,896]{2,1,0:T(8,128)(2,1)} %all_to_all.24), channel_id=1, source_target_pairs={{0,128},{64,192},{128,0},{192,64},{1,129},{65,193},{129,1},{193,65... | collective-permute-start | bytes 1376264 | tf_op jit(solution)/shard_map/ppermute | solution.py:34
  130.8 15.3 %collective-permute-start.4 = (bf16[80,3712]{1,0:T(8,128)(2,1)}, bf16[80,3712]{1,0:T(8,128)(2,1)}, u32[]{:S(2)}, u32[]{:S(2)}) collective-permute-start(bf16[80,3712]{1,0:T(8,128)(2,1)} %collective-permute-done.3.refs_4_), channel_id=1, source_target_pairs={{0,1},{1,2},{2,3},{3,0},{4,5},{5,6},{6,7},{7,4},{8,9},{9,10},{10,1... | collective-permute-start | bytes 1781768 | tf_op jit(solution)/shard_map/ppermute | solution.py:34
  136.4 15.1 %collective-permute-start.15 = (bf16[32,8,896]{2,1,0:T(8,128)(2,1)}, bf16[32,8,896]{2,1,0:T(8,128)(2,1)}, u32[]{:S(2)}, u32[]{:S(2)}) collective-permute-start(bf16[32,8,896]{2,1,0:T(8,128)(2,1)} %all_to_all.24), channel_id=1, source_target_pairs={{0,32},{32,0},{1,33},{33,1},{2,34},{34,2},{3,35},{35,3},{4,36},{36... | collective-permute-start | bytes 1376264 | tf_op jit(solution)/shard_map/ppermute | solution.py:34
  137.2 17.5 %collective-permute-start.21 = (bf16[32,8,896]{2,1,0:T(8,128)(2,1)}, bf16[32,8,896]{2,1,0:T(8,128)(2,1)}, u32[]{:S(2)}, u32[]{:S(2)}) collective-permute-start(bf16[32,8,896]{2,1,0:T(8,128)(2,1)} %collective-permute-done.20), channel_id=1, source_target_pairs={{0,32},{32,0},{1,33},{33,1},{2,34},{34,2},{3,35},{35,3},{4,36},{36... | collective-permute-start | bytes 1376264 | tf_op jit(solution)/shard_map/ppermute | solution.py:34
  137.2 17.5 %collective-permute-start.19 = (bf16[32,8,896]{2,1,0:T(8,128)(2,1)}, bf16[32,8,896]{2,1,0:T(8,128)(2,1)}, u32[]{:S(2)}, u32[]{:S(2)}) collective-permute-start(bf16[32,8,896]{2,1,0:T(8,128)(2,1)} %collective-permute-done.18), channel_id=1, source_target_pairs={{0,32},{32,0},{1,33},{33,1},{2,34},{34,2},{3,35},{35,3},{4,36},{36... | collective-permute-start | bytes 1376264 | tf_op jit(solution)/shard_map/ppermute | solution.py:34
  137.7 17.0 %collective-permute-start.17 = (bf16[32,8,896]{2,1,0:T(8,128)(2,1)}, bf16[32,8,896]{2,1,0:T(8,128)(2,1)}, u32[]{:S(2)}, u32[]{:S(2)}) collective-permute-start(bf16[32,8,896]{2,1,0:T(8,128)(2,1)} %collective-permute-done.16), channel_id=1, source_target_pairs={{0,32},{32,0},{1,33},{33,1},{2,34},{34,2},{3,35},{35,3},{4,36},{36... | collective-permute-start | bytes 1376264 | tf_op jit(solution)/shard_map/ppermute | solution.py:34
  146.0 19.3 %collective-permute-start.22 = (bf16[480,256]{1,0:T(8,128)(2,1)}, bf16[480,256]{1,0:T(8,128)(2,1)S(1)}, u32[]{:S(2)}, u32[]{:S(2)}) collective-permute-start(bf16[480,256]{1,0:T(8,128)(2,1)} %hidden.2.refs_4_), channel_id=1, source_target_pairs={{0,3},{1,0},{2,1},{3,2},{4,7},{5,4},{6,5},{7,6},{8,11},{9,8},{10,9... | collective-permute-start | bytes 737288 | tf_op jit(solution)/shard_map/ppermute | solution.py:34
  169.5 37.5 %all-to-all-start.3 = ((bf16[32,16,896]{2,1,0:T(8,128)(2,1)}), bf16[32,16,896]{2,1,0:T(8,128)(2,1)S(1)}, u32[]{:S(2)}, u32[]{:S(2)}) async-start(bf16[32,16,896]{2,1,0:T(8,128)(2,1)} %fisher.3), calls=%async_computation.3 | async-start | bytes 1835008 | tf_op jit(solution)/shard_map/all_to_all | solution.py:437
  213.8 44.4 %collective-permute-start.24 = (bf16[2,3,48,3584]{3,2,1,0:T(8,128)(2,1)}, bf16[2,3,48,3584]{3,2,1,0:T(8,128)(2,1)}, u32[]{:S(2)}, u32[]{:S(2)}) collective-permute-start(bf16[2,3,48,3584]{3,2,1,0:T(8,128)(2,1)} %get-tuple-element.34), channel_id=1, source_target_pairs={{0,32},{32,0},{1,33},{33,1},{2,34},{34,2},{3,35},{35,3},{4,36},{36... | collective-permute-start | bytes 6193160 | tf_op jit(solution)/shard_map/ppermute | solution.py:34
  213.8 28.6 %collective-permute-start.25 = (bf16[2,48,3584]{2,1,0:T(8,128)(2,1)}, bf16[2,48,3584]{2,1,0:T(8,128)(2,1)}, u32[]{:S(2)}, u32[]{:S(2)}) collective-permute-start(bf16[2,48,3584]{2,1,0:T(8,128)(2,1)} %get-tuple-element.36), channel_id=1, source_target_pairs={{0,32},{32,0},{1,33},{33,1},{2,34},{34,2},{3,35},{35,3},{4,36},{36... | collective-permute-start | bytes 2064392 | tf_op jit(solution)/shard_map/ppermute | solution.py:34
  216.4 16.2 %collective-permute-start.13 = (bf16[640,256]{1,0:T(8,128)(2,1)S(1)}, bf16[640,256]{1,0:T(8,128)(2,1)S(1)}, u32[]{:S(2)}, u32[]{:S(2)}) collective-permute-start(bf16[640,256]{1,0:T(8,128)(2,1)S(1)} %copy-done.18), channel_id=1, source_target_pairs={{0,1},{1,2},{2,3},{3,0},{4,5},{5,6},{6,7},{7,4},{8,9},{9,10},{10,1... | collective-permute-start | bytes 983048 | tf_op jit(solution)/shard_map/ppermute | solution.py:34
  236.7 31.1 %all-to-all-start.1 = ((bf16[32,16,896]{2,1,0:T(8,128)(2,1)}), bf16[32,16,896]{2,1,0:T(8,128)(2,1)S(1)}, u32[]{:S(2)}, u32[]{:S(2)}) async-start(bf16[32,16,896]{2,1,0:T(8,128)(2,1)} %fisher.2), calls=%async_computation.1 | async-start | bytes 1835008 | tf_op jit(solution)/shard_map/all_to_all | solution.py:437
  274.5 23.1 %collective-permute-start.28 = (bf16[2,3,48,3584]{3,2,1,0:T(8,128)(2,1)}, bf16[2,3,48,3584]{3,2,1,0:T(8,128)(2,1)S(1)}, u32[]{:S(2)}, u32[]{:S(2)}) collective-permute-start(bf16[2,3,48,3584]{3,2,1,0:T(8,128)(2,1)} %get-tuple-element.38), channel_id=1, source_target_pairs={{0,32},{32,0},{1,33},{33,1},{2,34},{34,2},{3,35},{35,3},{4,36},{36... | collective-permute-start | bytes 6193160 | tf_op jit(solution)/shard_map/ppermute | solution.py:34
  275.0 26.3 %collective-permute-start.39 = (bf16[48,3584]{1,0:T(8,128)(2,1)}, bf16[48,3584]{1,0:T(8,128)(2,1)S(1)}, u32[]{:S(2)}, u32[]{:S(2)}) collective-permute-start(bf16[48,3584]{1,0:T(8,128)(2,1)} %get-tuple-element.47.refs_1_), channel_id=1, source_target_pairs={{0,192},{64,0},{128,64},{192,128},{1,193},{65,1},{129,65},{193,129... | collective-permute-start | bytes 1032200 | tf_op jit(solution)/shard_map/ppermute | solution.py:34
  278.7 22.7 %collective-permute-start.36 = (bf16[48,3584]{1,0:T(8,128)(2,1)}, bf16[48,3584]{1,0:T(8,128)(2,1)S(1)}, u32[]{:S(2)}, u32[]{:S(2)}) collective-permute-start(bf16[48,3584]{1,0:T(8,128)(2,1)} %get-tuple-element.48.refs_0_), channel_id=1, source_target_pairs={{0,64},{64,128},{128,192},{192,0},{1,65},{65,129},{129,193},{193,1... | collective-permute-start | bytes 1032200 | tf_op jit(solution)/shard_map/ppermute | solution.py:34
  297.8 18.0 %collective-permute-start.35 = (bf16[48,3584]{1,0:T(8,128)(2,1)S(1)}, bf16[48,3584]{1,0:T(8,128)(2,1)S(1)}, u32[]{:S(2)}, u32[]{:S(2)}) collective-permute-start(bf16[48,3584]{1,0:T(8,128)(2,1)S(1)} %get-tuple-element.43), channel_id=1, source_target_pairs={{0,192},{64,0},{128,64},{192,128},{1,193},{65,1},{129,65},{193,129... | collective-permute-start | bytes 1032200 | tf_op jit(solution)/shard_map/ppermute | solution.py:34
  301.3 15.9 %collective-permute-start.31 = (bf16[48,3584]{1,0:T(8,128)(2,1)S(1)}, bf16[48,3584]{1,0:T(8,128)(2,1)}, u32[]{:S(2)}, u32[]{:S(2)}) collective-permute-start(bf16[48,3584]{1,0:T(8,128)(2,1)S(1)} %get-tuple-element.44), channel_id=1, source_target_pairs={{0,64},{64,128},{128,192},{192,0},{1,65},{65,129},{129,193},{193,1... | collective-permute-start | bytes 1032200 | tf_op jit(solution)/shard_map/ppermute | solution.py:34
  301.4 17.6 %collective-permute-start.33 = (bf16[48,3584]{1,0:T(8,128)(2,1)S(1)}, bf16[48,3584]{1,0:T(8,128)(2,1)}, u32[]{:S(2)}, u32[]{:S(2)}) collective-permute-start(bf16[48,3584]{1,0:T(8,128)(2,1)S(1)} %get-tuple-element.45), channel_id=1, source_target_pairs={{0,192},{64,0},{128,64},{192,128},{1,193},{65,1},{129,65},{193,129... | collective-permute-start | bytes 1032200 | tf_op jit(solution)/shard_map/ppermute | solution.py:34
  306.0 16.5 %collective-permute-start.32 = (bf16[48,3584]{1,0:T(8,128)(2,1)S(1)}, bf16[48,3584]{1,0:T(8,128)(2,1)}, u32[]{:S(2)}, u32[]{:S(2)}) collective-permute-start(bf16[48,3584]{1,0:T(8,128)(2,1)S(1)} %get-tuple-element.46), channel_id=1, source_target_pairs={{0,64},{64,128},{128,192},{192,0},{1,65},{65,129},{129,193},{193,1... | collective-permute-start | bytes 1032200 | tf_op jit(solution)/shard_map/ppermute | solution.py:34
  (36 other events, 396.9 us)

commit v2 on v1

--- a/solution.py
+++ b/solution.py
@@ -132,7 +132,7 @@
         for j in range(group):
             step = jnp.where(half == 0, STEPS[j], STEPS[group + j])
             zs = lax.rem(z + NZ - step, NZ)
-            blocks += [cot[zs, xs].astype(f32) for cot in cots]
+            blocks += [cot[zs, xs if cot.shape[1] > 1 else 0].astype(f32) for cot in cots]
         cot = jnp.concatenate(blocks, axis=0).astype(bf16)
         val = jnp.dot(high, cot, preferred_element_type=f32)
         val = val + jnp.dot(low, cot, preferred_element_type=f32)
@@ -149,13 +149,18 @@
     chunk = cots[0].shape[-1]
     count = len(pieces)
     tail = pl.BlockSpec((height, lanes), lambda i, src: (0, width // lanes))
-    whole = lambda a: pl.BlockSpec(a.shape, lambda i, src: (0,) * a.ndim)
+    if len(ahead) > 1:
+        part = lambda a: pl.BlockSpec(a.shape, lambda i, src: (0, 0, 0, 0))
+    else:
+        part = lambda a: pl.BlockSpec(
+            (NZ, 1) + a.shape[2:], lambda i, src: (0, lax.rem(src[3] + ahead[0], NX), 0, 0)
+        )
     return pl.pallas_call(
         functools.partial(pick_kernel, ahead=ahead),
         grid_spec=pltpu.PrefetchScalarGridSpec(
             num_scalar_prefetch=1,
             grid=(1,),
-            in_specs=[tail] * count + [whole(c) for c in cots],
+            in_specs=[tail] * count + [part(c) for c in cots],
             out_specs=pl.BlockSpec((count, ROWS // 2, chunk), lambda i, src: (0, 0, 0)),
             scratch_shapes=[pltpu.VMEM((count, height, lanes), bf16)],
         ),
@@ -252,32 +257,30 @@
 
 def mix_kernel(spot_ref, den_ref, da_ref, db_ref, *refs):
     two, rest, val_ref, acc_ref = refs[-6:-4], refs[-4:-2], refs[-2], refs[-1]
-    for j, down_ref in enumerate((da_ref, db_ref)):
-        den = den_ref[:, 0, j * PIECE : (j + 1) * PIECE, :].astype(f32)
-        val_ref[2 * j + 1] = den.astype(f32)
-        val_ref[2 * j] = (den * down_ref[:, 0].astype(f32)).astype(bf16).astype(f32)
-
-    def body(n, carry):
-        arr = n % 2
-        rows = pl.ds(pl.multiple_of(n // 2 * OWN * PIECE, PIECE), OWN * PIECE)
-        acc_ref[...] = jnp.zeros(acc_ref.shape, f32)
+    den = den_ref[:, 0]
+    down = jnp.concatenate([da_ref[:, 0].astype(f32), db_ref[:, 0].astype(f32)], axis=1)
+    val_ref[0] = (den.astype(f32) * down).astype(bf16)
+    val_ref[1] = den
+
+    def body(arr, carry):
+        acc_ref[...] = jnp.zeros(acc_ref.shape, bf16)
         for i in range(NZ):
-            acc_ref[spot_ref[i]] += val_ref[n, i]
+            acc_ref[spot_ref[i]] += val_ref[arr, i]
         for core in range(NC):
             for hop in range(NY):
                 start = (core * NY + hop) * OWN
                 res = acc_ref[start : start + OWN]
-                res = res.reshape(OWN * PIECE, res.shape[-1]).astype(bf16)
+                res = res.reshape(OWN * 2 * PIECE, res.shape[-1])
                 if hop == 2:
-                    two[core][arr, rows, :] = res
+                    two[core][arr] = res
                 else:
-                    rest[core][arr, HOPS.index(hop), rows, :] = res
+                    rest[core][arr, HOPS.index(hop)] = res
         return carry
 
-    lax.fori_loop(0, 4, body, 0)
-
-
-def mix(half, spots, den, down, after):
+    lax.fori_loop(0, 2, body, 0)
+
+
+def mix(half, spots, den, down):
     chunk = den.shape[-1]
     width = down.shape[-1]
     tall = 2 * OWN * PIECE
@@ -297,51 +300,55 @@
             pl.BlockSpec((NZ, 1, 2 * PIECE, chunk), lambda k: (0, k, 0, 0)),
             down_spec(half[0]),
             down_spec(half[1]),
-        ]
-        + [pl.BlockSpec(memory_space=pl.ANY)] * len(after),
+        ],
         out_specs=[two_spec, two_spec, rest_spec, rest_spec],
         out_shape=[two, two, rest, rest],
         scratch_shapes=[
-            pltpu.VMEM((4, NZ, PIECE, chunk), f32),
-            pltpu.VMEM((MERGED, PIECE, chunk), f32),
+            pltpu.VMEM((2, NZ, 2 * PIECE, chunk), bf16),
+            pltpu.VMEM((MERGED, 2 * PIECE, chunk), bf16),
         ],
         interpret=INTERPRET,
         name="mix",
-    )(spots, den.reshape(NZ, NX, 2 * PIECE, chunk), down, down, *after)
-
-
-def final_kernel(*refs):
-    own, oth, up_num, up_den, dn_num, dn_den = refs[:6]
-    out_ref = refs[-1]
+    )(spots, den.reshape(NZ, NX, 2 * PIECE, chunk), down, down)
+
+
+def ratio(group):
+    own, oth, up_num, up_den, dn_num, dn_den = group
+    num = own[0, 2].astype(f32) + oth[0, 2].astype(f32) + up_num.astype(f32) + dn_num.astype(f32)
+    den = own[1, 2].astype(f32) + oth[1, 2].astype(f32) + up_den.astype(f32) + dn_den.astype(f32)
+    return (num / den).astype(bf16)
+
+
+def final_kernel(first_ref, own, oth, up_num, up_den, dn_num, dn_den, out_ref):
+    k = pl.program_id(0)
     tot = []
     for arr, up, dn in ((0, up_num, dn_num), (1, up_den, dn_den)):
         tot.append(
             own[arr, 0].astype(f32) + oth[arr, 0].astype(f32) + up[...].astype(f32) + dn[...].astype(f32)
         )
-    res = (tot[0] / tot[1]).astype(bf16)
-    for m in range(OWN):
-        out_ref[m, 0] = res[m * PIECE : (m + 1) * PIECE]
-
-
-def final(half, group, *before):
-    _, width = group[2].shape
+    second = (tot[0] / tot[1]).astype(bf16)
+    for half, res in zip(HALVES, (first_ref[...], second)):
+        for j, e in enumerate(half):
+            s = lax.rem(k + e, NX)
+            for m in range(OWN):
+                start = (2 * m + j) * PIECE
+                out_ref[m, s] = res[start : start + PIECE]
+
+
+def final(first, group):
+    tall, width = first.shape
     chunk = width // NX
-    block = OWN * PIECE
-    flat = pl.BlockSpec((block, chunk), lambda k, j: (j, k))
-    rest = pl.BlockSpec((2, 1, block, chunk), lambda k, j: (0, 2, j, k))
-    first, gap = half[0], half[1] - half[0]
+    flat = pl.BlockSpec((tall, chunk), lambda k: (0, k))
+    rest = pl.BlockSpec((2, 1, tall, chunk), lambda k: (0, 2, 0, k))
     return pl.pallas_call(
         final_kernel,
-        grid=(NX, 2),
-        in_specs=[rest, rest, flat, flat, flat, flat] + [pl.BlockSpec(memory_space=pl.ANY)] * len(before),
-        out_specs=pl.BlockSpec(
-            (OWN, 1, PIECE, chunk), lambda k, j: (0, lax.rem(k + first + gap * j, NX), 0, k)
-        ),
+        grid=(NX,),
+        in_specs=[flat, rest, rest, flat, flat, flat, flat],
+        out_specs=pl.BlockSpec((OWN, NX, PIECE, chunk), lambda k: (0, 0, 0, k)),
         out_shape=jax.ShapeDtypeStruct((OWN, NX, PIECE, width), bf16),
-        input_output_aliases={6: 0} if before else {},
         interpret=INTERPRET,
         name="final",
-    )(*group, *before)
+    )(first, *group)
 
 
 def sums(*groups):
@@ -368,7 +375,7 @@
     )
     up_num = shift(one_num, "y", NY, 1)
     dn_den = shift(three_den, "y", NY, -1)
-    return (own, oth, up_num, up_den, dn_num, dn_den), (one_num, three_den)
+    return own, oth, up_num, up_den, dn_num, dn_den
 
 
 def per_device(tokens, cotangent, routes, route_weights, gate, up, down, cluster, merged_slot):
@@ -431,16 +438,14 @@
     spots = (core * NY + hop) * OWN + row
 
     groups = []
-    after = ()
     for half in HALVES:
         denom = fisher_half(half, parts, grad_near, grad_far)
         denom_recv = lax.all_to_all(denom, ("z", "x"), 0, 0, tiled=True)
-        mixed = mix(half, spots, denom_recv, down_recv, after)
+        mixed = mix(half, spots, denom_recv, down_recv)
         own2, snd2, own, snd = mixed
-        group, after = reduce_slots(snd2, snd, own2, own)
-        groups.append(group)
-    first = final(HALVES[0], groups[0])
-    return final(HALVES[1], groups[1], first)
+        groups.append(reduce_slots(snd2, snd, own2, own))
+    first = ratio(groups[0])
+    return final(first, groups[1])
 
 
 def solution(mesh):

time: 329 us -> 312 us (0.948)
  Pallas kernels: 56.9 us -> 48.3 us
  starting transfers between devices: 85.6 us -> 80.9 us
    all_to_all x2, waiting for transfers between devices: 31.9 us -> 21.4 us  [per_device(): denom_recv = lax.all_to_all(denom, ('z', 'x'), 0, 0, tiled=True)]
    ppermute x40, waiting for transfers between devices: 111 us -> 119 us  [shift(): return lax.ppermute(a, axis, [(i, (i + step) % size) for i in range(size)])]
    pallas_call x2 -> x1, Pallas kernels: 10.7 us -> 3.91 us  [final(): pl.pallas_call(final_kernel, grid=(NX,), in_specs=[flat, rest, rest, flat...]
    ppermute x40, starting transfers between devices: 62.3 us -> 56.9 us  [shift(): return lax.ppermute(a, axis, [(i, (i + step) % size) for i in range(size)])]
    convert_element_type x6, other arithmetic: 6.74 us -> 3.45 us  [sums(): outs.append(total.astype(bf16))]
  transfers between devices with their start and end apart: 43 -> 43, of which waited for: 22 -> 23; matrix products, arithmetic and copies ran while one was open for 3% -> 3% of each run, Pallas kernels for 12% -> 14%
where the time goes in v2:
time: 312 us; the launch traced here: 311 us
  waiting for transfers between devices  140 us (45%)
  starting transfers between devices  80.9 us (26%)
  Pallas kernels  48.3 us (15%)
  blocking collectives  26.9 us (9%)
  other arithmetic  8.26 us (3%)
  local copies, waits for them, and re-layouts  5.92 us (2%)
    ppermute x40, waiting for transfers between devices, shift(): return lax.ppermute(a, axis, [(i, (i + step) % size) for i in range(size)])  119 us
    ppermute x40, starting transfers between devices, shift(): return lax.ppermute(a, axis, [(i, (i + step) % size) for i in range(size)])  56.9 us
    all_to_all x1, blocking collectives, per_device(): cot0 = lax.all_to_all(cot_send, ('z', 'x'), 0, 0, tiled=True)  26.9 us
    all_to_all x2, waiting for transfers between devices, per_device(): denom_recv = lax.all_to_all(denom, ('z', 'x'), 0, 0, tiled=True)  21.4 us
    all_to_all x2, starting transfers between devices, per_device(): denom_recv = lax.all_to_all(denom, ('z', 'x'), 0, 0, tiled=True)  18.4 us
    pallas_call x2, Pallas kernels, hidden(): pl.pallas_call(functools.partial(hidden_kernel, pieces=len(pieces), known...  13.3 us
    pallas_call x2, Pallas kernels, mix(): pl.pallas_call(mix_kernel, grid=(NX,), in_specs=[pl.BlockSpec(memory_spac...  10.5 us
    pallas_call x2, Pallas kernels, pick(): pl.pallas_call(functools.partial(pick_kernel, ahead=ahead), grid_spec=plt...  9.79 us
  transfers between devices with their start and end apart: 43, of which 23 were waited for; matrix products, arithmetic and copies ran while one was open for 3% of the time, Pallas kernels for 14%

profile of v2, /device:TPU:2, one launch (start us, length us, event | category | flops | bytes accessed | tf_op | source)
XLA Modules:
  0.0 310.6 jit_solution(17070288242637517461)
XLA Ops:
  1.1 26.9 %all_to_all.24 = bf16[32,8,896]{2,1,0:T(8,128)(2,1)} all-to-all(bf16[32,8,896]{2,1,0:T(8,128)(2,1)S(1)} %bitcast.83), channel_id=1, replica_groups=mesh['y'=4,'c'=2,'z'=8,'x'=4] {'z','x'}, dimensions={0} | all-to-all | bytes 917504 | tf_op jit(solution)/shard_map/all_to_all | solution.py:407
  28.0 5.6 %all-to-all-start.2 = ((bf16[32,8,3584]{2,1,0:T(8,128)(2,1)}), bf16[32,8,3584]{2,1,0:T(8,128)(2,1)S(1)}, u32[]{:S(2)}, u32[]{:S(2)}) async-start(bf16[32,8,3584]{2,1,0:T(8,128)(2,1)} %bitcast.82), calls=%async_computation.2 | async-start | bytes 3670016 | tf_op jit(solution)/shard_map/all_to_all | solution.py:416
  34.2 3.8 %pack.1 = (bf16[20,3712]{1,0:T(8,128)(2,1)}, bf16[20,3712]{1,0:T(8,128)(2,1)}, bf16[20,3712]{1,0:T(8,128)(2,1)}, bf16[20,3712]{1,0:T(8,128)(2,1)}, bf16[20,3712]...) custom-call(s32[4]{0:T(128)} %pad_add_fusion.here_ref, ...), custom_call_target="tpu_custom_call" | custom-call | tf_op jit(solution)/shard_map/pack/pallas_call | solution.py:93
  42.4 4.2 %collective-permute-start.8 = (bf16[20,3712]{1,0:T(8,128)(2,1)}, bf16[20,3712]{1,0:T(8,128)(2,1)S(1)}, u32[]{:S(2)}, u32[]{:S(2)}) collective-permute-start(bf16[20,3712]{1,0:T(8,128)(2,1)} %get-tuple-element.30), channel_id=1, source_target_pairs={{0,16},{4,20},{8,24},{12,28},{16,0},{20,4},{24,8},{28,12},{1,17},{... | collective-permute-start | bytes 445448 | tf_op jit(solution)/shard_map/ppermute | solution.py:34
  49.0 36.1 %collective-permute-done.2 = bf16[20,3712]{1,0:T(8,128)(2,1)S(1)} collective-permute-done((bf16[20,3712]{1,0:T(8,128)(2,1)}, bf16[20,3712]{1,0:T(8,128)(2,1)S(1)}, u32[]{:S(2)}, u32[]{:S(2)}) %collective-permute-start.2) | collective-permute-done | bytes 148512 | tf_op jit(solution)/shard_map/ppermute | solution.py:34
  85.2 5.4 %collective-permute-start.5 = (bf16[20,3712]{1,0:T(8,128)(2,1)}, bf16[20,3712]{1,0:T(8,128)(2,1)S(1)}, u32[]{:S(2)}, u32[]{:S(2)}) collective-permute-start(bf16[20,3712]{1,0:T(8,128)(2,1)} %get-tuple-element.27), channel_id=1, source_target_pairs={{0,24},{4,28},{8,0},{12,4},{16,8},{20,12},{24,16},{28,20},{1,25},{... | collective-permute-start | bytes 445448 | tf_op jit(solution)/shard_map/ppermute | solution.py:34
  90.6 6.2 %collective-permute-done = bf16[20,3712]{1,0:T(8,128)(2,1)S(1)} collective-permute-done((bf16[20,3712]{1,0:T(8,128)(2,1)}, bf16[20,3712]{1,0:T(8,128)(2,1)S(1)}, u32[]{:S(2)}, u32[]{:S(2)}) %collective-permute-start) | collective-permute-done | bytes 148512 | tf_op jit(solution)/shard_map/ppermute | solution.py:34
  101.1 6.2 %collective-permute-done.6 = bf16[20,3712]{1,0:T(8,128)(2,1)S(1)} collective-permute-done((bf16[20,3712]{1,0:T(8,128)(2,1)}, bf16[20,3712]{1,0:T(8,128)(2,1)S(1)}, u32[]{:S(2)}, u32[]{:S(2)}) %collective-permute-start.6) | collective-permute-done | bytes 148512 | tf_op jit(solution)/shard_map/ppermute | solution.py:34
  114.6 9.3 %collective-permute-done.9.refs_3_ = bf16[80,3712]{1,0:T(8,128)(2,1)} collective-permute-done((bf16[80,3712]{1,0:T(8,128)(2,1)S(1)}, bf16[80,3712]{1,0:T(8,128)(2,1)}, u32[]{:S(2)}, u32[]{:S(2)}) %collective-permute-start.9) | collective-permute-done | bytes 593952 | tf_op jit(solution)/shard_map/ppermute | solution.py:34
  127.2 6.9 %collective-permute-done.11.refs_2_ = bf16[80,3712]{1,0:T(8,128)(2,1)S(1)} collective-permute-done((bf16[80,3712]{1,0:T(8,128)(2,1)S(1)}, bf16[80,3712]{1,0:T(8,128)(2,1)S(1)}, u32[]{:S(2)}, u32[]{:S(2)}) %collective-permute-start.11) | collective-permute-done | bytes 593952 | tf_op jit(solution)/shard_map/ppermute | solution.py:34
  138.5 7.2 %collective-permute-done.20 = bf16[32,8,896]{2,1,0:T(8,128)(2,1)} collective-permute-done((bf16[32,8,896]{2,1,0:T(8,128)(2,1)}, bf16[32,8,896]{2,1,0:T(8,128)(2,1)}, u32[]{:S(2)}, u32[]{:S(2)}) %collective-permute-start.20) | collective-permute-done | bytes 458784 | tf_op jit(solution)/shard_map/ppermute | solution.py:34
  145.7 8.2 %hidden.2.refs_4_ = bf16[480,256]{1,0:T(8,128)(2,1)} custom-call(bf16[80,3712]{1,0:T(8,128)(2,1)} %copy-done.4, bf16[80,3712]{1,0:T(8,128)(2,1)} %copy-done.5, bf16[80,3712]{1,0:T(8,128)(2,1)} %copy-done.9, bf16[80,3712]{1,0:T(8,128)(2,1)} %collective-permute-done.9.refs_3_, bf16[80,3712]{1,0:T(8,128)(2,1)} %copy-done.8, bf16[80,3712]{1,0:T(8,128)(2,1)} %copy-done.10, ...), custom_call_target="tpu_custom_call" | custom-call | tf_op jit(solution)/shard_map/hidden/pallas_call | solution.py:212
  155.7 5.0 %hidden.3 = (bf16[160,256]{1,0:T(8,128)(2,1)}, bf16[640,256]{1,0:T(8,128)(2,1)}) custom-call(bf16[80,3712]{1,0:T(8,128)(2,1)} %copy-done.11, bf16[80,3712]{1,0:T(8,128)(2,1)} %collective-permute-done.10.refs_1_, bf16[256,3584]{1,0:T(8,128)(2,1)} %refs_2_.1, bf16[256,3584]{1,0:T(8,128)(2,1)} %refs_3_.1, bf16[480,256]{1,0:T(8,128)(2,1)} %hidden.2.refs_4_), custom_call_target="tpu_custom_call" | custom-call | tf_op jit(solution)/shard_map/hidden/pallas_call | solution.py:212
  160.7 3.8 %collective-permute-start.14 = (bf16[160,256]{1,0:T(8,128)(2,1)}, bf16[160,256]{1,0:T(8,128)(2,1)S(1)}, u32[]{:S(2)}, u32[]{:S(2)}) collective-permute-start(bf16[160,256]{1,0:T(8,128)(2,1)} %get-tuple-element.32), channel_id=1, source_target_pairs={{0,3},{1,0},{2,1},{3,2},{4,7},{5,4},{6,5},{7,6},{8,11},{9,8},{10,9... | collective-permute-start | bytes 245768 | tf_op jit(solution)/shard_map/ppermute | solution.py:34
  164.6 6.2 %pick.2 = bf16[6,80,896]{2,1,0:T(8,128)(2,1)} custom-call(s32[4]{0:T(128)} %pad_add_fusion.here_ref, bf16[80,3712]{1,0:T(8,128)(2,1)} %copy-done.4, bf16[80,3712]{1,0:T(8,128)(2,1)} %copy-done.5, bf16[80,3712]{1,0:T(8,128)(2,1)} %copy-done.9, bf16[80,3712]{1,0:T(8,128)(2,1)} %collective-permute-done.9.refs_3_, bf16[80,3712]{1,0:T(8,128)(2,1)} %copy-done.8, ...), custom_call_target="tpu_custom_call" | custom-call | tf_op jit(solution)/shard_map/pick/pallas_call | solution.py:158
  170.8 3.6 %pick.3 = bf16[2,80,896]{2,1,0:T(8,128)(2,1)} custom-call(s32[4]{0:T(128)} %pad_add_fusion.here_ref, bf16[80,3712]{1,0:T(8,128)(2,1)} %copy-done.11, bf16[80,3712]{1,0:T(8,128)(2,1)} %collective-permute-done.10.refs_1_, bf16[8,4,8,896]{3,2,1,0:T(8,128)(2,1)} %bitcast.77, bf16[8,4,8,896]{3,2,1,0:T(8,128)(2,1)} %bitcast.10.refs_7_.refs_3_, ...), custom_call_target="tpu_custom_call" | custom-call | tf_op jit(solution)/shard_map/pick/pallas_call | solution.py:158
  175.1 3.5 %fisher.2 = bf16[32,16,896]{2,1,0:T(8,128)(2,1)} custom-call(bf16[640,256]{1,0:T(8,128)(2,1)} %get-tuple-element.31.refs_0_, bf16[480,256]{1,0:T(8,128)(2,1)} %copy-done.20, bf16[160,256]{1,0:T(8,128)(2,1)} %copy-done.21, bf16[3,160,896]{2,1,0:T(8,128)(2,1)} %bitcast.74, bf16[1,160,896]{2,1,0:T(8,128)(2,1)} %bitcast.80), custom_call_target="tpu_custom_call" | custom-call | tf_op jit(solution)/shard_map/fisher/pallas_call | solution.py:246
  178.6 5.6 %all-to-all-start.1 = ((bf16[32,16,896]{2,1,0:T(8,128)(2,1)}), bf16[32,16,896]{2,1,0:T(8,128)(2,1)S(1)}, u32[]{:S(2)}, u32[]{:S(2)}) async-start(bf16[32,16,896]{2,1,0:T(8,128)(2,1)} %fisher.2), calls=%async_computation.1 | async-start | bytes 1835008 | tf_op jit(solution)/shard_map/all_to_all | solution.py:443
  186.6 14.0 %collective-permute-done.30.refs_0_ = bf16[640,256]{1,0:T(8,128)(2,1)S(1)} collective-permute-done((bf16[640,256]{1,0:T(8,128)(2,1)S(1)}, bf16[640,256]{1,0:T(8,128)(2,1)S(1)}, u32[]{:S(2)}, u32[]{:S(2)}) %collective-permute-start.30) | collective-permute-done | bytes 327712 | tf_op jit(solution)/shard_map/ppermute | solution.py:34
  203.1 3.4 %fisher.3 = bf16[32,16,896]{2,1,0:T(8,128)(2,1)} custom-call(bf16[640,256]{1,0:T(8,128)(2,1)} %copy-done.19, bf16[640,256]{1,0:T(8,128)(2,1)} %collective-permute-done.31.refs_1_, bf16[3,160,896]{2,1,0:T(8,128)(2,1)} %bitcast.75, bf16[1,160,896]{2,1,0:T(8,128)(2,1)} %bitcast.81), custom_call_target="tpu_custom_call" | custom-call | tf_op jit(solution)/shard_map/fisher/pallas_call | solution.py:246
  209.5 12.9 %all-to-all-start.3 = ((bf16[32,16,896]{2,1,0:T(8,128)(2,1)}), bf16[32,16,896]{2,1,0:T(8,128)(2,1)S(1)}, u32[]{:S(2)}, u32[]{:S(2)}) async-start(bf16[32,16,896]{2,1,0:T(8,128)(2,1)} %fisher.3), calls=%async_computation.3 | async-start | bytes 1835008 | tf_op jit(solution)/shard_map/all_to_all | solution.py:443
  223.3 5.2 %mix.2 = (bf16[2,48,3584]{2,1,0:T(8,128)(2,1)}, bf16[2,48,3584]{2,1,0:T(8,128)(2,1)}, bf16[2,3,48,3584]{3,2,1,0:T(8,128)(2,1)}, bf16[2,3,48,3584]{3,2,1,0:T(8,128)(2,1)}) custom-call(s32[8]{0:T(128)} %fusion.17.spot_ref, bf16[8,4,16,896]{3,2,1,0:T(8,128)(2,1)} %bitcast.78, bf16[8,4,8,3584]{3,2,1,0:T(8,128)(2,1)} %bitcast.70, bf16[8,4,8,3584]{3,2,1,0:T(8,128)(2,1)} %bitcast.71), custom_call_target="tpu_custom_call" | custom-call | tf_op jit(solution)/shard_map/mix/pallas_call | solution.py:295
  229.0 18.4 %all-to-all-done.3 = bf16[32,16,896]{2,1,0:T(8,128)(2,1)S(1)} async-done(((bf16[32,16,896]{2,1,0:T(8,128)(2,1)}), bf16[32,16,896]{2,1,0:T(8,128)(2,1)S(1)}, u32[]{:S(2)}, u32[]{:S(2)}) %all-to-all-start.3) | async-done | bytes 917536 | tf_op jit(solution)/shard_map/all_to_all | solution.py:443
  248.3 5.3 %mix.3 = (bf16[2,48,3584]{2,1,0:T(8,128)(2,1)}, bf16[2,48,3584]{2,1,0:T(8,128)(2,1)}, bf16[2,3,48,3584]{3,2,1,0:T(8,128)(2,1)}, bf16[2,3,48,3584]{3,2,1,0:T(8,128)(2,1)}) custom-call(s32[8]{0:T(128)} %fusion.17.spot_ref, bf16[8,4,16,896]{3,2,1,0:T(8,128)(2,1)} %bitcast.79, bf16[8,4,8,3584]{3,2,1,0:T(8,128)(2,1)} %bitcast.72, bf16[8,4,8,3584]{3,2,1,0:T(8,128)(2,1)} %bitcast.73), custom_call_target="tpu_custom_call" | custom-call | tf_op jit(solution)/shard_map/mix/pallas_call | solution.py:295
  261.2 4.7 %collective-permute-done.24 = bf16[48,3584]{1,0:T(8,128)(2,1)S(1)} collective-permute-done((bf16[48,3584]{1,0:T(8,128)(2,1)S(1)}, bf16[48,3584]{1,0:T(8,128)(2,1)S(1)}, u32[]{:S(2)}, u32[]{:S(2)}) %collective-permute-start.24) | collective-permute-done | bytes 344096 | tf_op jit(solution)/shard_map/ppermute | solution.py:34
  267.9 3.8 %collective-permute-start.29 = (bf16[48,3584]{1,0:T(8,128)(2,1)S(1)}, bf16[48,3584]{1,0:T(8,128)(2,1)S(1)}, u32[]{:S(2)}, u32[]{:S(2)}) collective-permute-start(bf16[48,3584]{1,0:T(8,128)(2,1)S(1)} %get-tuple-element.46), channel_id=1, source_target_pairs={{0,192},{64,0},{128,64},{192,128},{1,193},{65,1},{129,65},{193,129... | collective-permute-start | bytes 1032200 | tf_op jit(solution)/shard_map/ppermute | solution.py:34
  273.7 3.7 %collective-permute-start.26 = (bf16[48,3584]{1,0:T(8,128)(2,1)S(1)}, bf16[48,3584]{1,0:T(8,128)(2,1)S(1)}, u32[]{:S(2)}, u32[]{:S(2)}) collective-permute-start(bf16[48,3584]{1,0:T(8,128)(2,1)S(1)} %get-tuple-element.47), channel_id=1, source_target_pairs={{0,192},{64,0},{128,64},{192,128},{1,193},{65,1},{129,65},{193,129... | collective-permute-start | bytes 1032200 | tf_op jit(solution)/shard_map/ppermute | solution.py:34
  282.1 3.3 %collective-permute-done.27 = bf16[48,3584]{1,0:T(8,128)(2,1)S(1)} collective-permute-done((bf16[48,3584]{1,0:T(8,128)(2,1)S(1)}, bf16[48,3584]{1,0:T(8,128)(2,1)S(1)}, u32[]{:S(2)}, u32[]{:S(2)}) %collective-permute-start.27) | collective-permute-done | bytes 344096 | tf_op jit(solution)/shard_map/ppermute | solution.py:34
  288.5 3.7 %collective-permute-start.39 = (bf16[48,3584]{1,0:T(8,128)(2,1)S(1)}, bf16[48,3584]{1,0:T(8,128)(2,1)}, u32[]{:S(2)}, u32[]{:S(2)}) collective-permute-start(bf16[48,3584]{1,0:T(8,128)(2,1)S(1)} %get-tuple-element.41), channel_id=1, source_target_pairs={{0,192},{64,0},{128,64},{192,128},{1,193},{65,1},{129,65},{193,129... | collective-permute-start | bytes 1032200 | tf_op jit(solution)/shard_map/ppermute | solution.py:34
  295.0 5.2 %collective-permute-done.35.up_num = bf16[48,3584]{1,0:T(8,128)(2,1)S(1)} collective-permute-done((bf16[48,3584]{1,0:T(8,128)(2,1)S(1)}, bf16[48,3584]{1,0:T(8,128)(2,1)S(1)}, u32[]{:S(2)}, u32[]{:S(2)}) %collective-permute-start.35) | collective-permute-done | bytes 344096 | tf_op jit(solution)/shard_map/ppermute | solution.py:34
  300.2 5.6 %collective-permute-done.36.up_den = bf16[48,3584]{1,0:T(8,128)(2,1)S(1)} collective-permute-done((bf16[48,3584]{1,0:T(8,128)(2,1)S(1)}, bf16[48,3584]{1,0:T(8,128)(2,1)S(1)}, u32[]{:S(2)}, u32[]{:S(2)}) %collective-permute-start.36) | collective-permute-done | bytes 344096 | tf_op jit(solution)/shard_map/ppermute | solution.py:34
  306.7 3.9 %final.1 = bf16[3,4,8,3584]{3,2,1,0:T(8,128)(2,1)} custom-call(bf16[48,3584]{1,0:T(8,128)(2,1)} %fusion.5.first_ref, bf16[2,3,48,3584]{3,2,1,0:T(8,128)(2,1)} %get-tuple-element.37.own, bf16[2,3,48,3584]{3,2,1,0:T(8,128)(2,1)} %copy-done.3, bf16[48,3584]{1,0:T(8,128)(2,1)} %copy-done.15, bf16[48,3584]{1,0:T(8,128)(2,1)} %copy-done.16, ...), custom_call_target="tpu_custom_call" | custom-call | tf_op jit(solution)/shard_map/final/pallas_call | solution.py:343
  (129 shorter events, 63.2 us)
Async XLA Ops:
  28.0 150.6 %all-to-all-start.2 = ((bf16[32,8,3584]{2,1,0:T(8,128)(2,1)}), bf16[32,8,3584]{2,1,0:T(8,128)(2,1)S(1)}, u32[]{:S(2)}, u32[]{:S(2)}) async-start(bf16[32,8,3584]{2,1,0:T(8,128)(2,1)} %bitcast.82), calls=%async_computation.2 | async-start | bytes 3670016 | tf_op jit(solution)/shard_map/all_to_all | solution.py:416
  38.0 47.1 %collective-permute-start.2 = (bf16[20,3712]{1,0:T(8,128)(2,1)}, bf16[20,3712]{1,0:T(8,128)(2,1)S(1)}, u32[]{:S(2)}, u32[]{:S(2)}) collective-permute-start(bf16[20,3712]{1,0:T(8,128)(2,1)} %get-tuple-element.26), channel_id=1, source_target_pairs={{0,8},{4,12},{8,16},{12,20},{16,24},{20,28},{24,0},{28,4},{1,9},{5... | collective-permute-start | bytes 445448 | tf_op jit(solution)/shard_map/ppermute | solution.py:34
  40.4 44.7 %collective-permute-start.1 = (bf16[20,3712]{1,0:T(8,128)(2,1)}, bf16[20,3712]{1,0:T(8,128)(2,1)S(1)}, u32[]{:S(2)}, u32[]{:S(2)}) collective-permute-start(bf16[20,3712]{1,0:T(8,128)(2,1)} %get-tuple-element.25), channel_id=1, source_target_pairs={{0,28},{4,0},{8,4},{12,8},{16,12},{20,16},{24,20},{28,24},{1,29},{... | collective-permute-start | bytes 445448 | tf_op jit(solution)/shard_map/ppermute | solution.py:34
  42.2 54.6 %collective-permute-start = (bf16[20,3712]{1,0:T(8,128)(2,1)}, bf16[20,3712]{1,0:T(8,128)(2,1)S(1)}, u32[]{:S(2)}, u32[]{:S(2)}) collective-permute-start(bf16[20,3712]{1,0:T(8,128)(2,1)} %get-tuple-element.24), channel_id=1, source_target_pairs={{0,4},{4,8},{8,12},{12,16},{16,20},{20,24},{24,28},{28,0},{1,5},{5... | collective-permute-start | bytes 445448 | tf_op jit(solution)/shard_map/ppermute | solution.py:34
  42.4 58.7 %collective-permute-start.8 = (bf16[20,3712]{1,0:T(8,128)(2,1)}, bf16[20,3712]{1,0:T(8,128)(2,1)S(1)}, u32[]{:S(2)}, u32[]{:S(2)}) collective-permute-start(bf16[20,3712]{1,0:T(8,128)(2,1)} %get-tuple-element.30), channel_id=1, source_target_pairs={{0,16},{4,20},{8,24},{12,28},{16,0},{20,4},{24,8},{28,12},{1,17},{... | collective-permute-start | bytes 445448 | tf_op jit(solution)/shard_map/ppermute | solution.py:34
  46.7 54.4 %collective-permute-start.7 = (bf16[20,3712]{1,0:T(8,128)(2,1)}, bf16[20,3712]{1,0:T(8,128)(2,1)S(1)}, u32[]{:S(2)}, u32[]{:S(2)}) collective-permute-start(bf16[20,3712]{1,0:T(8,128)(2,1)} %get-tuple-element.29), channel_id=1, source_target_pairs={{0,20},{4,24},{8,28},{12,0},{16,4},{20,8},{24,12},{28,16},{1,21},{... | collective-permute-start | bytes 445448 | tf_op jit(solution)/shard_map/ppermute | solution.py:34
  85.1 22.2 %collective-permute-start.6 = (bf16[20,3712]{1,0:T(8,128)(2,1)}, bf16[20,3712]{1,0:T(8,128)(2,1)S(1)}, u32[]{:S(2)}, u32[]{:S(2)}) collective-permute-start(bf16[20,3712]{1,0:T(8,128)(2,1)} %get-tuple-element.28), channel_id=1, source_target_pairs={{0,12},{4,16},{8,20},{12,24},{16,28},{20,0},{24,4},{28,8},{1,13},{... | collective-permute-start | bytes 445448 | tf_op jit(solution)/shard_map/ppermute | solution.py:34
  85.2 22.2 %collective-permute-start.5 = (bf16[20,3712]{1,0:T(8,128)(2,1)}, bf16[20,3712]{1,0:T(8,128)(2,1)S(1)}, u32[]{:S(2)}, u32[]{:S(2)}) collective-permute-start(bf16[20,3712]{1,0:T(8,128)(2,1)} %get-tuple-element.27), channel_id=1, source_target_pairs={{0,24},{4,28},{8,0},{12,4},{16,8},{20,12},{24,16},{28,20},{1,25},{... | collective-permute-start | bytes 445448 | tf_op jit(solution)/shard_map/ppermute | solution.py:34
  107.5 16.5 %collective-permute-start.9 = (bf16[80,3712]{1,0:T(8,128)(2,1)S(1)}, bf16[80,3712]{1,0:T(8,128)(2,1)}, u32[]{:S(2)}, u32[]{:S(2)}) collective-permute-start(bf16[80,3712]{1,0:T(8,128)(2,1)S(1)} %pad_maximum_fusion.1.refs_1_), channel_id=1, source_target_pairs={{0,3},{1,0},{2,1},{3,2},{4,7},{5,4},{6,5},{7,6},{8,11},{9,8},{10,9... | collective-permute-start | bytes 1781768 | tf_op jit(solution)/shard_map/ppermute | solution.py:34
  108.2 25.9 %collective-permute-start.11 = (bf16[80,3712]{1,0:T(8,128)(2,1)S(1)}, bf16[80,3712]{1,0:T(8,128)(2,1)S(1)}, u32[]{:S(2)}, u32[]{:S(2)}) collective-permute-start(bf16[80,3712]{1,0:T(8,128)(2,1)S(1)} %pad_maximum_fusion.refs_0_), channel_id=1, source_target_pairs={{0,3},{1,0},{2,1},{3,2},{4,7},{5,4},{6,5},{7,6},{8,11},{9,8},{10,9... | collective-permute-start | bytes 1781768 | tf_op jit(solution)/shard_map/ppermute | solution.py:34
  110.8 24.8 %collective-permute-start.12 = (bf16[80,3712]{1,0:T(8,128)(2,1)S(1)}, bf16[80,3712]{1,0:T(8,128)(2,1)S(1)}, u32[]{:S(2)}, u32[]{:S(2)}) collective-permute-start(bf16[80,3712]{1,0:T(8,128)(2,1)S(1)} %pad_maximum_fusion.1.refs_1_), channel_id=1, source_target_pairs={{0,1},{1,2},{2,3},{3,0},{4,5},{5,6},{6,7},{7,4},{8,9},{9,10},{10,1... | collective-permute-start | bytes 1781768 | tf_op jit(solution)/shard_map/ppermute | solution.py:34
  110.8 26.4 %collective-permute-start.4 = (bf16[80,3712]{1,0:T(8,128)(2,1)S(1)}, bf16[80,3712]{1,0:T(8,128)(2,1)S(1)}, u32[]{:S(2)}, u32[]{:S(2)}) collective-permute-start(bf16[80,3712]{1,0:T(8,128)(2,1)S(1)} %collective-permute-done.3.refs_4_), channel_id=1, source_target_pairs={{0,1},{1,2},{2,3},{3,0},{4,5},{5,6},{6,7},{7,4},{8,9},{9,10},{10,1... | collective-permute-start | bytes 1781768 | tf_op jit(solution)/shard_map/ppermute | solution.py:34
  111.6 25.6 %collective-permute-start.16 = (bf16[32,8,896]{2,1,0:T(8,128)(2,1)}, bf16[32,8,896]{2,1,0:T(8,128)(2,1)}, u32[]{:S(2)}, u32[]{:S(2)}) collective-permute-start(bf16[32,8,896]{2,1,0:T(8,128)(2,1)} %all_to_all.24), channel_id=1, source_target_pairs={{0,192},{64,0},{128,64},{192,128},{1,193},{65,1},{129,65},{193,129... | collective-permute-start | bytes 1376264 | tf_op jit(solution)/shard_map/ppermute | solution.py:34
  135.6 18.3 %collective-permute-start.10 = (bf16[80,3712]{1,0:T(8,128)(2,1)}, bf16[80,3712]{1,0:T(8,128)(2,1)}, u32[]{:S(2)}, u32[]{:S(2)}) collective-permute-start(bf16[80,3712]{1,0:T(8,128)(2,1)} %collective-permute-done.9.refs_3_), channel_id=1, source_target_pairs={{0,3},{1,0},{2,1},{3,2},{4,7},{5,4},{6,5},{7,6},{8,11},{9,8},{10,9... | collective-permute-start | bytes 1781768 | tf_op jit(solution)/shard_map/ppermute | solution.py:34
  137.2 23.5 %collective-permute-start.15 = (bf16[32,8,896]{2,1,0:T(8,128)(2,1)}, bf16[32,8,896]{2,1,0:T(8,128)(2,1)}, u32[]{:S(2)}, u32[]{:S(2)}) collective-permute-start(bf16[32,8,896]{2,1,0:T(8,128)(2,1)} %all_to_all.24), channel_id=1, source_target_pairs={{0,32},{32,0},{1,33},{33,1},{2,34},{34,2},{3,35},{35,3},{4,36},{36... | collective-permute-start | bytes 1376264 | tf_op jit(solution)/shard_map/ppermute | solution.py:34
  138.0 26.5 %collective-permute-start.17 = (bf16[32,8,896]{2,1,0:T(8,128)(2,1)}, bf16[32,8,896]{2,1,0:T(8,128)(2,1)}, u32[]{:S(2)}, u32[]{:S(2)}) collective-permute-start(bf16[32,8,896]{2,1,0:T(8,128)(2,1)} %collective-permute-done.16), channel_id=1, source_target_pairs={{0,32},{32,0},{1,33},{33,1},{2,34},{34,2},{3,35},{35,3},{4,36},{36... | collective-permute-start | bytes 1376264 | tf_op jit(solution)/shard_map/ppermute | solution.py:34
  138.0 26.5 %collective-permute-start.19 = (bf16[32,8,896]{2,1,0:T(8,128)(2,1)}, bf16[32,8,896]{2,1,0:T(8,128)(2,1)}, u32[]{:S(2)}, u32[]{:S(2)}) collective-permute-start(bf16[32,8,896]{2,1,0:T(8,128)(2,1)} %collective-permute-done.18), channel_id=1, source_target_pairs={{0,32},{32,0},{1,33},{33,1},{2,34},{34,2},{3,35},{35,3},{4,36},{36... | collective-permute-start | bytes 1376264 | tf_op jit(solution)/shard_map/ppermute | solution.py:34
  145.7 18.9 %collective-permute-start.21 = (bf16[32,8,896]{2,1,0:T(8,128)(2,1)}, bf16[32,8,896]{2,1,0:T(8,128)(2,1)}, u32[]{:S(2)}, u32[]{:S(2)}) collective-permute-start(bf16[32,8,896]{2,1,0:T(8,128)(2,1)} %collective-permute-done.20), channel_id=1, source_target_pairs={{0,32},{32,0},{1,33},{33,1},{2,34},{34,2},{3,35},{35,3},{4,36},{36... | collective-permute-start | bytes 1376264 | tf_op jit(solution)/shard_map/ppermute | solution.py:34
  153.9 20.4 %collective-permute-start.13 = (bf16[480,256]{1,0:T(8,128)(2,1)}, bf16[480,256]{1,0:T(8,128)(2,1)S(1)}, u32[]{:S(2)}, u32[]{:S(2)}) collective-permute-start(bf16[480,256]{1,0:T(8,128)(2,1)} %hidden.2.refs_4_), channel_id=1, source_target_pairs={{0,3},{1,0},{2,1},{3,2},{4,7},{5,4},{6,5},{7,6},{8,11},{9,8},{10,9... | collective-permute-start | bytes 737288 | tf_op jit(solution)/shard_map/ppermute | solution.py:34
  178.6 30.9 %all-to-all-start.1 = ((bf16[32,16,896]{2,1,0:T(8,128)(2,1)}), bf16[32,16,896]{2,1,0:T(8,128)(2,1)S(1)}, u32[]{:S(2)}, u32[]{:S(2)}) async-start(bf16[32,16,896]{2,1,0:T(8,128)(2,1)} %fisher.2), calls=%async_computation.1 | async-start | bytes 1835008 | tf_op jit(solution)/shard_map/all_to_all | solution.py:443
  184.2 16.4 %collective-permute-start.30 = (bf16[640,256]{1,0:T(8,128)(2,1)S(1)}, bf16[640,256]{1,0:T(8,128)(2,1)S(1)}, u32[]{:S(2)}, u32[]{:S(2)}) collective-permute-start(bf16[640,256]{1,0:T(8,128)(2,1)S(1)} %copy-done.18), channel_id=1, source_target_pairs={{0,1},{1,2},{2,3},{3,0},{4,5},{5,6},{6,7},{7,4},{8,9},{9,10},{10,1... | collective-permute-start | bytes 983048 | tf_op jit(solution)/shard_map/ppermute | solution.py:34
  185.7 17.4 %collective-permute-start.31 = (bf16[640,256]{1,0:T(8,128)(2,1)S(1)}, bf16[640,256]{1,0:T(8,128)(2,1)}, u32[]{:S(2)}, u32[]{:S(2)}) collective-permute-start(bf16[640,256]{1,0:T(8,128)(2,1)S(1)} %copy-done.18), channel_id=1, source_target_pairs={{0,2},{1,3},{2,0},{3,1},{4,6},{5,7},{6,4},{7,5},{8,10},{9,11},{10,... | collective-permute-start | bytes 983048 | tf_op jit(solution)/shard_map/ppermute | solution.py:34
  209.5 37.9 %all-to-all-start.3 = ((bf16[32,16,896]{2,1,0:T(8,128)(2,1)}), bf16[32,16,896]{2,1,0:T(8,128)(2,1)S(1)}, u32[]{:S(2)}, u32[]{:S(2)}) async-start(bf16[32,16,896]{2,1,0:T(8,128)(2,1)} %fisher.3), calls=%async_computation.3 | async-start | bytes 1835008 | tf_op jit(solution)/shard_map/all_to_all | solution.py:443
  228.5 26.0 %collective-permute-start.23 = (bf16[2,48,3584]{2,1,0:T(8,128)(2,1)}, bf16[2,48,3584]{2,1,0:T(8,128)(2,1)S(1)}, u32[]{:S(2)}, u32[]{:S(2)}) collective-permute-start(bf16[2,48,3584]{2,1,0:T(8,128)(2,1)} %get-tuple-element.36), channel_id=1, source_target_pairs={{0,32},{32,0},{1,33},{33,1},{2,34},{34,2},{3,35},{35,3},{4,36},{36... | collective-permute-start | bytes 2064392 | tf_op jit(solution)/shard_map/ppermute | solution.py:34
  228.5 37.9 %collective-permute-start.22 = (bf16[2,3,48,3584]{3,2,1,0:T(8,128)(2,1)}, bf16[2,3,48,3584]{3,2,1,0:T(8,128)(2,1)}, u32[]{:S(2)}, u32[]{:S(2)}) collective-permute-start(bf16[2,3,48,3584]{3,2,1,0:T(8,128)(2,1)} %get-tuple-element.34), channel_id=1, source_target_pairs={{0,32},{32,0},{1,33},{33,1},{2,34},{34,2},{3,35},{35,3},{4,36},{36... | collective-permute-start | bytes 6193160 | tf_op jit(solution)/shard_map/ppermute | solution.py:34
  253.7 24.4 %collective-permute-start.32 = (bf16[2,3,48,3584]{3,2,1,0:T(8,128)(2,1)}, bf16[2,3,48,3584]{3,2,1,0:T(8,128)(2,1)S(1)}, u32[]{:S(2)}, u32[]{:S(2)}) collective-permute-start(bf16[2,3,48,3584]{3,2,1,0:T(8,128)(2,1)} %get-tuple-element.38), channel_id=1, source_target_pairs={{0,32},{32,0},{1,33},{33,1},{2,34},{34,2},{3,35},{35,3},{4,36},{36... | collective-permute-start | bytes 6193160 | tf_op jit(solution)/shard_map/ppermute | solution.py:34
  273.7 14.7 %collective-permute-start.26 = (bf16[48,3584]{1,0:T(8,128)(2,1)S(1)}, bf16[48,3584]{1,0:T(8,128)(2,1)S(1)}, u32[]{:S(2)}, u32[]{:S(2)}) collective-permute-start(bf16[48,3584]{1,0:T(8,128)(2,1)S(1)} %get-tuple-element.47), channel_id=1, source_target_pairs={{0,192},{64,0},{128,64},{192,128},{1,193},{65,1},{129,65},{193,129... | collective-permute-start | bytes 1032200 | tf_op jit(solution)/shard_map/ppermute | solution.py:34
  278.1 14.7 %collective-permute-start.25 = (bf16[48,3584]{1,0:T(8,128)(2,1)S(1)}, bf16[48,3584]{1,0:T(8,128)(2,1)S(1)}, u32[]{:S(2)}, u32[]{:S(2)}) collective-permute-start(bf16[48,3584]{1,0:T(8,128)(2,1)S(1)} %get-tuple-element.45), channel_id=1, source_target_pairs={{0,64},{64,128},{128,192},{192,0},{1,65},{65,129},{129,193},{193,1... | collective-permute-start | bytes 1032200 | tf_op jit(solution)/shard_map/ppermute | solution.py:34
  278.4 21.8 %collective-permute-start.35 = (bf16[48,3584]{1,0:T(8,128)(2,1)S(1)}, bf16[48,3584]{1,0:T(8,128)(2,1)S(1)}, u32[]{:S(2)}, u32[]{:S(2)}) collective-permute-start(bf16[48,3584]{1,0:T(8,128)(2,1)S(1)} %get-tuple-element.42), channel_id=1, source_target_pairs={{0,64},{64,128},{128,192},{192,0},{1,65},{65,129},{129,193},{193,1... | collective-permute-start | bytes 1032200 | tf_op jit(solution)/shard_map/ppermute | solution.py:34
  281.1 24.8 %collective-permute-start.36 = (bf16[48,3584]{1,0:T(8,128)(2,1)S(1)}, bf16[48,3584]{1,0:T(8,128)(2,1)S(1)}, u32[]{:S(2)}, u32[]{:S(2)}) collective-permute-start(bf16[48,3584]{1,0:T(8,128)(2,1)S(1)} %get-tuple-element.44), channel_id=1, source_target_pairs={{0,64},{64,128},{128,192},{192,0},{1,65},{65,129},{129,193},{193,1... | collective-permute-start | bytes 1032200 | tf_op jit(solution)/shard_map/ppermute | solution.py:34
  285.5 20.4 %collective-permute-start.37 = (bf16[48,3584]{1,0:T(8,128)(2,1)S(1)}, bf16[48,3584]{1,0:T(8,128)(2,1)S(1)}, u32[]{:S(2)}, u32[]{:S(2)}) collective-permute-start(bf16[48,3584]{1,0:T(8,128)(2,1)S(1)} %get-tuple-element.43), channel_id=1, source_target_pairs={{0,192},{64,0},{128,64},{192,128},{1,193},{65,1},{129,65},{193,129... | collective-permute-start | bytes 1032200 | tf_op jit(solution)/shard_map/ppermute | solution.py:34
  288.5 17.4 %collective-permute-start.39 = (bf16[48,3584]{1,0:T(8,128)(2,1)S(1)}, bf16[48,3584]{1,0:T(8,128)(2,1)}, u32[]{:S(2)}, u32[]{:S(2)}) collective-permute-start(bf16[48,3584]{1,0:T(8,128)(2,1)S(1)} %get-tuple-element.41), channel_id=1, source_target_pairs={{0,192},{64,0},{128,64},{192,128},{1,193},{65,1},{129,65},{193,129... | collective-permute-start | bytes 1032200 | tf_op jit(solution)/shard_map/ppermute | solution.py:34
  (35 other events, 424.5 us)

commit v3 on v2

--- a/solution.py
+++ b/solution.py
@@ -314,9 +314,9 @@
 
 def ratio(group):
     own, oth, up_num, up_den, dn_num, dn_den = group
-    num = own[0, 2].astype(f32) + oth[0, 2].astype(f32) + up_num.astype(f32) + dn_num.astype(f32)
-    den = own[1, 2].astype(f32) + oth[1, 2].astype(f32) + up_den.astype(f32) + dn_den.astype(f32)
-    return (num / den).astype(bf16)
+    num = [(own, (0, 2)), (oth, (0, 2)), (up_num, ()), (dn_num, ())]
+    den = [(own, (1, 2)), (oth, (1, 2)), (up_den, ()), (dn_den, ())]
+    return looped((num, den), True)[0]
 
 
 def final_kernel(first_ref, own, oth, up_num, up_den, dn_num, dn_den, out_ref):
@@ -351,6 +351,49 @@
     )(first, *group)
 
 
+def looped_kernel(*refs, counts, divide):
+    outs = refs[sum(counts) :]
+    step = outs[0].shape[1] // COLS
+
+    def body(k, carry):
+        cols = pl.ds(pl.multiple_of(k * step, step), step)
+        start = 0
+        totals = []
+        for count in counts:
+            total = refs[start][:, cols].astype(f32)
+            for r in refs[start + 1 : start + count]:
+                total = total + r[:, cols].astype(f32)
+            totals.append(total)
+            start += count
+        if divide:
+            totals = [totals[0] / totals[1]]
+        for out, total in zip(outs, totals):
+            out[:, cols] = total.astype(bf16)
+        return carry
+
+    lax.fori_loop(0, COLS, body, 0)
+
+
+def looped(groups, divide=False):
+    specs, args = [], []
+    for group in groups:
+        for arr, lead in group:
+            shape = (None,) * len(lead) + arr.shape[len(lead) :]
+            specs.append(pl.BlockSpec(shape, lambda i, lead=lead: lead + (0, 0)))
+            args.append(arr)
+    shape = groups[0][0][0].shape[-2:]
+    count = 1 if divide else len(groups)
+    return pl.pallas_call(
+        functools.partial(looped_kernel, counts=[len(g) for g in groups], divide=divide),
+        grid=(1,),
+        in_specs=specs,
+        out_specs=[pl.BlockSpec(shape, lambda i: (0, 0))] * count,
+        out_shape=[jax.ShapeDtypeStruct(shape, bf16)] * count,
+        interpret=INTERPRET,
+        name="looped",
+    )(*args)
+
+
 def sums(*groups):
     outs = []
     for group in groups:
@@ -361,16 +404,17 @@
     return outs
 
 
-def reduce_slots(snd2, snd, own2, own):
+def reduce_slots(n, snd2, snd, own2, own):
     oth2 = shift(snd2, "c", NC, 1)
     oth = shift(snd, "c", NC, 1)
-    two_num, two_den = sums([(own2, (0,)), (oth2, (0,))], [(own2, (1,)), (oth2, (1,))])
-    one_den, three_num = sums([(own, (1, 0)), (oth, (1, 0))], [(own, (0, 1)), (oth, (0, 1))])
+    add = sums if n else lambda *groups: looped(groups)
+    two_num, two_den = add([(own2, (0,)), (oth2, (0,))], [(own2, (1,)), (oth2, (1,))])
+    one_den, three_num = add([(own, (1, 0)), (oth, (1, 0))], [(own, (0, 1)), (oth, (0, 1))])
     up1 = shift(two_num, "y", NY, 1)
     dn1 = shift(two_den, "y", NY, -1)
     up_den = shift(one_den, "y", NY, 1)
     dn_num = shift(three_num, "y", NY, -1)
-    one_num, three_den = sums(
+    one_num, three_den = add(
         [(own, (0, 0)), (oth, (0, 0)), (up1, ())], [(own, (1, 1)), (oth, (1, 1)), (dn1, ())]
     )
     up_num = shift(one_num, "y", NY, 1)
@@ -416,7 +460,7 @@
     down_recv = lax.all_to_all(down, ("z", "x"), 0, 0, tiled=True)
     down_recv = down_recv.reshape(NZ, NX, PIECE, width)
 
-    (main,) = hidden(COLS, (part_a, part_b, left_a, left_b, right_a, right_b), gate, up)
+    (main,) = hidden(2 * COLS, (part_a, part_b, left_a, left_b, right_a, right_b), gate, up)
     main1 = shift(main, "x", NX, -1)
     late, full = hidden(NX, (far_a, far_b), gate, up, main)
     late1 = shift(late, "x", NX, -1)
@@ -438,12 +482,12 @@
     spots = (core * NY + hop) * OWN + row
 
     groups = []
-    for half in HALVES:
+    for n, half in enumerate(HALVES):
         denom = fisher_half(half, parts, grad_near, grad_far)
         denom_recv = lax.all_to_all(denom, ("z", "x"), 0, 0, tiled=True)
         mixed = mix(half, spots, denom_recv, down_recv)
         own2, snd2, own, snd = mixed
-        groups.append(reduce_slots(snd2, snd, own2, own))
+        groups.append(reduce_slots(n, snd2, snd, own2, own))
     first = ratio(groups[0])
     return final(first, groups[1])
 

time: 312 us -> 324 us (1.038)
  Pallas kernels: 48.3 us -> 62.5 us
  starting transfers between devices: 80.9 us -> 75.9 us
    pallas_call x0 -> x4, Pallas kernels: none -> 10.2 us  [looped(): pl.pallas_call(functools.partial(looped_kernel, counts=[len(g) for g in g...]
    ppermute x40, starting transfers between devices: 56.9 us -> 51.9 us  [shift(): return lax.ppermute(a, axis, [(i, (i + step) % size) for i in range(size)])]
    pallas_call x2, Pallas kernels: 13.3 us -> 17.4 us  [hidden(): pl.pallas_call(functools.partial(hidden_kernel, pieces=len(pieces), known...]
    convert_element_type x6 -> x3, other arithmetic: 3.45 us -> 6.95 us  [sums(): outs.append(total.astype(bf16))]
    unnamed x48 -> x54, local copies, waits for them, and re-layouts: 5.88 us -> 8.66 us
  transfers between devices with their start and end apart: 43 -> 43, of which waited for: 23 -> 20; matrix products, arithmetic and copies ran while one was open for 3% -> 3% of each run, Pallas kernels for 14% -> 18%
where the time goes in v3:
time: 324 us; the launch traced here: 323 us
  waiting for transfers between devices  139 us (43%)
  starting transfers between devices  75.9 us (23%)
  Pallas kernels  62.5 us (19%)
  blocking collectives  26.9 us (8%)
  other arithmetic  9.61 us (3%)
  local copies, waits for them, and re-layouts  8.71 us (3%)
    ppermute x40, waiting for transfers between devices, shift(): return lax.ppermute(a, axis, [(i, (i + step) % size) for i in range(size)])  117 us
    ppermute x40, starting transfers between devices, shift(): return lax.ppermute(a, axis, [(i, (i + step) % size) for i in range(size)])  51.9 us
    all_to_all x1, blocking collectives, per_device(): cot0 = lax.all_to_all(cot_send, ('z', 'x'), 0, 0, tiled=True)  26.9 us
    all_to_all x2, waiting for transfers between devices, per_device(): denom_recv = lax.all_to_all(denom, ('z', 'x'), 0, 0, tiled=True)  22 us
    all_to_all x2, starting transfers between devices, per_device(): denom_recv = lax.all_to_all(denom, ('z', 'x'), 0, 0, tiled=True)  18.4 us
    pallas_call x2, Pallas kernels, hidden(): pl.pallas_call(functools.partial(hidden_kernel, pieces=len(pieces), known...  17.4 us
    pallas_call x2, Pallas kernels, mix(): pl.pallas_call(mix_kernel, grid=(NX,), in_specs=[pl.BlockSpec(memory_spac...  10.4 us
    pallas_call x4, Pallas kernels, looped(): pl.pallas_call(functools.partial(looped_kernel, counts=[len(g) for g in g...  10.2 us
  transfers between devices with their start and end apart: 43, of which 20 were waited for; matrix products, arithmetic and copies ran while one was open for 3% of the time, Pallas kernels for 18%

profile of v3, /device:TPU:2, one launch (start us, length us, event | category | flops | bytes accessed | tf_op | source)
XLA Modules:
  0.0 322.7 jit_solution(14302162551621085699)
XLA Ops:
  1.1 26.9 %all_to_all.24 = bf16[32,8,896]{2,1,0:T(8,128)(2,1)} all-to-all(bf16[32,8,896]{2,1,0:T(8,128)(2,1)S(1)} %bitcast.52), channel_id=1, replica_groups=mesh['y'=4,'c'=2,'z'=8,'x'=4] {'z','x'}, dimensions={0} | all-to-all | bytes 917504 | tf_op jit(solution)/shard_map/all_to_all | solution.py:451
  28.0 5.6 %all-to-all-start.2 = ((bf16[32,8,3584]{2,1,0:T(8,128)(2,1)}), bf16[32,8,3584]{2,1,0:T(8,128)(2,1)S(1)}, u32[]{:S(2)}, u32[]{:S(2)}) async-start(bf16[32,8,3584]{2,1,0:T(8,128)(2,1)} %bitcast.51), calls=%async_computation.2 | async-start | bytes 3670016 | tf_op jit(solution)/shard_map/all_to_all | solution.py:460
  34.2 3.8 %pack.1 = (bf16[20,3712]{1,0:T(8,128)(2,1)}, bf16[20,3712]{1,0:T(8,128)(2,1)}, bf16[20,3712]{1,0:T(8,128)(2,1)}, bf16[20,3712]{1,0:T(8,128)(2,1)}, bf16[20,3712]...) custom-call(s32[4]{0:T(128)} %pad_add_fusion.here_ref, ...), custom_call_target="tpu_custom_call" | custom-call | tf_op jit(solution)/shard_map/pack/pallas_call | solution.py:93
  42.4 4.2 %collective-permute-start.8 = (bf16[20,3712]{1,0:T(8,128)(2,1)}, bf16[20,3712]{1,0:T(8,128)(2,1)S(1)}, u32[]{:S(2)}, u32[]{:S(2)}) collective-permute-start(bf16[20,3712]{1,0:T(8,128)(2,1)} %get-tuple-element.36), channel_id=1, source_target_pairs={{0,16},{4,20},{8,24},{12,28},{16,0},{20,4},{24,8},{28,12},{1,17},{... | collective-permute-start | bytes 445448 | tf_op jit(solution)/shard_map/ppermute | solution.py:34
  49.0 36.1 %collective-permute-done.2 = bf16[20,3712]{1,0:T(8,128)(2,1)S(1)} collective-permute-done((bf16[20,3712]{1,0:T(8,128)(2,1)}, bf16[20,3712]{1,0:T(8,128)(2,1)S(1)}, u32[]{:S(2)}, u32[]{:S(2)}) %collective-permute-start.2) | collective-permute-done | bytes 148512 | tf_op jit(solution)/shard_map/ppermute | solution.py:34
  85.2 5.4 %collective-permute-start.5 = (bf16[20,3712]{1,0:T(8,128)(2,1)}, bf16[20,3712]{1,0:T(8,128)(2,1)S(1)}, u32[]{:S(2)}, u32[]{:S(2)}) collective-permute-start(bf16[20,3712]{1,0:T(8,128)(2,1)} %get-tuple-element.33), channel_id=1, source_target_pairs={{0,24},{4,28},{8,0},{12,4},{16,8},{20,12},{24,16},{28,20},{1,25},{... | collective-permute-start | bytes 445448 | tf_op jit(solution)/shard_map/ppermute | solution.py:34
  90.6 6.2 %collective-permute-done = bf16[20,3712]{1,0:T(8,128)(2,1)S(1)} collective-permute-done((bf16[20,3712]{1,0:T(8,128)(2,1)}, bf16[20,3712]{1,0:T(8,128)(2,1)S(1)}, u32[]{:S(2)}, u32[]{:S(2)}) %collective-permute-start) | collective-permute-done | bytes 148512 | tf_op jit(solution)/shard_map/ppermute | solution.py:34
  101.1 6.2 %collective-permute-done.6 = bf16[20,3712]{1,0:T(8,128)(2,1)S(1)} collective-permute-done((bf16[20,3712]{1,0:T(8,128)(2,1)}, bf16[20,3712]{1,0:T(8,128)(2,1)S(1)}, u32[]{:S(2)}, u32[]{:S(2)}) %collective-permute-start.6) | collective-permute-done | bytes 148512 | tf_op jit(solution)/shard_map/ppermute | solution.py:34
  114.6 9.3 %collective-permute-done.9.refs_3_ = bf16[80,3712]{1,0:T(8,128)(2,1)} collective-permute-done((bf16[80,3712]{1,0:T(8,128)(2,1)S(1)}, bf16[80,3712]{1,0:T(8,128)(2,1)}, u32[]{:S(2)}, u32[]{:S(2)}) %collective-permute-start.9) | collective-permute-done | bytes 593952 | tf_op jit(solution)/shard_map/ppermute | solution.py:34
  124.0 3.2 collective-permute-start.18
  127.2 6.9 %collective-permute-done.11.refs_2_ = bf16[80,3712]{1,0:T(8,128)(2,1)S(1)} collective-permute-done((bf16[80,3712]{1,0:T(8,128)(2,1)S(1)}, bf16[80,3712]{1,0:T(8,128)(2,1)S(1)}, u32[]{:S(2)}, u32[]{:S(2)}) %collective-permute-start.11) | collective-permute-done | bytes 593952 | tf_op jit(solution)/shard_map/ppermute | solution.py:34
  138.5 7.2 %collective-permute-done.20 = bf16[32,8,896]{2,1,0:T(8,128)(2,1)} collective-permute-done((bf16[32,8,896]{2,1,0:T(8,128)(2,1)}, bf16[32,8,896]{2,1,0:T(8,128)(2,1)}, u32[]{:S(2)}, u32[]{:S(2)}) %collective-permute-start.20) | collective-permute-done | bytes 458784 | tf_op jit(solution)/shard_map/ppermute | solution.py:34
  145.7 12.3 %hidden.2.refs_4_ = bf16[480,256]{1,0:T(8,128)(2,1)} custom-call(bf16[80,3712]{1,0:T(8,128)(2,1)} %copy-done.4, bf16[80,3712]{1,0:T(8,128)(2,1)} %copy-done.5, bf16[80,3712]{1,0:T(8,128)(2,1)} %copy-done.9, bf16[80,3712]{1,0:T(8,128)(2,1)} %collective-permute-done.9.refs_3_, bf16[80,3712]{1,0:T(8,128)(2,1)} %copy-done.8, bf16[80,3712]{1,0:T(8,128)(2,1)} %copy-done.10, ...), custom_call_target="tpu_custom_call" | custom-call | tf_op jit(solution)/shard_map/hidden/pallas_call | solution.py:212
  159.8 5.0 %hidden.3 = (bf16[160,256]{1,0:T(8,128)(2,1)}, bf16[640,256]{1,0:T(8,128)(2,1)}) custom-call(bf16[80,3712]{1,0:T(8,128)(2,1)} %copy-done.11, bf16[80,3712]{1,0:T(8,128)(2,1)} %collective-permute-done.10.refs_1_, bf16[256,3584]{1,0:T(8,128)(2,1)} %refs_2_.1, bf16[256,3584]{1,0:T(8,128)(2,1)} %refs_3_.1, bf16[480,256]{1,0:T(8,128)(2,1)} %hidden.2.refs_4_), custom_call_target="tpu_custom_call" | custom-call | tf_op jit(solution)/shard_map/hidden/pallas_call | solution.py:212
  164.8 3.8 %collective-permute-start.14 = (bf16[160,256]{1,0:T(8,128)(2,1)}, bf16[160,256]{1,0:T(8,128)(2,1)S(1)}, u32[]{:S(2)}, u32[]{:S(2)}) collective-permute-start(bf16[160,256]{1,0:T(8,128)(2,1)} %get-tuple-element.38), channel_id=1, source_target_pairs={{0,3},{1,0},{2,1},{3,2},{4,7},{5,4},{6,5},{7,6},{8,11},{9,8},{10,9... | collective-permute-start | bytes 245768 | tf_op jit(solution)/shard_map/ppermute | solution.py:34
  168.7 6.3 %pick.2 = bf16[6,80,896]{2,1,0:T(8,128)(2,1)} custom-call(s32[4]{0:T(128)} %pad_add_fusion.here_ref, bf16[80,3712]{1,0:T(8,128)(2,1)} %copy-done.4, bf16[80,3712]{1,0:T(8,128)(2,1)} %copy-done.5, bf16[80,3712]{1,0:T(8,128)(2,1)} %copy-done.9, bf16[80,3712]{1,0:T(8,128)(2,1)} %collective-permute-done.9.refs_3_, bf16[80,3712]{1,0:T(8,128)(2,1)} %copy-done.8, ...), custom_call_target="tpu_custom_call" | custom-call | tf_op jit(solution)/shard_map/pick/pallas_call | solution.py:158
  175.0 3.6 %pick.3 = bf16[2,80,896]{2,1,0:T(8,128)(2,1)} custom-call(s32[4]{0:T(128)} %pad_add_fusion.here_ref, bf16[80,3712]{1,0:T(8,128)(2,1)} %copy-done.11, bf16[80,3712]{1,0:T(8,128)(2,1)} %collective-permute-done.10.refs_1_, bf16[8,4,8,896]{3,2,1,0:T(8,128)(2,1)} %bitcast.47, bf16[8,4,8,896]{3,2,1,0:T(8,128)(2,1)} %bitcast.10.refs_7_.refs_3_, ...), custom_call_target="tpu_custom_call" | custom-call | tf_op jit(solution)/shard_map/pick/pallas_call | solution.py:158
  179.2 3.5 %fisher.2 = bf16[32,16,896]{2,1,0:T(8,128)(2,1)} custom-call(bf16[640,256]{1,0:T(8,128)(2,1)} %get-tuple-element.37.refs_0_, bf16[480,256]{1,0:T(8,128)(2,1)} %copy-done.23, bf16[160,256]{1,0:T(8,128)(2,1)} %copy-done.24, bf16[3,160,896]{2,1,0:T(8,128)(2,1)} %bitcast.44, bf16[1,160,896]{2,1,0:T(8,128)(2,1)} %bitcast.49), custom_call_target="tpu_custom_call" | custom-call | tf_op jit(solution)/shard_map/fisher/pallas_call | solution.py:246
  182.8 5.6 %all-to-all-start.1 = ((bf16[32,16,896]{2,1,0:T(8,128)(2,1)}), bf16[32,16,896]{2,1,0:T(8,128)(2,1)S(1)}, u32[]{:S(2)}, u32[]{:S(2)}) async-start(bf16[32,16,896]{2,1,0:T(8,128)(2,1)} %fisher.2), calls=%async_computation.1 | async-start | bytes 1835008 | tf_op jit(solution)/shard_map/all_to_all | solution.py:487
  190.7 14.0 %collective-permute-done.30.refs_0_ = bf16[640,256]{1,0:T(8,128)(2,1)S(1)} collective-permute-done((bf16[640,256]{1,0:T(8,128)(2,1)S(1)}, bf16[640,256]{1,0:T(8,128)(2,1)S(1)}, u32[]{:S(2)}, u32[]{:S(2)}) %collective-permute-start.30) | collective-permute-done | bytes 327712 | tf_op jit(solution)/shard_map/ppermute | solution.py:34
  207.3 3.4 %fisher.3 = bf16[32,16,896]{2,1,0:T(8,128)(2,1)} custom-call(bf16[640,256]{1,0:T(8,128)(2,1)} %copy-done.22, bf16[640,256]{1,0:T(8,128)(2,1)} %collective-permute-done.31.refs_1_, bf16[3,160,896]{2,1,0:T(8,128)(2,1)} %bitcast.45, bf16[1,160,896]{2,1,0:T(8,128)(2,1)} %bitcast.50), custom_call_target="tpu_custom_call" | custom-call | tf_op jit(solution)/shard_map/fisher/pallas_call | solution.py:246
  213.7 12.9 %all-to-all-start.3 = ((bf16[32,16,896]{2,1,0:T(8,128)(2,1)}), bf16[32,16,896]{2,1,0:T(8,128)(2,1)}, u32[]{:S(2)}, u32[]{:S(2)}) async-start(bf16[32,16,896]{2,1,0:T(8,128)(2,1)} %fisher.3), calls=%async_computation.3 | async-start | bytes 1835008 | tf_op jit(solution)/shard_map/all_to_all | solution.py:487
  227.5 5.2 %mix.2 = (bf16[2,48,3584]{2,1,0:T(8,128)(2,1)}, bf16[2,48,3584]{2,1,0:T(8,128)(2,1)}, bf16[2,3,48,3584]{3,2,1,0:T(8,128)(2,1)}, bf16[2,3,48,3584]{3,2,1,0:T(8,128)(2,1)}) custom-call(s32[8]{0:T(128)} %fusion.7.spot_ref, bf16[8,4,16,896]{3,2,1,0:T(8,128)(2,1)} %bitcast.48, bf16[8,4,8,3584]{3,2,1,0:T(8,128)(2,1)} %bitcast.40, bf16[8,4,8,3584]{3,2,1,0:T(8,128)(2,1)} %bitcast.41), custom_call_target="tpu_custom_call" | custom-call | tf_op jit(solution)/shard_map/mix/pallas_call | solution.py:295
  232.7 19.0 %all-to-all-done.3 = bf16[32,16,896]{2,1,0:T(8,128)(2,1)} async-done(((bf16[32,16,896]{2,1,0:T(8,128)(2,1)}), bf16[32,16,896]{2,1,0:T(8,128)(2,1)}, u32[]{:S(2)}, u32[]{:S(2)}) %all-to-all-start.3) | async-done | bytes 917536 | tf_op jit(solution)/shard_map/all_to_all | solution.py:487
  251.7 5.2 %mix.3 = (bf16[2,48,3584]{2,1,0:T(8,128)(2,1)}, bf16[2,48,3584]{2,1,0:T(8,128)(2,1)}, bf16[2,3,48,3584]{3,2,1,0:T(8,128)(2,1)}, bf16[2,3,48,3584]{3,2,1,0:T(8,128)(2,1)}) custom-call(s32[8]{0:T(128)} %fusion.7.spot_ref, bf16[8,4,16,896]{3,2,1,0:T(8,128)(2,1)} %bitcast.22.den_ref, bf16[8,4,8,3584]{3,2,1,0:T(8,128)(2,1)} %bitcast.42, ...), custom_call_target="tpu_custom_call" | custom-call | tf_op jit(solution)/shard_map/mix/pallas_call | solution.py:295
  257.7 4.5 %collective-permute-done.23.refs_1_.refs_3_ = bf16[2,48,3584]{2,1,0:T(8,128)(2,1)S(1)} collective-permute-done((bf16[2,48,3584]{2,1,0:T(8,128)(2,1)}, bf16[2,48,3584]{2,1,0:T(8,128)(2,1)S(1)}, u32[]{:S(2)}, u32[]{:S(2)}) %collective-permute-start.23) | collective-permute-done | bytes 688160 | tf_op jit(solution)/shard_map/ppermute | solution.py:34
  271.5 5.4 %collective-permute-done.24.refs_2_ = bf16[48,3584]{1,0:T(8,128)(2,1)S(1)} collective-permute-done((bf16[48,3584]{1,0:T(8,128)(2,1)}, bf16[48,3584]{1,0:T(8,128)(2,1)S(1)}, u32[]{:S(2)}, u32[]{:S(2)}) %collective-permute-start.24) | collective-permute-done | bytes 344096 | tf_op jit(solution)/shard_map/ppermute | solution.py:34
  296.7 3.2 %collective-permute-start.37 = (bf16[48,3584]{1,0:T(8,128)(2,1)}, bf16[48,3584]{1,0:T(8,128)(2,1)S(1)}, u32[]{:S(2)}, u32[]{:S(2)}) collective-permute-start(bf16[48,3584]{1,0:T(8,128)(2,1)} %get-tuple-element.55), channel_id=1, source_target_pairs={{0,192},{64,0},{128,64},{192,128},{1,193},{65,1},{129,65},{193,129... | collective-permute-start | bytes 1032200 | tf_op jit(solution)/shard_map/ppermute | solution.py:34
  299.9 4.1 %collective-permute-done.28.refs_6_ = bf16[48,3584]{1,0:T(8,128)(2,1)S(1)} collective-permute-done((bf16[48,3584]{1,0:T(8,128)(2,1)}, bf16[48,3584]{1,0:T(8,128)(2,1)S(1)}, u32[]{:S(2)}, u32[]{:S(2)}) %collective-permute-start.28) | collective-permute-done | bytes 344096 | tf_op jit(solution)/shard_map/ppermute | solution.py:34
  307.7 3.8 %collective-permute-done.35.up_num = bf16[48,3584]{1,0:T(8,128)(2,1)} collective-permute-done((bf16[48,3584]{1,0:T(8,128)(2,1)}, bf16[48,3584]{1,0:T(8,128)(2,1)}, u32[]{:S(2)}, u32[]{:S(2)}) %collective-permute-start.35) | collective-permute-done | bytes 344096 | tf_op jit(solution)/shard_map/ppermute | solution.py:34
  311.5 5.6 %collective-permute-done.36.up_den = bf16[48,3584]{1,0:T(8,128)(2,1)S(1)} collective-permute-done((bf16[48,3584]{1,0:T(8,128)(2,1)}, bf16[48,3584]{1,0:T(8,128)(2,1)S(1)}, u32[]{:S(2)}, u32[]{:S(2)}) %collective-permute-start.36) | collective-permute-done | bytes 344096 | tf_op jit(solution)/shard_map/ppermute | solution.py:34
  318.7 3.9 %final.1 = bf16[3,4,8,3584]{3,2,1,0:T(8,128)(2,1)} custom-call(bf16[48,3584]{1,0:T(8,128)(2,1)} %looped.7.first_ref, bf16[2,3,48,3584]{3,2,1,0:T(8,128)(2,1)} %get-tuple-element.49.own, bf16[2,3,48,3584]{3,2,1,0:T(8,128)(2,1)} %collective-permute-done.32.oth, bf16[48,3584]{1,0:T(8,128)(2,1)} %collective-permute-done.35.up_num, bf16[48,3584]{1,0:T(8,128)(2,1)} %copy-done.18, ...), custom_call_target="tpu_custom_call" | custom-call | tf_op jit(solution)/shard_map/final/pallas_call | solution.py:343
  (135 shorter events, 70.8 us)
Async XLA Ops:
  28.0 154.7 %all-to-all-start.2 = ((bf16[32,8,3584]{2,1,0:T(8,128)(2,1)}), bf16[32,8,3584]{2,1,0:T(8,128)(2,1)S(1)}, u32[]{:S(2)}, u32[]{:S(2)}) async-start(bf16[32,8,3584]{2,1,0:T(8,128)(2,1)} %bitcast.51), calls=%async_computation.2 | async-start | bytes 3670016 | tf_op jit(solution)/shard_map/all_to_all | solution.py:460
  38.1 47.1 %collective-permute-start.2 = (bf16[20,3712]{1,0:T(8,128)(2,1)}, bf16[20,3712]{1,0:T(8,128)(2,1)S(1)}, u32[]{:S(2)}, u32[]{:S(2)}) collective-permute-start(bf16[20,3712]{1,0:T(8,128)(2,1)} %get-tuple-element.32), channel_id=1, source_target_pairs={{0,8},{4,12},{8,16},{12,20},{16,24},{20,28},{24,0},{28,4},{1,9},{5... | collective-permute-start | bytes 445448 | tf_op jit(solution)/shard_map/ppermute | solution.py:34
  40.4 44.7 %collective-permute-start.1 = (bf16[20,3712]{1,0:T(8,128)(2,1)}, bf16[20,3712]{1,0:T(8,128)(2,1)S(1)}, u32[]{:S(2)}, u32[]{:S(2)}) collective-permute-start(bf16[20,3712]{1,0:T(8,128)(2,1)} %get-tuple-element.31), channel_id=1, source_target_pairs={{0,28},{4,0},{8,4},{12,8},{16,12},{20,16},{24,20},{28,24},{1,29},{... | collective-permute-start | bytes 445448 | tf_op jit(solution)/shard_map/ppermute | solution.py:34
  42.2 54.6 %collective-permute-start = (bf16[20,3712]{1,0:T(8,128)(2,1)}, bf16[20,3712]{1,0:T(8,128)(2,1)S(1)}, u32[]{:S(2)}, u32[]{:S(2)}) collective-permute-start(bf16[20,3712]{1,0:T(8,128)(2,1)} %get-tuple-element.30), channel_id=1, source_target_pairs={{0,4},{4,8},{8,12},{12,16},{16,20},{20,24},{24,28},{28,0},{1,5},{5... | collective-permute-start | bytes 445448 | tf_op jit(solution)/shard_map/ppermute | solution.py:34
  42.4 58.7 %collective-permute-start.8 = (bf16[20,3712]{1,0:T(8,128)(2,1)}, bf16[20,3712]{1,0:T(8,128)(2,1)S(1)}, u32[]{:S(2)}, u32[]{:S(2)}) collective-permute-start(bf16[20,3712]{1,0:T(8,128)(2,1)} %get-tuple-element.36), channel_id=1, source_target_pairs={{0,16},{4,20},{8,24},{12,28},{16,0},{20,4},{24,8},{28,12},{1,17},{... | collective-permute-start | bytes 445448 | tf_op jit(solution)/shard_map/ppermute | solution.py:34
  46.7 54.4 %collective-permute-start.7 = (bf16[20,3712]{1,0:T(8,128)(2,1)}, bf16[20,3712]{1,0:T(8,128)(2,1)S(1)}, u32[]{:S(2)}, u32[]{:S(2)}) collective-permute-start(bf16[20,3712]{1,0:T(8,128)(2,1)} %get-tuple-element.35), channel_id=1, source_target_pairs={{0,20},{4,24},{8,28},{12,0},{16,4},{20,8},{24,12},{28,16},{1,21},{... | collective-permute-start | bytes 445448 | tf_op jit(solution)/shard_map/ppermute | solution.py:34
  85.1 22.2 %collective-permute-start.6 = (bf16[20,3712]{1,0:T(8,128)(2,1)}, bf16[20,3712]{1,0:T(8,128)(2,1)S(1)}, u32[]{:S(2)}, u32[]{:S(2)}) collective-permute-start(bf16[20,3712]{1,0:T(8,128)(2,1)} %get-tuple-element.34), channel_id=1, source_target_pairs={{0,12},{4,16},{8,20},{12,24},{16,28},{20,0},{24,4},{28,8},{1,13},{... | collective-permute-start | bytes 445448 | tf_op jit(solution)/shard_map/ppermute | solution.py:34
  85.2 22.2 %collective-permute-start.5 = (bf16[20,3712]{1,0:T(8,128)(2,1)}, bf16[20,3712]{1,0:T(8,128)(2,1)S(1)}, u32[]{:S(2)}, u32[]{:S(2)}) collective-permute-start(bf16[20,3712]{1,0:T(8,128)(2,1)} %get-tuple-element.33), channel_id=1, source_target_pairs={{0,24},{4,28},{8,0},{12,4},{16,8},{20,12},{24,16},{28,20},{1,25},{... | collective-permute-start | bytes 445448 | tf_op jit(solution)/shard_map/ppermute | solution.py:34
  107.5 16.5 %collective-permute-start.9 = (bf16[80,3712]{1,0:T(8,128)(2,1)S(1)}, bf16[80,3712]{1,0:T(8,128)(2,1)}, u32[]{:S(2)}, u32[]{:S(2)}) collective-permute-start(bf16[80,3712]{1,0:T(8,128)(2,1)S(1)} %pad_maximum_fusion.1.refs_1_), channel_id=1, source_target_pairs={{0,3},{1,0},{2,1},{3,2},{4,7},{5,4},{6,5},{7,6},{8,11},{9,8},{10,9... | collective-permute-start | bytes 1781768 | tf_op jit(solution)/shard_map/ppermute | solution.py:34
  108.2 25.9 %collective-permute-start.11 = (bf16[80,3712]{1,0:T(8,128)(2,1)S(1)}, bf16[80,3712]{1,0:T(8,128)(2,1)S(1)}, u32[]{:S(2)}, u32[]{:S(2)}) collective-permute-start(bf16[80,3712]{1,0:T(8,128)(2,1)S(1)} %pad_maximum_fusion.refs_0_), channel_id=1, source_target_pairs={{0,3},{1,0},{2,1},{3,2},{4,7},{5,4},{6,5},{7,6},{8,11},{9,8},{10,9... | collective-permute-start | bytes 1781768 | tf_op jit(solution)/shard_map/ppermute | solution.py:34
  110.8 24.8 %collective-permute-start.12 = (bf16[80,3712]{1,0:T(8,128)(2,1)S(1)}, bf16[80,3712]{1,0:T(8,128)(2,1)S(1)}, u32[]{:S(2)}, u32[]{:S(2)}) collective-permute-start(bf16[80,3712]{1,0:T(8,128)(2,1)S(1)} %pad_maximum_fusion.1.refs_1_), channel_id=1, source_target_pairs={{0,1},{1,2},{2,3},{3,0},{4,5},{5,6},{6,7},{7,4},{8,9},{9,10},{10,1... | collective-permute-start | bytes 1781768 | tf_op jit(solution)/shard_map/ppermute | solution.py:34
  110.8 26.4 %collective-permute-start.4 = (bf16[80,3712]{1,0:T(8,128)(2,1)S(1)}, bf16[80,3712]{1,0:T(8,128)(2,1)S(1)}, u32[]{:S(2)}, u32[]{:S(2)}) collective-permute-start(bf16[80,3712]{1,0:T(8,128)(2,1)S(1)} %collective-permute-done.3.refs_4_), channel_id=1, source_target_pairs={{0,1},{1,2},{2,3},{3,0},{4,5},{5,6},{6,7},{7,4},{8,9},{9,10},{10,1... | collective-permute-start | bytes 1781768 | tf_op jit(solution)/shard_map/ppermute | solution.py:34
  111.6 25.6 %collective-permute-start.16 = (bf16[32,8,896]{2,1,0:T(8,128)(2,1)}, bf16[32,8,896]{2,1,0:T(8,128)(2,1)}, u32[]{:S(2)}, u32[]{:S(2)}) collective-permute-start(bf16[32,8,896]{2,1,0:T(8,128)(2,1)} %all_to_all.24), channel_id=1, source_target_pairs={{0,192},{64,0},{128,64},{192,128},{1,193},{65,1},{129,65},{193,129... | collective-permute-start | bytes 1376264 | tf_op jit(solution)/shard_map/ppermute | solution.py:34
  135.6 22.4 %collective-permute-start.10 = (bf16[80,3712]{1,0:T(8,128)(2,1)}, bf16[80,3712]{1,0:T(8,128)(2,1)}, u32[]{:S(2)}, u32[]{:S(2)}) collective-permute-start(bf16[80,3712]{1,0:T(8,128)(2,1)} %collective-permute-done.9.refs_3_), channel_id=1, source_target_pairs={{0,3},{1,0},{2,1},{3,2},{4,7},{5,4},{6,5},{7,6},{8,11},{9,8},{10,9... | collective-permute-start | bytes 1781768 | tf_op jit(solution)/shard_map/ppermute | solution.py:34
  137.2 27.6 %collective-permute-start.15 = (bf16[32,8,896]{2,1,0:T(8,128)(2,1)}, bf16[32,8,896]{2,1,0:T(8,128)(2,1)}, u32[]{:S(2)}, u32[]{:S(2)}) collective-permute-start(bf16[32,8,896]{2,1,0:T(8,128)(2,1)} %all_to_all.24), channel_id=1, source_target_pairs={{0,32},{32,0},{1,33},{33,1},{2,34},{34,2},{3,35},{35,3},{4,36},{36... | collective-permute-start | bytes 1376264 | tf_op jit(solution)/shard_map/ppermute | solution.py:34
  138.0 30.7 %collective-permute-start.17 = (bf16[32,8,896]{2,1,0:T(8,128)(2,1)}, bf16[32,8,896]{2,1,0:T(8,128)(2,1)}, u32[]{:S(2)}, u32[]{:S(2)}) collective-permute-start(bf16[32,8,896]{2,1,0:T(8,128)(2,1)} %collective-permute-done.16), channel_id=1, source_target_pairs={{0,32},{32,0},{1,33},{33,1},{2,34},{34,2},{3,35},{35,3},{4,36},{36... | collective-permute-start | bytes 1376264 | tf_op jit(solution)/shard_map/ppermute | solution.py:34
  138.0 30.7 %collective-permute-start.19 = (bf16[32,8,896]{2,1,0:T(8,128)(2,1)}, bf16[32,8,896]{2,1,0:T(8,128)(2,1)}, u32[]{:S(2)}, u32[]{:S(2)}) collective-permute-start(bf16[32,8,896]{2,1,0:T(8,128)(2,1)} %collective-permute-done.18), channel_id=1, source_target_pairs={{0,32},{32,0},{1,33},{33,1},{2,34},{34,2},{3,35},{35,3},{4,36},{36... | collective-permute-start | bytes 1376264 | tf_op jit(solution)/shard_map/ppermute | solution.py:34
  145.7 23.0 %collective-permute-start.21 = (bf16[32,8,896]{2,1,0:T(8,128)(2,1)}, bf16[32,8,896]{2,1,0:T(8,128)(2,1)}, u32[]{:S(2)}, u32[]{:S(2)}) collective-permute-start(bf16[32,8,896]{2,1,0:T(8,128)(2,1)} %collective-permute-done.20), channel_id=1, source_target_pairs={{0,32},{32,0},{1,33},{33,1},{2,34},{34,2},{3,35},{35,3},{4,36},{36... | collective-permute-start | bytes 1376264 | tf_op jit(solution)/shard_map/ppermute | solution.py:34
  158.0 20.5 %collective-permute-start.13 = (bf16[480,256]{1,0:T(8,128)(2,1)}, bf16[480,256]{1,0:T(8,128)(2,1)S(1)}, u32[]{:S(2)}, u32[]{:S(2)}) collective-permute-start(bf16[480,256]{1,0:T(8,128)(2,1)} %hidden.2.refs_4_), channel_id=1, source_target_pairs={{0,3},{1,0},{2,1},{3,2},{4,7},{5,4},{6,5},{7,6},{8,11},{9,8},{10,9... | collective-permute-start | bytes 737288 | tf_op jit(solution)/shard_map/ppermute | solution.py:34
  182.8 30.9 %all-to-all-start.1 = ((bf16[32,16,896]{2,1,0:T(8,128)(2,1)}), bf16[32,16,896]{2,1,0:T(8,128)(2,1)S(1)}, u32[]{:S(2)}, u32[]{:S(2)}) async-start(bf16[32,16,896]{2,1,0:T(8,128)(2,1)} %fisher.2), calls=%async_computation.1 | async-start | bytes 1835008 | tf_op jit(solution)/shard_map/all_to_all | solution.py:487
  188.4 16.4 %collective-permute-start.30 = (bf16[640,256]{1,0:T(8,128)(2,1)S(1)}, bf16[640,256]{1,0:T(8,128)(2,1)S(1)}, u32[]{:S(2)}, u32[]{:S(2)}) collective-permute-start(bf16[640,256]{1,0:T(8,128)(2,1)S(1)} %copy-done.21), channel_id=1, source_target_pairs={{0,1},{1,2},{2,3},{3,0},{4,5},{5,6},{6,7},{7,4},{8,9},{9,10},{10,1... | collective-permute-start | bytes 983048 | tf_op jit(solution)/shard_map/ppermute | solution.py:34
  189.9 17.4 %collective-permute-start.31 = (bf16[640,256]{1,0:T(8,128)(2,1)S(1)}, bf16[640,256]{1,0:T(8,128)(2,1)}, u32[]{:S(2)}, u32[]{:S(2)}) collective-permute-start(bf16[640,256]{1,0:T(8,128)(2,1)S(1)} %copy-done.21), channel_id=1, source_target_pairs={{0,2},{1,3},{2,0},{3,1},{4,6},{5,7},{6,4},{7,5},{8,10},{9,11},{10,... | collective-permute-start | bytes 983048 | tf_op jit(solution)/shard_map/ppermute | solution.py:34
  213.7 38.0 %all-to-all-start.3 = ((bf16[32,16,896]{2,1,0:T(8,128)(2,1)}), bf16[32,16,896]{2,1,0:T(8,128)(2,1)}, u32[]{:S(2)}, u32[]{:S(2)}) async-start(bf16[32,16,896]{2,1,0:T(8,128)(2,1)} %fisher.3), calls=%async_computation.3 | async-start | bytes 1835008 | tf_op jit(solution)/shard_map/all_to_all | solution.py:487
  232.7 44.8 %collective-permute-start.22 = (bf16[2,3,48,3584]{3,2,1,0:T(8,128)(2,1)}, bf16[2,3,48,3584]{3,2,1,0:T(8,128)(2,1)S(1)}, u32[]{:S(2)}, u32[]{:S(2)}) collective-permute-start(bf16[2,3,48,3584]{3,2,1,0:T(8,128)(2,1)} %get-tuple-element.40), channel_id=1, source_target_pairs={{0,32},{32,0},{1,33},{33,1},{2,34},{34,2},{3,35},{35,3},{4,36},{36... | collective-permute-start | bytes 6193160 | tf_op jit(solution)/shard_map/ppermute | solution.py:34
  256.9 34.7 %collective-permute-start.32 = (bf16[2,3,48,3584]{3,2,1,0:T(8,128)(2,1)}, bf16[2,3,48,3584]{3,2,1,0:T(8,128)(2,1)}, u32[]{:S(2)}, u32[]{:S(2)}) collective-permute-start(bf16[2,3,48,3584]{3,2,1,0:T(8,128)(2,1)} %get-tuple-element.50), channel_id=1, source_target_pairs={{0,32},{32,0},{1,33},{33,1},{2,34},{34,2},{3,35},{35,3},{4,36},{36... | collective-permute-start | bytes 6193160 | tf_op jit(solution)/shard_map/ppermute | solution.py:34
  271.0 16.6 %collective-permute-start.38 = (bf16[48,3584]{1,0:T(8,128)(2,1)}, bf16[48,3584]{1,0:T(8,128)(2,1)S(1)}, u32[]{:S(2)}, u32[]{:S(2)}) collective-permute-start(bf16[48,3584]{1,0:T(8,128)(2,1)} %get-tuple-element.57), channel_id=1, source_target_pairs={{0,192},{64,0},{128,64},{192,128},{1,193},{65,1},{129,65},{193,129... | collective-permute-start | bytes 1032200 | tf_op jit(solution)/shard_map/ppermute | solution.py:34
  281.5 15.2 %collective-permute-start.26 = (bf16[48,3584]{1,0:T(8,128)(2,1)}, bf16[48,3584]{1,0:T(8,128)(2,1)S(1)}, u32[]{:S(2)}, u32[]{:S(2)}) collective-permute-start(bf16[48,3584]{1,0:T(8,128)(2,1)} %get-tuple-element.45), channel_id=1, source_target_pairs={{0,64},{64,128},{128,192},{192,0},{1,65},{65,129},{129,193},{193,1... | collective-permute-start | bytes 1032200 | tf_op jit(solution)/shard_map/ppermute | solution.py:34
  288.3 15.7 %collective-permute-start.28 = (bf16[48,3584]{1,0:T(8,128)(2,1)}, bf16[48,3584]{1,0:T(8,128)(2,1)S(1)}, u32[]{:S(2)}, u32[]{:S(2)}) collective-permute-start(bf16[48,3584]{1,0:T(8,128)(2,1)} %get-tuple-element.47), channel_id=1, source_target_pairs={{0,64},{64,128},{128,192},{192,0},{1,65},{65,129},{129,193},{193,1... | collective-permute-start | bytes 1032200 | tf_op jit(solution)/shard_map/ppermute | solution.py:34
  289.4 14.6 %collective-permute-start.29 = (bf16[48,3584]{1,0:T(8,128)(2,1)}, bf16[48,3584]{1,0:T(8,128)(2,1)}, u32[]{:S(2)}, u32[]{:S(2)}) collective-permute-start(bf16[48,3584]{1,0:T(8,128)(2,1)} %get-tuple-element.48), channel_id=1, source_target_pairs={{0,192},{64,0},{128,64},{192,128},{1,193},{65,1},{129,65},{193,129... | collective-permute-start | bytes 1032200 | tf_op jit(solution)/shard_map/ppermute | solution.py:34
  294.0 17.5 %collective-permute-start.35 = (bf16[48,3584]{1,0:T(8,128)(2,1)}, bf16[48,3584]{1,0:T(8,128)(2,1)}, u32[]{:S(2)}, u32[]{:S(2)}) collective-permute-start(bf16[48,3584]{1,0:T(8,128)(2,1)} %get-tuple-element.54), channel_id=1, source_target_pairs={{0,64},{64,128},{128,192},{192,0},{1,65},{65,129},{129,193},{193,1... | collective-permute-start | bytes 1032200 | tf_op jit(solution)/shard_map/ppermute | solution.py:34
  296.7 20.4 %collective-permute-start.36 = (bf16[48,3584]{1,0:T(8,128)(2,1)}, bf16[48,3584]{1,0:T(8,128)(2,1)S(1)}, u32[]{:S(2)}, u32[]{:S(2)}) collective-permute-start(bf16[48,3584]{1,0:T(8,128)(2,1)} %get-tuple-element.56), channel_id=1, source_target_pairs={{0,64},{64,128},{128,192},{192,0},{1,65},{65,129},{129,193},{193,1... | collective-permute-start | bytes 1032200 | tf_op jit(solution)/shard_map/ppermute | solution.py:34
  296.7 20.4 %collective-permute-start.37 = (bf16[48,3584]{1,0:T(8,128)(2,1)}, bf16[48,3584]{1,0:T(8,128)(2,1)S(1)}, u32[]{:S(2)}, u32[]{:S(2)}) collective-permute-start(bf16[48,3584]{1,0:T(8,128)(2,1)} %get-tuple-element.55), channel_id=1, source_target_pairs={{0,192},{64,0},{128,64},{192,128},{1,193},{65,1},{129,65},{193,129... | collective-permute-start | bytes 1032200 | tf_op jit(solution)/shard_map/ppermute | solution.py:34
  (38 other events, 409.2 us)
